TPU v7x, 32 devices: a whole 2x2x4 slice. The times are simulated.
32 devices in a mesh: req: 8 (over z, x), grp: 4 (over y, core).
Axes of the slice: x: 2, y: 2, z: 4, core: 2. Of those that a mesh axis runs over, the one named last changes fastest.
Arguments:
- hidden: bfloat16 [256, 16, 1024], P(('grp', 'req')), parts along dimension 0, may hold values from -6 to 6
- norm_gain: float32 [1024], replicated, may hold values from 0.1 to 1.9
- in_weight: bfloat16 [1024, 4096], replicated, may hold values from -0.1875 to 0.1875
- conv_weight: float32 [4, 2048], P(None, 'req'), may hold values from -3 to 3
- conv_bias: float32 [2048], P('req'), may hold values from -3 to 3
- x_weight: bfloat16 [2048, 160], P('req'), may hold values from -0.125 to 0.125
- step_weight: bfloat16 [128, 2048], P(None, 'req'), may hold values from -0.5 to 0.5
- step_bias: float32 [2048], P('req'), may hold values from -5 to -1
- log_decay: float32 [16, 2048], P(None, 'req'), may hold values from -0.7 to 2.8
- skip_gain: float32 [2048], P('req'), may hold values from 0.5 to 1.5
- out_weight: bfloat16 [2048, 1024], replicated, may hold values from -0.125 to 0.125
- old_states: float32 [256, 16, 2048], P(('grp', 'req')), parts along dimension 0, may hold values from -3 to 3
- old_edges: bfloat16 [256, 3, 2048], P(('grp', 'req')), parts along dimension 0, may hold values from -6 to 6
- anchor: int32 [256], P('grp'), parts along dimension 0, may hold values from 0 to 63, each once
- fresh_flag: int32 [256], P('grp'), parts along dimension 0, may hold values 0 or 1
- accepted: int32 [256], P('grp'), parts along dimension 0, may hold values from 1 to 16
- request_ages: int32 [256], P('grp'), parts along dimension 0, may hold values from 0 to 7
Outputs:
- layer_out: bfloat16 [256, 16, 1024], P(('grp', 'req')), parts along dimension 0
- new_states: float32 [256, 16, 2048], P(('grp', 'req')), parts along dimension 0
There are 4 independent parts, one for each index of `grp`. A program takes and returns all parts, laid end to end along the dimension named above; an argument that names none is the same for every part. Nothing has to cross between parts.
Inputs may be any that keep to these rules, and one draw needn't show every extreme that they name: Every old slot is the anchor of exactly one request.
All inputs are finite; a program needn't handle non-finite values.
Results may differ from a plain program's by a relative error of at most 0.0091.
Values may be sent and summed in bfloat16 or wider, within the bound.
No kernel may reach another device: no remote copies, remote signals or barrier semaphores. Data moves between devices by JAX's collectives and lax.ppermute only.
A program may use at most 128 MiB of HBM per device.

v0:
```python
import jax
import jax.numpy as jnp
from jax import lax
from jax.sharding import PartitionSpec as P

EPS = 1e-05


def rms_normed(values_in, norm_gain):
    values = values_in.astype(jnp.float32)
    factor = lax.rsqrt(jnp.mean(values * values, axis=-1, keepdims=True) + EPS)
    return (values * factor * norm_gain).astype(jnp.bfloat16)


def on_device(
    hidden,
    norm_gain,
    in_weight,
    conv_weight,
    conv_bias,
    x_weight,
    step_weight,
    step_bias,
    log_decay,
    skip_gain,
    out_weight,
    old_states,
    old_edges,
    anchor,
    fresh_flag,
    accepted,
    request_ages,
):
    local_reqs, draft_len, width = hidden.shape
    inner_width = out_weight.shape[0]
    channels = conv_weight.shape[1]
    state_size = log_decay.shape[0]
    low_rank = step_weight.shape[0]
    span = old_edges.shape[1]
    state_lead = jnp.swapaxes(old_states, 0, 1)
    edge_lead = jnp.swapaxes(old_edges.astype(jnp.float32), 0, 1)
    moved_states, moved_edges = (
        lax.all_to_all(state_lead, "req", split_axis=2, concat_axis=1, tiled=True),
        lax.all_to_all(edge_lead, "req", split_axis=2, concat_axis=1, tiled=True),
    )
    token_major = jnp.swapaxes(hidden, 0, 1).reshape(draft_len * local_reqs, width)
    normed = rms_normed(token_major, norm_gain)
    projected = jnp.dot(normed, in_weight, preferred_element_type=jnp.float32).astype(jnp.bfloat16)
    projected = jnp.moveaxis(projected.reshape(draft_len, local_reqs, 2, inner_width), 2, 0)
    grouped = lax.all_to_all(projected, "req", split_axis=3, concat_axis=2, tiled=True)
    all_reqs = grouped.shape[2]
    inner_part = grouped[0]
    gate_part = grouped[1]
    keep_state = (1 - fresh_flag).astype(jnp.float32)
    start_state = jnp.take(moved_states, anchor, axis=1) * keep_state[None, :, None]
    edges = jnp.take(moved_edges, anchor, axis=1)
    distance = span - jnp.arange(span, dtype=jnp.int32)
    usable = (distance[:, None] <= request_ages[None, :]) & (fresh_flag[None, :] == 0)
    history = jnp.where(usable[:, :, None], edges, jnp.zeros((), jnp.float32))
    sequence = jnp.concatenate([history, inner_part.astype(jnp.float32)], axis=0)
    running = conv_bias + conv_weight[0] * sequence[0:draft_len]
    for offset in range(1, conv_weight.shape[0]):
        running = running + conv_weight[offset] * sequence[offset : offset + draft_len]
    conv_out = jax.nn.silu(running).astype(jnp.bfloat16)
    conv_rows = conv_out.reshape(draft_len * all_reqs, channels)
    partial_value = jnp.dot(conv_rows, x_weight, preferred_element_type=jnp.float32)
    mixed_rows = lax.psum(partial_value, "req").astype(jnp.bfloat16)
    flat = all_reqs * channels
    step_sizes = jax.nn.softplus(
        jnp.dot(mixed_rows[:, :low_rank], step_weight, preferred_element_type=jnp.float32)
        + step_bias
    )
    step_sizes = step_sizes.reshape(draft_len, flat)
    coeffs = (
        mixed_rows[:, low_rank:].astype(jnp.float32).reshape(draft_len, all_reqs, 2 * state_size)
    )
    b_coeff = coeffs[:, :, :state_size]
    c_coeff = coeffs[:, :, state_size:]
    inputs = conv_out.astype(jnp.float32)
    flat_inputs = inputs.reshape(draft_len, flat)
    decay = jnp.broadcast_to(
        (-jnp.exp(log_decay))[:, None, :], (state_size, all_reqs, channels)
    ).reshape(state_size, flat)
    start_flat = start_state.reshape(state_size, flat)

    def spread(per_token):
        return jnp.broadcast_to(
            jnp.swapaxes(per_token, 0, 1)[:, :, None], (state_size, all_reqs, channels)
        ).reshape(state_size, flat)

    def advance(carried, sliced):
        current, chosen = carried
        step_delta, step_b, step_c, step_input, step_index = sliced
        factor = jnp.exp(step_delta[None, :] * decay)
        current = factor * current + (step_delta * step_input)[None, :] * spread(step_b)
        result = jnp.sum(spread(step_c) * current, axis=0)
        picked = jnp.broadcast_to(
            (accepted == step_index + 1)[:, None], (all_reqs, channels)
        ).reshape(flat)
        chosen = jnp.where(picked[None, :], current, chosen)
        return ((current, chosen), result)

    sliced = (step_sizes, b_coeff, c_coeff, flat_inputs, jnp.arange(draft_len, dtype=jnp.int32))
    (final_state, chosen), outputs = lax.scan(advance, (start_flat, start_flat), sliced)
    outputs = outputs.reshape(draft_len, all_reqs, channels)
    gated_rows = (
        (outputs + skip_gain * inputs) * jax.nn.silu(gate_part.astype(jnp.float32))
    ).astype(jnp.bfloat16)
    returned = lax.all_to_all(gated_rows, "req", split_axis=1, concat_axis=2, tiled=True)
    layer_out = jnp.dot(
        returned.reshape(draft_len * local_reqs, inner_width),
        out_weight,
        preferred_element_type=jnp.float32,
    ).astype(jnp.bfloat16)
    layer_out = jnp.swapaxes(layer_out.reshape(draft_len, local_reqs, width), 0, 1)
    owned = lax.all_to_all(
        chosen.reshape(state_size, all_reqs, channels),
        "req",
        split_axis=1,
        concat_axis=2,
        tiled=True,
    )
    return (layer_out, jnp.swapaxes(owned, 0, 1))


def solution(mesh):
    return jax.shard_map(
        on_device,
        mesh=mesh,
        in_specs=(
            P(("grp", "req"), None, None),
            P(),
            P(),
            P(None, "req"),
            P("req"),
            P("req", None),
            P(None, "req"),
            P("req"),
            P(None, "req"),
            P("req"),
            P(),
            P(("grp", "req"), None, None),
            P(("grp", "req"), None, None),
            P("grp"),
            P("grp"),
            P("grp"),
            P("grp"),
        ),
        out_specs=(P(("grp", "req"), None, None), P(("grp", "req"), None, None)),
        check_vma=False,
    )
```

profile of v0, /device:TPU:0, one launch (start us, length us, event | category | flops | bytes accessed | tf_op | source)
XLA Modules:
  0.0 369.8 jit_solution(14479661632174473123)
XLA Ops:
  0.7 4.0 %copy.100 = f32[8,3,2048]{0,1,2:T(4,128)} copy(bf16[8,3,2048]{2,0,1:T(8,128)(2,1)} %param.31) | data formatting | bytes 294912 | tf_op jit(solution)/shard_map/transpose | solution.py:41
  4.7 3.9 %bitcast_bitcast_fusion.2 = f32[2048,3,8]{2,1,0:T(4,128)} fusion(f32[8,3,2048]{0,1,2:T(4,128)} %copy.100), kind=kLoop, calls=%fused_computation.72 | loop fusion | bytes 393216
  8.6 5.1 %reshape.188 = f32[8,1,6144]{2,1,0:T(1,128)} reshape(f32[2048,3,8]{2,1,0:T(4,128)} %bitcast_bitcast_fusion.2) | data formatting | bytes 393216
  13.7 7.3 %all-to-all-start.1 = ((f32[8,1,6144]{2,1,0:T(1,128)}), f32[8,1,6144]{2,1,0:T(1,128)S(1)}, u32[]{:S(2)}, u32[]{:S(2)}) async-start(f32[8,1,6144]{2,1,0:T(1,128)} %reshape.188), calls=%async_computation.1 | async-start | bytes 393216 | tf_op jit(solution)/shard_map/all_to_all | solution.py:44
  20.9 4.7 %copy.94 = f32[8,16,2048]{1,0,2:T(8,128)} copy(f32[8,16,2048]{2,1,0:T(8,128)S(1)} %copy-done.3) | data formatting | bytes 2097152 | tf_op args[11]
  26.0 4.8 %convolution_convert_fusion = bf16[128,4096]{1,0:T(8,128)(2,1)S(1)} fusion(bf16[1024,4096]{1,0:T(8,128)(2,1)} %param.21, f32[1024]{0:T(1024)S(1)} %copy-done.4, f32[128]{0:T(128)S(1)} %rsqrt.12, bf16[8,16,1024]{2,1,0:T(8,128)(2,1)S(1)} %copy-done.2), kind=kOutput, calls=%fused_computation.11 | convolution fusion | flops 1074790400 | bytes 9703936 | tf_op jit(solution)/shard_map/dot_general | solution.py:48
  30.8 8.9 %copy.103 = bf16[16,8,2,2048]{0,1,2,3:T(8,128)(2,1)} copy(bf16[16,8,2,2048]{3,1,2,0:T(8,128)(2,1)S(1)} %bitcast.169) | data formatting | bytes 2097152 | tf_op jit(solution)/shard_map/reshape | solution.py:49
  39.6 7.5 %bitcast_bitcast_fusion = bf16[2048,2,8,16]{3,2,1,0:T(8,128)(2,1)} fusion(bf16[16,8,2,2048]{0,1,2,3:T(8,128)(2,1)} %copy.103), kind=kLoop, calls=%fused_computation.70 | loop fusion | bytes 2097152
  47.1 5.8 %bitcast_bitcast_fusion.1 = f32[2048,8,16]{2,1,0:T(8,128)} fusion(f32[8,16,2048]{1,0,2:T(8,128)} %copy.94), kind=kLoop, calls=%fused_computation.71 | loop fusion | bytes 2097152
  52.9 8.1 %reshape.184 = f32[8,1,32768]{2,1,0:T(1,128)} reshape(f32[2048,8,16]{2,1,0:T(8,128)} %bitcast_bitcast_fusion.1) | data formatting | bytes 2097152
  61.1 6.0 %all-to-all-start = ((f32[8,1,32768]{2,1,0:T(1,128)}), f32[8,1,32768]{2,1,0:T(1,128)S(1)}, u32[]{:S(2)}, u32[]{:S(2)}) async-start(f32[8,1,32768]{2,1,0:T(1,128)} %reshape.184), calls=%async_computation | async-start | bytes 2097152 | tf_op jit(solution)/shard_map/all_to_all | solution.py:43
  67.3 11.3 %reshape.186 = bf16[8,2,32768]{2,1,0:T(2,128)(2,1)} reshape(bf16[2048,2,8,16]{3,2,1,0:T(8,128)(2,1)} %bitcast_bitcast_fusion) | data formatting | bytes 2097152
  80.5 4.7 %reshape.189 = f32[2048,3,8]{2,1,0:T(4,128)} reshape(f32[8,6144]{1,0:T(8,128)S(1)} %reduce.3) | data formatting | bytes 393216
  92.5 3.7 %all-to-all-start.2 = ((bf16[8,2,32768]{2,1,0:T(2,128)(2,1)}), bf16[8,2,32768]{2,1,0:T(2,128)(2,1)S(1)}, u32[]{:S(2)}, u32[]{:S(2)}) async-start(bf16[8,2,32768]{2,1,0:T(2,128)(2,1)} %reshape.186), calls=%async_computation.2 | async-start | bytes 2097152 | tf_op jit(solution)/shard_map/all_to_all | solution.py:50
  99.4 6.1 %reshape.185 = f32[2048,8,16]{2,1,0:T(8,128)} reshape(f32[8,32768]{1,0:T(8,128)S(1)} %reduce.2) | data formatting | bytes 2097152
  105.5 5.4 %copy.96 = f32[16,8,8,256]{3,2,1,0:T(8,128)S(1)} copy(f32[16,8,8,256]{0,2,3,1:T(8,128)} %bitcast.155) | data formatting | bytes 2097152 | tf_op jit(solution)/shard_map/all_to_all | solution.py:43
  112.4 9.5 %all-to-all-done.2 = bf16[8,2,32768]{2,1,0:T(2,128)(2,1)S(1)} async-done(((bf16[8,2,32768]{2,1,0:T(2,128)(2,1)}), bf16[8,2,32768]{2,1,0:T(2,128)(2,1)S(1)}, u32[]{:S(2)}, u32[]{:S(2)}) %all-to-all-start.2) | async-done | bytes 1048608 | tf_op jit(solution)/shard_map/all_to_all | solution.py:50
  121.9 7.6 %reshape.187 = bf16[2048,2,8,16]{3,2,1,0:T(8,128)(2,1)} reshape(bf16[8,2,32768]{2,1,0:T(2,128)(2,1)S(1)} %all-to-all-done.2) | data formatting | bytes 2097152
  129.5 8.9 %copy.104 = bf16[2,16,8,8,256]{4,2,3,1,0:T(8,128)(2,1)S(1)} copy(bf16[2,16,8,8,256]{1,2,0,4,3:T(8,128)(2,1)} %bitcast.156) | data formatting | bytes 2097152 | tf_op jit(solution)/shard_map/all_to_all | solution.py:50
  140.2 43.6 %all-reduce.1 = bf16[1024,160]{0,1:T(8,128)(2,1)} all-reduce(f32[1024,160]{0,1:T(8,128)S(1)} %fusion.29), channel_id=1, replica_groups=mesh['req'=8,'grp'=4] {'req'}, use_global_device_ids=true, to_apply=%region_1.2 | all-reduce | flops 163840 | bytes 983040 | tf_op jit(solution)/shard_map/psum | solution.py:67
  191.2 132.7 %while.15 = (s32[]{:T(128)}, f32[16,16384]{1,0:T(8,128)S(1)}, f32[16,16384]{1,0:T(8,128)S(1)}, f32[16,16384]{1,0:T(8,128)}, f32[16,16384]{1,0:T(8,128)}, /*index...) while((s32[]{:T(128)}, f32[16,16384]{1,0:T(8,128)S(1)}, ...), condition=%wide.region_4.5_spmd.clone, body=%wide.region_2.4_spmd.clone.sunk | while | flops 1835075 | bytes 18522676 | solution.py:104
  332.7 9.4 %all-to-all-done.3 = bf16[16,64,256]{2,0,1:T(8,128)(2,1)S(1)} async-done(((bf16[16,64,256]{2,0,1:T(8,128)(2,1)}), bf16[16,64,256]{2,0,1:T(8,128)(2,1)S(1)}, u32[]{:S(2)}, u32[]{:S(2)}) %all-to-all-start.3) | async-done | bytes 524320 | tf_op jit(solution)/shard_map/all_to_all | solution.py:109
  342.1 9.1 %all-to-all-start.4 = ((f32[16,64,256]{2,0,1:T(8,128)}), f32[16,64,256]{2,0,1:T(8,128)S(1)}, u32[]{:S(2)}, u32[]{:S(2)}) async-start(f32[16,64,256]{2,0,1:T(8,128)} %bitcast.121), calls=%async_computation.4 | async-start | bytes 2097152 | tf_op jit(solution)/shard_map/all_to_all | solution.py:116
  355.4 12.2 %all-to-all-done.4 = f32[16,64,256]{2,0,1:T(8,128)S(1)} async-done(((f32[16,64,256]{2,0,1:T(8,128)}), f32[16,64,256]{2,0,1:T(8,128)S(1)}, u32[]{:S(2)}, u32[]{:S(2)}) %all-to-all-start.4) | async-done | bytes 1048608 | tf_op jit(solution)/shard_map/all_to_all | solution.py:116
  (323 shorter events, 159.0 us)
Async XLA Ops:
  0.6 139.3 %copy-start = (bf16[256,160]{0,1:T(8,128)(2,1)S(1)}, bf16[256,160]{0,1:T(8,128)(2,1)}, u32[]{:S(2)}) copy-start(bf16[256,160]{0,1:T(8,128)(2,1)} %param.24) | copy-start | bytes 245764
  0.6 20.3 %copy-start.3 = (f32[8,16,2048]{2,1,0:T(8,128)S(1)}, f32[8,16,2048]{2,1,0:T(8,128)}, u32[]{:S(2)}) copy-start(f32[8,16,2048]{2,1,0:T(8,128)} %param.30) | copy-start | bytes 3145732
  8.6 17.1 %copy-start.2 = (bf16[8,16,1024]{2,1,0:T(8,128)(2,1)S(1)}, bf16[8,16,1024]{2,1,0:T(8,128)(2,1)}, u32[]{:S(2)}) copy-start(bf16[8,16,1024]{2,1,0:T(8,128)(2,1)} %param.19) | copy-start | bytes 786436
  8.6 17.4 %copy-start.4 = (f32[1024]{0:T(1024)S(1)}, f32[1024]{0:T(1024)}, u32[]{:S(2)}) copy-start(f32[1024]{0:T(1024)} %param.20) | copy-start | bytes 12292
  13.7 47.4 %all-to-all-start.1 = ((f32[8,1,6144]{2,1,0:T(1,128)}), f32[8,1,6144]{2,1,0:T(1,128)S(1)}, u32[]{:S(2)}, u32[]{:S(2)}) async-start(f32[8,1,6144]{2,1,0:T(1,128)} %reshape.188), calls=%async_computation.1 | async-start | bytes 393216 | tf_op jit(solution)/shard_map/all_to_all | solution.py:44
  52.9 8.2 %copy-start.12 = (s32[64]{0:T(128)S(1)}, s32[64]{0:T(128)}, u32[]{:S(2)}) copy-start(s32[64]{0:T(128)} %param.33) | copy-start | bytes 772
  52.9 14.3 %copy-start.13 = (s32[64]{0:T(128)S(1)}, s32[64]{0:T(128)}, u32[]{:S(2)}) copy-start(s32[64]{0:T(128)} %param.32) | copy-start | bytes 772
  52.9 25.7 %copy-start.9 = (s32[64]{0:T(128)S(1)}, s32[64]{0:T(128)}, u32[]{:S(2)}) copy-start(s32[64]{0:T(128)} %param.35) | copy-start | bytes 772
  52.9 25.9 %copy-start.6 = (f32[4,256]{1,0:T(4,128)S(1)}, f32[4,256]{1,0:T(4,128)}, u32[]{:S(2)}) copy-start(f32[4,256]{1,0:T(4,128)} %param.22) | copy-start | bytes 12292
  52.9 25.9 %copy-start.5 = (f32[16,256]{1,0:T(8,128)S(1)}, f32[16,256]{1,0:T(8,128)}, u32[]{:S(2)}) copy-start(f32[16,256]{1,0:T(8,128)} %param.27) | copy-start | bytes 49156
  61.1 31.4 %all-to-all-start = ((f32[8,1,32768]{2,1,0:T(1,128)}), f32[8,1,32768]{2,1,0:T(1,128)S(1)}, u32[]{:S(2)}, u32[]{:S(2)}) async-start(f32[8,1,32768]{2,1,0:T(1,128)} %reshape.184), calls=%async_computation | async-start | bytes 2097152 | tf_op jit(solution)/shard_map/all_to_all | solution.py:43
  92.5 29.4 %all-to-all-start.2 = ((bf16[8,2,32768]{2,1,0:T(2,128)(2,1)}), bf16[8,2,32768]{2,1,0:T(2,128)(2,1)S(1)}, u32[]{:S(2)}, u32[]{:S(2)}) async-start(bf16[8,2,32768]{2,1,0:T(2,128)(2,1)} %reshape.186), calls=%async_computation.2 | async-start | bytes 2097152 | tf_op jit(solution)/shard_map/all_to_all | solution.py:50
  112.4 27.0 %copy-start.7 = (f32[256]{0:T(256)S(1)}, f32[256]{0:T(256)}, u32[]{:S(2)}) copy-start(f32[256]{0:T(256)} %param.23) | copy-start | bytes 3076
  129.5 55.2 %copy-start.10 = (bf16[128,256]{1,0:T(8,128)(2,1)S(1)}, bf16[128,256]{1,0:T(8,128)(2,1)}, u32[]{:S(2)}) copy-start(bf16[128,256]{1,0:T(8,128)(2,1)} %param.25) | copy-start | bytes 196612
  129.5 55.2 %copy-start.11 = (f32[256]{0:T(256)S(1)}, f32[256]{0:T(256)}, u32[]{:S(2)}) copy-start(f32[256]{0:T(256)} %param.26) | copy-start | bytes 3076
  138.4 1.0 copy-start.1
  138.4 52.8 %copy-start.14 = (s32[64]{0:T(128)S(1)}, s32[64]{0:T(128)}, u32[]{:S(2)}) copy-start(s32[64]{0:T(128)} %param.34) | copy-start | bytes 772
  191.2 134.3 %copy-start.8 = (f32[256]{0:T(256)S(1)}, f32[256]{0:T(256)}, u32[]{:S(2)}) copy-start(f32[256]{0:T(256)} %param.28) | copy-start | bytes 3076
  328.1 14.0 %all-to-all-start.3 = ((bf16[16,64,256]{2,0,1:T(8,128)(2,1)}), bf16[16,64,256]{2,0,1:T(8,128)(2,1)S(1)}, u32[]{:S(2)}, u32[]{:S(2)}) async-start(bf16[16,64,256]{2,0,1:T(8,128)(2,1)} %copy.108), calls=%async_computation.3 | async-start | bytes 1048576 | tf_op jit(solution)/shard_map/all_to_all | solution.py:109
  342.1 25.5 %all-to-all-start.4 = ((f32[16,64,256]{2,0,1:T(8,128)}), f32[16,64,256]{2,0,1:T(8,128)S(1)}, u32[]{:S(2)}, u32[]{:S(2)}) async-start(f32[16,64,256]{2,0,1:T(8,128)} %bitcast.121), calls=%async_computation.4 | async-start | bytes 2097152 | tf_op jit(solution)/shard_map/all_to_all | solution.py:116
where the time goes:
time: 372 us; the launch traced here: 370 us
  local copies, waits for them, and re-layouts  191 us (51%)
  other arithmetic  47.8 us (13%)
  blocking collectives  43.6 us (12%)
  waiting for transfers between devices  33.9 us (9%)
  starting transfers between devices  29.5 us (8%)
  loops' own time  12.3 us (3%)
  matrix products  10.8 us (3%)
    unnamed x47, local copies, waits for them, and re-layouts  70.4 us
    psum x1, blocking collectives, on_device(): mixed_rows = lax.psum(partial_value, 'req').astype(jnp.bfloat16)  43.6 us
    dynamic_update_slice x16, local copies, waits for them, and re-layouts, on_device(): lax.scan(advance, (start_flat, start_flat), sliced)  31.1 us
    while x48, local copies, waits for them, and re-layouts  29.4 us
    dynamic_slice x16, other arithmetic, on_device(): lax.scan(advance, (start_flat, start_flat), sliced)  20.9 us
    reduce_sum x16, other arithmetic, advance(): result = jnp.sum(spread(step_c) * current, axis=0)  14.9 us
    another operation x1, loops' own time, on_device(): lax.scan(advance, (start_flat, start_flat), sliced)  12.3 us
    all_to_all x1, waiting for transfers between devices, on_device(): lax.all_to_all(chosen.reshape(state_size, all_reqs, channels), 'req', spl...  12.2 us
  transfers between devices with their start and end apart: 5, of which 4 were waited for; matrix products, arithmetic and copies ran while one was open for 23% of the time, Pallas kernels for 0%

commit v1 on v0

v1 whole, which is shorter than its diff:
```python
import functools

import jax
import jax.numpy as jnp
from jax import lax
from jax.experimental import pallas as pl
from jax.experimental.pallas import tpu as pltpu
from jax.sharding import PartitionSpec as P

EPS = 1e-05
LOG2E = 1.4426950408889634
LANES = 128
BLOCK = 256


def rms_normed(values_in, norm_gain):
    values = values_in.astype(jnp.float32)
    factor = lax.rsqrt(jnp.mean(values * values, axis=-1, keepdims=True) + EPS)
    return (values * factor * norm_gain).astype(jnp.bfloat16)


def pack_kernel(state_ref, edge_ref, out_ref, tile_ref):
    blocks, slots, _ = out_ref.shape
    width = state_ref.shape[1] // blocks
    states = state_ref.shape[0] // slots
    for dest in range(blocks):
        cols = pl.ds(dest * width, width)
        for part in range(width // LANES):
            at = dest * width + part * LANES
            tile = tile_ref.at[at // LANES]
            tile[...] = state_ref[:, pl.ds(at, LANES)]
            for n in range(states):
                rows = tile[pl.ds(n, slots, stride=states), :]
                out_ref[dest, :, pl.ds(n * width + part * LANES, LANES)] = rows.astype(jnp.bfloat16)
        for e in range(edge_ref.shape[0]):
            out_ref[dest, :, pl.ds((states + e) * width, width)] = edge_ref[e, :, cols]


def pack(old_states, old_edges, blocks):
    slots, states, inner = old_states.shape
    span = old_edges.shape[1]
    width = inner // blocks
    edges = jnp.swapaxes(old_edges, 0, 1)
    if width % LANES == 0 and slots == 8:
        return pl.pallas_call(
            pack_kernel,
            out_shape=jax.ShapeDtypeStruct((blocks, slots, (states + span) * width), jnp.bfloat16),
            in_specs=[pl.BlockSpec(memory_space=pltpu.VMEM)] * 2,
            out_specs=pl.BlockSpec(memory_space=pltpu.VMEM),
            scratch_shapes=[pltpu.VMEM((inner // LANES, slots * states, LANES), jnp.float32)],
            compiler_params=pltpu.CompilerParams(vmem_limit_bytes=16 << 20),
            name="pack_states",
        )(old_states.reshape(slots * states, inner), edges)
    lead = jnp.swapaxes(old_states.astype(jnp.bfloat16), 0, 1)
    both = jnp.concatenate([lead, edges], axis=0)
    both = both.reshape(states + span, slots, blocks, width)
    return both.transpose(2, 1, 0, 3).reshape(blocks, slots, (states + span) * width)


def scan_kernel(
    h0_ref, dt_ref, conv_ref, gate_ref, coef_ref, acc_ref, decay_ref, skip_ref, ow_ref,
    out_ref, ns_ref, b_ref, c_ref, pick_ref, y_ref, sum_ref,
):
    step = pl.program_id(0)
    reqs, draft, _ = out_ref.shape
    states = decay_ref.shape[0]

    @pl.when(step == 0)
    def _():
        for t in range(draft):
            rows = coef_ref[pl.ds(t * reqs, reqs), :]
            for n in range(states):
                b_ref[t * states + n] = jnp.broadcast_to(rows[:, n : n + 1], (reqs, LANES))
                c_ref[t * states + n] = jnp.broadcast_to(
                    rows[:, states + n : states + n + 1], (reqs, LANES)
                )
        sum_ref[...] = jnp.zeros_like(sum_ref)

    accepted = acc_ref[...]
    for tile in range(BLOCK // LANES):
        cols = pl.ds(tile * LANES, LANES)
        decay = [
            jnp.broadcast_to(decay_ref[pl.ds(n, 1), cols], (reqs, LANES)) for n in range(states)
        ]
        state = [
            h0_ref[0, :, pl.ds(n * BLOCK + tile * LANES, LANES)].astype(jnp.float32)
            for n in range(states)
        ]
        values = conv_ref[:, cols].astype(jnp.float32)
        for t in range(draft):
            delta = dt_ref[pl.ds(t * reqs, reqs), cols]
            driven = delta * values[t * reqs : (t + 1) * reqs]
            chosen = accepted == t + 1
            totals = [None, None]
            for n in range(states):
                state[n] = jnp.exp2(delta * decay[n]) * state[n] + driven * b_ref[t * states + n]
                term = c_ref[t * states + n] * state[n]
                totals[n % 2] = term if totals[n % 2] is None else totals[n % 2] + term
                pltpu.store(pick_ref.at[pl.ds(n * reqs, reqs), :], state[n], mask=chosen)
            y_ref[pl.ds(t * reqs, reqs), cols] = totals[0] + totals[1]
        for r in range(reqs):
            ns_ref[pl.ds(r * states, states), cols] = pick_ref[pl.ds(r, states, stride=reqs), :]
    gate = gate_ref[...].astype(jnp.float32)
    mixed = y_ref[...] + skip_ref[...] * conv_ref[...].astype(jnp.float32)
    gated = (mixed * (gate / (1.0 + jnp.exp(-gate)))).astype(jnp.bfloat16)
    added = jnp.dot(gated, ow_ref[...], preferred_element_type=jnp.float32)
    for k in range(sum_ref.shape[0]):
        sum_ref[k] += added[:, k * LANES : (k + 1) * LANES]

    @pl.when(step == pl.num_programs(0) - 1)
    def _():
        for k in range(sum_ref.shape[0]):
            for r in range(reqs):
                rows = sum_ref[k, pl.ds(r, draft, stride=reqs), :]
                out_ref[r, :, pl.ds(k * LANES, LANES)] = rows.astype(jnp.bfloat16)


def scan_layer(h0, dt, conv_rows, projected, coeffs, accepted, decay2, skip, out_weight):
    blocks, reqs, _ = h0.shape
    tokens, inner = dt.shape
    draft = tokens // reqs
    states = decay2.shape[0]
    width = out_weight.shape[1]
    once = lambda j: (0, 0)
    cols = lambda j: (0, j)
    return pl.pallas_call(
        scan_kernel,
        grid=(blocks,),
        out_shape=(
            jax.ShapeDtypeStruct((reqs, draft, width), jnp.bfloat16),
            jax.ShapeDtypeStruct((reqs * states, inner), jnp.float32),
        ),
        in_specs=[
            pl.BlockSpec((1, reqs, states * BLOCK), lambda j: (j, 0, 0)),
            pl.BlockSpec((tokens, BLOCK), cols),
            pl.BlockSpec((tokens, BLOCK), cols),
            pl.BlockSpec((tokens, BLOCK), lambda j: (0, blocks + j)),
            pl.BlockSpec((tokens, 2 * states), once),
            pl.BlockSpec((reqs, LANES), once),
            pl.BlockSpec((states, BLOCK), cols),
            pl.BlockSpec((1, BLOCK), cols),
            pl.BlockSpec((BLOCK, width), lambda j: (j, 0)),
        ],
        out_specs=(
            pl.BlockSpec((reqs, draft, width), lambda j: (0, 0, 0)),
            pl.BlockSpec((reqs * states, BLOCK), cols),
        ),
        scratch_shapes=[
            pltpu.VMEM((draft * states, reqs, LANES), jnp.float32),
            pltpu.VMEM((draft * states, reqs, LANES), jnp.float32),
            pltpu.VMEM((states * reqs, LANES), jnp.float32),
            pltpu.VMEM((tokens, BLOCK), jnp.float32),
            pltpu.VMEM((width // LANES, tokens, LANES), jnp.float32),
        ],
        compiler_params=pltpu.CompilerParams(vmem_limit_bytes=32 << 20),
        cost_estimate=pl.CostEstimate(
            flops=2 * tokens * inner * width, bytes_accessed=8 << 20, transcendentals=tokens * inner * states
        ),
        name="scan_layer",
    )(h0, dt, conv_rows, projected, coeffs, accepted, decay2, skip, out_weight)


def exchange(values):
    return lax.all_to_all(values, "req", split_axis=0, concat_axis=0, tiled=True)


def split_float(values):
    high = values.astype(jnp.bfloat16)
    low = (values - high.astype(jnp.float32)).astype(jnp.bfloat16)
    return high, low


def gather_weights(x_weight, step_weight, vectors, groups):
    channels, mixed = x_weight.shape
    rank = step_weight.shape[0]
    count = vectors.shape[0]
    blocks = lax.axis_size("req")
    high, low = split_float(vectors)
    pad = (-2 * count) % (16 * groups)
    tail = jnp.concatenate([high, low, jnp.zeros((pad, channels), jnp.bfloat16)], axis=0)
    pieces = [x_weight.T, step_weight, tail]
    rows = [p.shape[0] // groups for p in pieces]
    stacked = jnp.concatenate([p.reshape(groups, -1, channels) for p in pieces], axis=1)
    mine = lax.dynamic_index_in_dim(stacked, lax.axis_index("grp"), 0, keepdims=False)
    share = mine.shape[0]
    sent = jnp.broadcast_to(mine[None], (blocks, share, channels))
    held = exchange(sent.reshape(blocks * share, channels))
    full = lax.all_gather(held, "grp", axis=0, tiled=True)
    full = full.reshape(groups, blocks, share, channels).swapaxes(1, 2)
    at = 0
    outs = []
    for size in rows:
        part = full[:, at : at + size].reshape(groups * size, blocks * channels)
        outs.append(part)
        at += size
    x_full, step_full, tail_full = outs
    tail_full = tail_full.astype(jnp.float32)
    return x_full, step_full, tail_full[:count] + tail_full[count : 2 * count]


def on_device(
    groups,
    hidden,
    norm_gain,
    in_weight,
    conv_weight,
    conv_bias,
    x_weight,
    step_weight,
    step_bias,
    log_decay,
    skip_gain,
    out_weight,
    old_states,
    old_edges,
    anchor,
    fresh_flag,
    accepted,
    request_ages,
):
    local_reqs, draft_len, width = hidden.shape
    inner_width = out_weight.shape[0]
    channels = conv_weight.shape[1]
    taps = conv_weight.shape[0]
    state_size = log_decay.shape[0]
    low_rank = step_weight.shape[0]
    span = old_edges.shape[1]
    all_reqs = anchor.shape[0]
    blocks = inner_width // channels
    tokens = draft_len * local_reqs

    arrived = exchange(
        pack(old_states, old_edges, blocks).reshape(all_reqs, (state_size + span) * channels)
    )
    old_slot = jnp.arange(all_reqs, dtype=jnp.int32)
    select = (anchor[:, None] == old_slot[None, :]) & (fresh_flag[:, None] == 0)

    def picked(mask, values):
        return jnp.dot(
            mask.astype(jnp.bfloat16), values, preferred_element_type=jnp.float32
        ).astype(jnp.bfloat16)

    edge_at = state_size * channels
    edges = jnp.concatenate(
        [
            picked(
                select & (span - e <= request_ages)[:, None],
                arrived[:, edge_at + e * channels : edge_at + (e + 1) * channels],
            )
            for e in range(span)
        ],
        axis=1,
    )
    history = exchange(edges).reshape(blocks, local_reqs, span, channels)
    history = history.transpose(2, 1, 0, 3).reshape(span, local_reqs, inner_width)
    starts = exchange(picked(select, arrived[:, :edge_at]))
    if channels == BLOCK:
        starts = starts.reshape(blocks, local_reqs, state_size * BLOCK)
    else:
        starts = starts.reshape(blocks, local_reqs, state_size, channels)
        starts = starts.transpose(1, 2, 0, 3).reshape(local_reqs, state_size, -1, BLOCK)
        starts = starts.transpose(2, 0, 1, 3).reshape(-1, local_reqs, state_size * BLOCK)

    vectors = jnp.concatenate(
        [conv_weight, conv_bias[None], step_bias[None], skip_gain[None], log_decay], axis=0
    )
    x_full, step_full, vectors = gather_weights(x_weight, step_weight, vectors, groups)
    conv_full = vectors[:taps]
    bias_full = vectors[taps]
    step_bias_full = vectors[taps + 1]
    skip_full = vectors[taps + 2 : taps + 3]
    decay2 = jnp.exp(vectors[taps + 3 :]) * (-LOG2E)

    token_major = jnp.swapaxes(hidden, 0, 1).reshape(tokens, width)
    normed = rms_normed(token_major, norm_gain)
    projected = jnp.dot(normed, in_weight, preferred_element_type=jnp.float32).astype(jnp.bfloat16)
    inner_part = projected[:, :inner_width].reshape(draft_len, local_reqs, inner_width)
    sequence = jnp.concatenate([history, inner_part], axis=0).astype(jnp.float32)
    running = bias_full + conv_full[0] * sequence[0:draft_len]
    for offset in range(1, taps):
        running = running + conv_full[offset] * sequence[offset : offset + draft_len]
    conv_rows = jax.nn.silu(running).astype(jnp.bfloat16).reshape(tokens, inner_width)
    mixed_rows = lax.dot_general(
        conv_rows, x_full, (((1,), (1,)), ((), ())), preferred_element_type=jnp.float32
    ).astype(jnp.bfloat16)
    dt = jax.nn.softplus(
        jnp.dot(mixed_rows[:, :low_rank], step_full, preferred_element_type=jnp.float32)
        + step_bias_full
    )
    coeffs = mixed_rows[:, low_rank:].astype(jnp.float32)
    mine = lax.dynamic_slice_in_dim(accepted, lax.axis_index("req") * local_reqs, local_reqs, 0)
    mine = jnp.broadcast_to(mine[:, None], (local_reqs, LANES))
    layer_out, new_states = scan_layer(
        starts, dt, conv_rows, projected, coeffs, mine, decay2, skip_full, out_weight
    )
    return layer_out, new_states.reshape(local_reqs, state_size, inner_width)


def solution(mesh):
    return jax.shard_map(
        functools.partial(on_device, mesh.shape["grp"]),
        mesh=mesh,
        in_specs=(
            P(("grp", "req"), None, None),
            P(),
            P(),
            P(None, "req"),
            P("req"),
            P("req", None),
            P(None, "req"),
            P("req"),
            P(None, "req"),
            P("req"),
            P(),
            P(("grp", "req"), None, None),
            P(("grp", "req"), None, None),
            P("grp"),
            P("grp"),
            P("grp"),
            P("grp"),
        ),
        out_specs=(P(("grp", "req"), None, None), P(("grp", "req"), None, None)),
        check_vma=False,
    )
```

time: 372 us -> 96.8 us (0.26)
  local copies, waits for them, and re-layouts: 191 us -> 9.28 us
  other arithmetic: 47.8 us -> 3.34 us
  blocking collectives: 43.6 us -> 0 us
  between operations: 1.01 us -> 14.3 us
  loops' own time: 12.3 us -> 0 us
  starting transfers between devices: 29.5 us -> 18.2 us
  Pallas kernels: 0 us -> 10.6 us
    unnamed x47 -> x23, local copies, waits for them, and re-layouts: 70.4 us -> 3.54 us
    psum x1 -> x0, blocking collectives: 43.6 us -> none  [on_device(): mixed_rows = lax.psum(partial_value, 'req').astype(jnp.bfloat16)]
    dynamic_update_slice x16 -> x0, local copies, waits for them, and re-layouts: 31.1 us -> none  [on_device(): lax.scan(advance, (start_flat, start_flat), sliced)]
    while x48 -> x0, local copies, waits for them, and re-layouts: 29.4 us -> none
    dynamic_slice x16 -> x0, other arithmetic: 20.9 us -> none  [on_device(): lax.scan(advance, (start_flat, start_flat), sliced)]
    all_to_all x7 -> x0, local copies, waits for them, and re-layouts: 19.8 us -> none  [the longest x1 8.9 us: on_device(): lax.all_to_all(projected, 'req', split_axis=3, concat_axis=2, tiled=True)]
    reduce_sum x16 -> x0, other arithmetic: 14.9 us -> none  [advance(): result = jnp.sum(spread(step_c) * current, axis=0)]
    reshape x5 -> x2, local copies, waits for them, and re-layouts: 13.3 us -> 0.05 us  [the longest x1 0.04 us: on_device(): projected[:, :inner_width].reshape(draft_len, local_reqs, inner_width)]
  transfers between devices with their start and end apart: 5 -> 5, of which waited for: 4 -> 4; matrix products, arithmetic and copies ran while one was open for 23% -> 14% of each run, Pallas kernels for 0% -> 1%
where the time goes in v1:
time: 96.8 us; the launch traced here: 96 us
  waiting for transfers between devices  32.7 us (34%)
  starting transfers between devices  18.2 us (19%)
  between operations  14.3 us (15%)
  Pallas kernels  10.6 us (11%)
  local copies, waits for them, and re-layouts  9.28 us (10%)
  matrix products  7.63 us (8%)
  other arithmetic  3.34 us (3%)
    all_to_all x4, waiting for transfers between devices, exchange(): lax.all_to_all(values, 'req', split_axis=0, concat_axis=0, tiled=True)  32.4 us
    all_to_all x4, starting transfers between devices, exchange(): lax.all_to_all(values, 'req', split_axis=0, concat_axis=0, tiled=True)  18.1 us
    pallas_call x1, Pallas kernels, scan_layer(): pl.pallas_call(scan_kernel, grid=(blocks,), out_shape=(jax.ShapeDtypeStru...  9.31 us
    dot_general x1, matrix products, on_device(): jnp.dot(normed, in_weight, preferred_element_type=jnp.float32)  4.79 us
    unnamed x23, local copies, waits for them, and re-layouts  3.54 us
    slice x4, local copies, waits for them, and re-layouts, gather_weights(): part = full[:, at:at + size].reshape(groups * size, blocks * channels)  2.65 us
  transfers between devices with their start and end apart: 5, of which 4 were waited for; matrix products, arithmetic and copies ran while one was open for 14% of the time, Pallas kernels for 1%

profile of v1, /device:TPU:0, one launch (start us, length us, event | category | flops | bytes accessed | tf_op | source)
XLA Modules:
  0.0 96.0 jit_solution(3314530441273748084)
XLA Ops:
  7.2 1.6 %concatenate.15 = f32[23,256]{1,0:T(8,128)S(1)} concatenate(f32[4,256]{1,0:T(4,128)} %param.20, f32[1,256]{1,0:T(1,128)} %bitcast.89, f32[1,256]{1,0:T(1,128)} %bitcast.90, f32[1,256]{1,0:T(1,128)} %bitcast.91, f32[16,256]{1,0:T(8,128)} %param.25), dimensions={0} | concatenate | bytes 47104 | tf_op jit(solution)/shard_map/concatenate | solution.py:264
  9.0 0.7 fusion.18
  9.7 0.8 broadcast_in_dim.19
  10.5 7.4 %all-to-all-start.2 = ((bf16[8,88,256]{2,1,0:T(8,128)(2,1)}), bf16[8,88,256]{2,1,0:T(8,128)(2,1)S(1)}, u32[]{:S(2)}, u32[]{:S(2)}) async-start(bf16[8,88,256]{2,1,0:T(8,128)(2,1)} %broadcast_in_dim.19), calls=%async_computation.2 | async-start | bytes 720896 | tf_op jit(solution)/shard_map/all_to_all | solution.py:164
  17.9 0.9 copy-done.1
  18.8 1.3 %pack_states.1 = bf16[8,8,4864]{2,1,0:T(8,128)(2,1)} custom-call(f32[128,2048]{1,0:T(8,128)S(1)} %bitcast.62, bf16[3,8,2048]{2,1,0:T(8,128)(2,1)S(1)} %bitcast.63), custom_call_target="tpu_custom_call" | custom-call | tf_op jit(solution)/shard_map/pack_states/pallas_call | solution.py:45
  20.0 8.8 %all-to-all-done.2 = bf16[8,88,256]{2,1,0:T(8,128)(2,1)S(1)} async-done(((bf16[8,88,256]{2,1,0:T(8,128)(2,1)}), bf16[8,88,256]{2,1,0:T(8,128)(2,1)S(1)}, u32[]{:S(2)}, u32[]{:S(2)}) %all-to-all-start.2) | async-done | bytes 360480 | tf_op jit(solution)/shard_map/all_to_all | solution.py:164
  28.9 3.6 %all-to-all-start = ((bf16[8,8,4864]{2,1,0:T(8,128)(2,1)}), bf16[8,8,4864]{2,1,0:T(8,128)(2,1)S(1)}, u32[]{:S(2)}, u32[]{:S(2)}) async-start(bf16[8,8,4864]{2,1,0:T(8,128)(2,1)} %pack_states.1), calls=%async_computation | async-start | bytes 1245184 | tf_op jit(solution)/shard_map/all_to_all | solution.py:164
  33.2 4.8 %convolution_convert_fusion.gate_ref = bf16[128,4096]{1,0:T(8,128)(2,1)S(1)} fusion(bf16[1024,4096]{1,0:T(8,128)(2,1)} %param.19, f32[1024]{0:T(1024)S(1)} %copy-done.5, f32[128]{0:T(128)S(1)} %rsqrt.12, bf16[8,16,1024]{2,1,0:T(8,128)(2,1)S(1)} %copy-done.3), kind=kOutput, calls=%fused_computation | convolution fusion | flops 1074790400 | bytes 9703936 | tf_op jit(solution)/shard_map/dot_general | solution.py:276
  38.0 10.6 %all-to-all-done = bf16[8,8,4864]{2,1,0:T(8,128)(2,1)S(1)} async-done(((bf16[8,8,4864]{2,1,0:T(8,128)(2,1)}), bf16[8,8,4864]{2,1,0:T(8,128)(2,1)S(1)}, u32[]{:S(2)}, u32[]{:S(2)}) %all-to-all-start) | async-done | bytes 622624 | tf_op jit(solution)/shard_map/all_to_all | solution.py:164
  49.3 0.7 maximum_bitcast_fusion
  49.9 3.6 %all-to-all-start.3 = ((bf16[8,8,768]{2,1,0:T(8,128)(2,1)}), bf16[8,8,768]{2,1,0:T(8,128)(2,1)S(1)}, u32[]{:S(2)}, u32[]{:S(2)}) async-start(bf16[8,8,768]{2,1,0:T(8,128)(2,1)} %maximum_bitcast_fusion), calls=%async_computation.3 | async-start | bytes 196608 | tf_op jit(solution)/shard_map/all_to_all | solution.py:164
  53.7 1.1 %fusion = bf16[8,8,4096]{2,1,0:T(8,128)(2,1)} fusion(bf16[64,4864]{1,0:T(8,128)(2,1)S(1)} %bitcast.69, s32[64]{0:T(128)S(1)} %copy-done.6, pred[64]{0:T(512)(128)(4,1)S(1)} %get-tuple-element.18), kind=kOutput, calls=%fused_computation.2 | convolution fusion | flops 33824768 | bytes 1049600 | tf_op jit(solution)/shard_map/dot_general | solution.py:239
  54.8 5.8 %all-to-all-done.3 = bf16[8,8,768]{2,1,0:T(8,128)(2,1)S(1)} async-done(((bf16[8,8,768]{2,1,0:T(8,128)(2,1)}), bf16[8,8,768]{2,1,0:T(8,128)(2,1)S(1)}, u32[]{:S(2)}, u32[]{:S(2)}) %all-to-all-start.3) | async-done | bytes 98336 | tf_op jit(solution)/shard_map/all_to_all | solution.py:164
  60.7 3.5 %all-to-all-start.1 = ((bf16[8,8,4096]{2,1,0:T(8,128)(2,1)}), bf16[8,8,4096]{2,1,0:T(8,128)(2,1)S(1)}, u32[]{:S(2)}, u32[]{:S(2)}) async-start(bf16[8,8,4096]{2,1,0:T(8,128)(2,1)} %fusion), calls=%async_computation.1 | async-start | bytes 1048576 | tf_op jit(solution)/shard_map/all_to_all | solution.py:164
  64.3 1.1 %slice.120 = bf16[4,32,8,256]{3,1,2,0:T(8,128)(2,1)S(1)} slice(bf16[4,88,8,256]{3,1,2,0:T(8,128)(2,1)} %bitcast.73), slice={[0:4], [40:72], [0:8], [0:256]} | slice | bytes 1048576 | tf_op jit(solution)/shard_map/slice | solution.py:193
  65.4 1.0 %slice_convert_fusion = f32[4,16,8,256]{3,1,2,0:T(8,128)S(1)} fusion(bf16[4,88,8,256]{3,1,2,0:T(8,128)(2,1)} %bitcast.74), kind=kLoop, calls=%fused_computation.28 | loop fusion | flops 131072 | bytes 786432 | tf_op jit(solution)/shard_map/convert_element_type | solution.py:197
  66.4 1.1 %slice.118 = bf16[4,40,8,256]{3,1,2,0:T(8,128)(2,1)S(1)} slice(bf16[4,88,8,256]{3,1,2,0:T(8,128)(2,1)} %bitcast.75), slice={[0:4], [0:40], [0:8], [0:256]} | slice | bytes 1310720 | tf_op jit(solution)/shard_map/slice | solution.py:193
  68.9 0.5 fusion.10.conv_ref
  69.3 0.4 convolution_convert_fusion.2
  69.7 0.7 compare_select_fusion.dt_ref
  70.5 7.1 %all-to-all-done.1.h0_ref = bf16[8,8,4096]{2,1,0:T(8,128)(2,1)S(1)} async-done(((bf16[8,8,4096]{2,1,0:T(8,128)(2,1)}), bf16[8,8,4096]{2,1,0:T(8,128)(2,1)S(1)}, u32[]{:S(2)}, u32[]{:S(2)}) %all-to-all-start.1) | async-done | bytes 524320 | tf_op jit(solution)/shard_map/all_to_all | solution.py:164
  77.7 2.2 %copy-done.2 = bf16[2048,1024]{1,0:T(8,128)(2,1)S(1)} copy-done((bf16[2048,1024]{1,0:T(8,128)(2,1)S(1)}, bf16[2048,1024]{1,0:T(8,128)(2,1)}, u32[]{:S(2)}) %copy-start.2) | copy-done | bytes 4194328
  79.9 9.3 %scan_layer.1 = (bf16[8,16,1024]{2,1,0:T(8,128)(2,1)}, f32[128,2048]{1,0:T(8,128)}) custom-call(bf16[8,8,4096]{2,1,0:T(8,128)(2,1)S(1)} %all-to-all-done.1.h0_ref, f32[128,2048]{1,0:T(8,128)S(1)} %compare_select_fusion.dt_ref, bf16[128,2048]{1,0:T(8,128)(2,1)S(1)} %fusion.10.conv_ref, bf16[128,4096]{1,0:T(8,128)(2,1)S(1)} %convolution_convert_fusion.gate_ref, ...), custom_call_target="tpu_custom_call" | custom-call | flops 536870912 | bytes 8388608 | tf_op jit(solution)/shard_map/scan_layer/pallas_call | solution.py:126
  (47 shorter events, 3.0 us)
Async XLA Ops:
  7.2 10.7 %copy-start = (f32[8,16,2048]{2,1,0:T(8,128)S(1)}, f32[8,16,2048]{2,1,0:T(8,128)}, u32[]{:S(2)}) copy-start(f32[8,16,2048]{2,1,0:T(8,128)} %param.28) | copy-start | bytes 3145732
  9.7 22.8 %copy-start.3 = (bf16[8,16,1024]{2,1,0:T(8,128)(2,1)S(1)}, bf16[8,16,1024]{2,1,0:T(8,128)(2,1)}, u32[]{:S(2)}) copy-start(bf16[8,16,1024]{2,1,0:T(8,128)(2,1)} %param.17) | copy-start | bytes 786436
  10.5 22.4 %copy-start.7 = (s32[64]{0:T(128)S(1)}, s32[64]{0:T(128)}, u32[]{:S(2)}) copy-start(s32[64]{0:T(128)} %param.33) | copy-start | bytes 772
  10.5 22.4 %copy-start.8 = (s32[64]{0:T(128)S(1)}, s32[64]{0:T(128)}, u32[]{:S(2)}) copy-start(s32[64]{0:T(128)} %param.31) | copy-start | bytes 772
  10.5 22.7 %copy-start.5 = (f32[1024]{0:T(1024)S(1)}, f32[1024]{0:T(1024)}, u32[]{:S(2)}) copy-start(f32[1024]{0:T(1024)} %param.18) | copy-start | bytes 12292
  10.5 18.4 %all-to-all-start.2 = ((bf16[8,88,256]{2,1,0:T(8,128)(2,1)}), bf16[8,88,256]{2,1,0:T(8,128)(2,1)S(1)}, u32[]{:S(2)}, u32[]{:S(2)}) async-start(bf16[8,88,256]{2,1,0:T(8,128)(2,1)} %broadcast_in_dim.19), calls=%async_computation.2 | async-start | bytes 720896 | tf_op jit(solution)/shard_map/all_to_all | solution.py:164
  17.9 0.9 copy-start.1
  28.9 4.0 %copy-start.4 = (bf16[8,88,256]{2,1,0:T(8,128)(2,1)}, bf16[8,88,256]{2,1,0:T(8,128)(2,1)S(1)}, u32[]{:S(2)}) copy-start(bf16[8,88,256]{2,1,0:T(8,128)(2,1)S(1)} %all-to-all-done.2) | copy-start | bytes 1081348
  28.9 19.8 %all-to-all-start = ((bf16[8,8,4864]{2,1,0:T(8,128)(2,1)}), bf16[8,8,4864]{2,1,0:T(8,128)(2,1)S(1)}, u32[]{:S(2)}, u32[]{:S(2)}) async-start(bf16[8,8,4864]{2,1,0:T(8,128)(2,1)} %pack_states.1), calls=%async_computation | async-start | bytes 1245184 | tf_op jit(solution)/shard_map/all_to_all | solution.py:164
  32.5 31.8 %all-gather.2.cloned.1.call-start = ((), (), s32[]{:S(2)}) async-start(), calls=%async_computation.4 | async-start | bytes 1802240 | tf_op jit(solution)/shard_map/all_gather | solution.py:188
  33.2 15.4 %copy-start.6 = (s32[64]{0:T(128)S(1)}, s32[64]{0:T(128)}, u32[]{:S(2)}) copy-start(s32[64]{0:T(128)} %param.30) | copy-start | bytes 772
  33.2 20.4 %copy-start.9 = (s32[64]{0:T(128)S(1)}, s32[64]{0:T(128)}, u32[]{:S(2)}) copy-start(s32[64]{0:T(128)} %param.32) | copy-start | bytes 772
  49.9 10.8 %all-to-all-start.3 = ((bf16[8,8,768]{2,1,0:T(8,128)(2,1)}), bf16[8,8,768]{2,1,0:T(8,128)(2,1)S(1)}, u32[]{:S(2)}, u32[]{:S(2)}) async-start(bf16[8,8,768]{2,1,0:T(8,128)(2,1)} %maximum_bitcast_fusion), calls=%async_computation.3 | async-start | bytes 196608 | tf_op jit(solution)/shard_map/all_to_all | solution.py:164
  60.7 16.9 %all-to-all-start.1 = ((bf16[8,8,4096]{2,1,0:T(8,128)(2,1)}), bf16[8,8,4096]{2,1,0:T(8,128)(2,1)S(1)}, u32[]{:S(2)}, u32[]{:S(2)}) async-start(bf16[8,8,4096]{2,1,0:T(8,128)(2,1)} %fusion), calls=%async_computation.1 | async-start | bytes 1048576 | tf_op jit(solution)/shard_map/all_to_all | solution.py:164
  77.7 2.2 %copy-start.2 = (bf16[2048,1024]{1,0:T(8,128)(2,1)S(1)}, bf16[2048,1024]{1,0:T(8,128)(2,1)}, u32[]{:S(2)}) copy-start(bf16[2048,1024]{1,0:T(8,128)(2,1)} %ow_ref.1) | copy-start | bytes 12582916
Sparse Core Ops, SparseCore 0:
  34.9 20.3 all-gather.1

commit v2 on v1

v2 whole, which is shorter than its diff:
```python
import functools

import jax
import jax.numpy as jnp
from jax import lax
from jax.experimental import pallas as pl
from jax.experimental.pallas import tpu as pltpu
from jax.sharding import PartitionSpec as P

EPS = 1e-05
LOG2E = 1.4426950408889634
LANES = 128
BLOCK = 256
SHARE = 88


def rms_normed(values_in, norm_gain):
    values = values_in.astype(jnp.float32)
    factor = lax.rsqrt(jnp.mean(values * values, axis=-1, keepdims=True) + EPS)
    return (values * factor * norm_gain).astype(jnp.bfloat16)


def pack_kernel(state_ref, edge_ref, out_ref, tile_ref):
    blocks, slots, _ = out_ref.shape
    width = state_ref.shape[1] // blocks
    states = state_ref.shape[0] // slots
    for dest in range(blocks):
        cols = pl.ds(dest * width, width)
        for part in range(width // LANES):
            at = dest * width + part * LANES
            tile = tile_ref.at[at // LANES]
            tile[...] = state_ref[:, pl.ds(at, LANES)]
            for n in range(states):
                rows = tile[pl.ds(n, slots, stride=states), :]
                out_ref[dest, :, pl.ds(n * width + part * LANES, LANES)] = rows.astype(jnp.bfloat16)
        for e in range(edge_ref.shape[0]):
            out_ref[dest, :, pl.ds((states + e) * width, width)] = edge_ref[e, :, cols]


def pack(old_states, old_edges, blocks):
    slots, states, inner = old_states.shape
    span = old_edges.shape[1]
    width = inner // blocks
    edges = jnp.swapaxes(old_edges, 0, 1)
    if width % LANES == 0 and slots == 8:
        return pl.pallas_call(
            pack_kernel,
            out_shape=jax.ShapeDtypeStruct((blocks, slots, (states + span) * width), jnp.bfloat16),
            in_specs=[pl.BlockSpec(memory_space=pltpu.VMEM)] * 2,
            out_specs=pl.BlockSpec(memory_space=pltpu.VMEM),
            scratch_shapes=[pltpu.VMEM((inner // LANES, slots * states, LANES), jnp.float32)],
            compiler_params=pltpu.CompilerParams(vmem_limit_bytes=16 << 20),
            name="pack_states",
        )(old_states.reshape(slots * states, inner), edges)
    lead = jnp.swapaxes(old_states.astype(jnp.bfloat16), 0, 1)
    both = jnp.concatenate([lead, edges], axis=0)
    both = both.reshape(states + span, slots, blocks, width)
    return both.transpose(2, 1, 0, 3).reshape(blocks, slots, (states + span) * width)


def share_kernel(group_ref, xt_ref, sw_ref, cw_ref, cb_ref, sb_ref, sk_ref, ld_ref, out_ref, vec_ref):
    rank = sw_ref.shape[0]
    groups = rank // 32
    vec_ref[...] = jnp.zeros_like(vec_ref)
    vec_ref[pl.ds(0, 4), :] = cw_ref[...]
    vec_ref[pl.ds(4, 1), :] = cb_ref[...]
    vec_ref[pl.ds(5, 1), :] = sb_ref[...]
    vec_ref[pl.ds(6, 1), :] = sk_ref[...]
    vec_ref[pl.ds(8, 16), :] = ld_ref[...]
    for k in range(groups):

        @pl.when(group_ref[0] == k)
        def _():
            vec = vec_ref[pl.ds(16 * (k % 2), 16), :]
            high = vec.astype(jnp.bfloat16).astype(jnp.float32)
            part = high if k < 2 else vec - high
            rows = [
                xt_ref[pl.ds(32 * k, 32), :].astype(jnp.float32),
                xt_ref[pl.ds(rank + 8 * k, 8), :].astype(jnp.float32),
                part[:8],
                sw_ref[pl.ds(32 * k, 32), :].astype(jnp.float32),
                part[8:],
            ]
            out_ref[...] = jnp.concatenate(rows, axis=0).astype(jnp.bfloat16)


def weight_share(groups, x_weight, step_weight, conv_weight, conv_bias, step_bias, skip_gain, log_decay):
    channels = x_weight.shape[0]
    rank = step_weight.shape[0]
    xt = x_weight.T
    group = lax.axis_index("grp").astype(jnp.int32)
    if channels % LANES == 0:
        return pl.pallas_call(
            share_kernel,
            out_shape=jax.ShapeDtypeStruct((SHARE, channels), jnp.bfloat16),
            in_specs=[pl.BlockSpec(memory_space=pltpu.SMEM)] + [pl.BlockSpec(memory_space=pltpu.VMEM)] * 7,
            out_specs=pl.BlockSpec(memory_space=pltpu.VMEM),
            scratch_shapes=[pltpu.VMEM((32, channels), jnp.float32)],
            name="weight_share",
        )(
            group[None], xt, step_weight, conv_weight, conv_bias[None], step_bias[None],
            skip_gain[None], log_decay,
        )
    vec = jnp.concatenate(
        [conv_weight, conv_bias[None], step_bias[None], skip_gain[None], jnp.zeros_like(conv_bias)[None], log_decay],
        axis=0,
    )
    vec = jnp.pad(vec, ((0, 8), (0, 0)))
    high = vec.astype(jnp.bfloat16)
    both = jnp.concatenate([high, (vec - high.astype(jnp.float32)).astype(jnp.bfloat16)], axis=0)
    both = both.reshape(4, 16, channels)
    stacked = jnp.concatenate(
        [
            xt[:rank].reshape(4, 32, channels),
            xt[rank:].reshape(4, 8, channels),
            both[:, :8],
            step_weight.reshape(4, 32, channels),
            both[:, 8:],
        ],
        axis=1,
    )
    return lax.dynamic_index_in_dim(stacked, group, 0, keepdims=False)


def doubled(values, axis):
    size = lax.axis_size(axis)
    bit = size // 2
    while bit:
        other = lax.ppermute(values, axis, [(i, i ^ bit) for i in range(size)])
        values = jnp.concatenate([values, other], axis=0)
        bit //= 2
    return values


def places(axis):
    size = lax.axis_size(axis)
    offset = jnp.arange(size, dtype=jnp.int32) ^ lax.axis_index(axis).astype(jnp.int32)
    place = jnp.zeros_like(offset)
    bit, top = 1, size // 2
    while top:
        place = place | jnp.where((offset & bit) != 0, top, 0)
        bit, top = bit * 2, top // 2
    return place


def block_weights(w_ref, q_ref, j_ref, j):
    at = j_ref[j]
    quarters = [w_ref.at[q_ref[q], at] for q in range(4)]
    f32 = jnp.float32
    xw = jnp.concatenate(
        [w[pl.ds(0, 32), :].astype(f32) for w in quarters] + [w[pl.ds(32, 8), :].astype(f32) for w in quarters],
        axis=0,
    ).astype(jnp.bfloat16)
    sw = jnp.concatenate([w[pl.ds(48, 32), :] for w in quarters], axis=0)
    first = [w[pl.ds(40, 8), :].astype(f32) for w in quarters]
    second = [w[pl.ds(80, 8), :].astype(f32) for w in quarters]
    high = jnp.concatenate([first[0], second[0], first[1]], axis=0)
    low = jnp.concatenate([first[2], second[2], first[3]], axis=0)
    return xw, sw, high + low


def silu(values):
    return values / (1.0 + jnp.exp(-values))


def convolved(sequence, vec, count):
    reqs = (sequence.shape[0] - count) // 3
    running = vec[4:5]
    for k in range(4):
        running = running + vec[k : k + 1] * sequence[k * reqs : k * reqs + count]
    return silu(running).astype(jnp.bfloat16)


def softplus(values):
    return jnp.maximum(values, 0.0) + jnp.log1p(jnp.exp(-jnp.abs(values)))


def mixed_of(conv, xw):
    return lax.dot_general(conv, xw, (((1,), (1,)), ((), ())), preferred_element_type=jnp.float32)


def early_kernel(q_ref, j_ref, inner_ref, w_ref, conv_ref, dt_ref, coef_ref, vec_ref):
    blocks = w_ref.shape[1]
    count = conv_ref.shape[0]
    rank = coef_ref.shape[1] * 4
    mixed = jnp.zeros((count, rank + coef_ref.shape[1]), jnp.float32)
    steps = []
    for j in range(blocks):
        cols = pl.ds(j * BLOCK, BLOCK)
        xw, sw, vec = block_weights(w_ref, q_ref, j_ref, j)
        conv = convolved(inner_ref[:, cols].astype(jnp.float32), vec, count)
        conv_ref[:, cols] = conv
        vec_ref[:, cols] = vec
        mixed = mixed + mixed_of(conv, xw)
        steps.append((sw, vec[5:6]))
    rounded = mixed.astype(jnp.bfloat16)
    coef_ref[...] = rounded[:, rank:].astype(jnp.float32)
    for j in range(blocks):
        cols = pl.ds(j * BLOCK, BLOCK)
        sw, bias = steps[j]
        dt_ref[:, cols] = softplus(
            jnp.dot(rounded[:, :rank], sw, preferred_element_type=jnp.float32) + bias
        )


def early(q_place, j_place, projected, weights, late):
    tokens = projected.shape[0]
    blocks = weights.shape[1]
    inner = blocks * BLOCK
    count = tokens - late
    smem = pl.BlockSpec(memory_space=pltpu.SMEM)
    return pl.pallas_call(
        early_kernel,
        grid=(1,),
        out_shape=(
            jax.ShapeDtypeStruct((count, inner), jnp.bfloat16),
            jax.ShapeDtypeStruct((count, inner), jnp.float32),
            jax.ShapeDtypeStruct((count, 32), jnp.float32),
            jax.ShapeDtypeStruct((24, inner), jnp.float32),
        ),
        in_specs=[
            smem,
            smem,
            pl.BlockSpec((tokens, inner), lambda i: (0, 0)),
            pl.BlockSpec(weights.shape, lambda i: (0, 0, 0, 0)),
        ],
        out_specs=(
            pl.BlockSpec((count, inner), lambda i: (0, 0)),
            pl.BlockSpec((count, inner), lambda i: (0, 0)),
            pl.BlockSpec((count, 32), lambda i: (0, 0)),
            pl.BlockSpec((24, inner), lambda i: (0, 0)),
        ),
        compiler_params=pltpu.CompilerParams(vmem_limit_bytes=32 << 20),
        cost_estimate=pl.CostEstimate(flops=140_000_000, bytes_accessed=4 << 20, transcendentals=800_000),
        name="early_tokens",
    )(q_place, j_place, projected, weights)


def scan_kernel(
    q_ref, j_ref, moved_ref, inner_ref, w_ref, dt_ref, conv_ref, gate_ref, coef_ref, acc_ref, vec_ref, ow_ref,
    out_ref, ns_ref, b_ref, c_ref, pick_ref, y_ref, sum_ref, dt_late, conv_late,
):
    step = pl.program_id(0)
    reqs, draft, _ = out_ref.shape
    states = 16
    blocks = moved_ref.shape[0]
    late = conv_late.shape[1]
    rank = coef_ref.shape[1] * 4

    def spread(rows, t):
        for n in range(states):
            b_ref[t * states + n] = jnp.broadcast_to(rows[:, n : n + 1], (reqs, LANES))
            c_ref[t * states + n] = jnp.broadcast_to(
                rows[:, states + n : states + n + 1], (reqs, LANES)
            )

    @pl.when(step == 0)
    def _():
        mixed = jnp.zeros((late, rank + coef_ref.shape[1]), jnp.float32)
        steps = []
        for j in range(blocks):
            xw, sw, vec = block_weights(w_ref, q_ref, j_ref, j)
            history = [
                moved_ref[j, :, pl.ds((states + e) * BLOCK, BLOCK)].astype(jnp.float32) for e in range(3)
            ]
            drafted = inner_ref[:, pl.ds(j * BLOCK, BLOCK)].astype(jnp.float32)[:late]
            conv = convolved(jnp.concatenate(history + [drafted], axis=0), vec, late)
            conv_late[j] = conv.astype(jnp.float32)
            mixed = mixed + mixed_of(conv, xw)
            steps.append((sw, vec[5:6]))
        rounded = mixed.astype(jnp.bfloat16)
        for j in range(blocks):
            sw, bias = steps[j]
            dt_late[j] = softplus(
                jnp.dot(rounded[:, :rank], sw, preferred_element_type=jnp.float32) + bias
            )
        coefs = rounded[:, rank:].astype(jnp.float32)
        for t in range(draft):
            if t * reqs < late:
                spread(coefs[t * reqs : (t + 1) * reqs], t)
            else:
                spread(coef_ref[pl.ds(t * reqs - late, reqs), :], t)
        sum_ref[...] = jnp.zeros_like(sum_ref)

    accepted = acc_ref[...]
    for tile in range(BLOCK // LANES):
        cols = pl.ds(tile * LANES, LANES)
        decay2 = jnp.exp(vec_ref[pl.ds(8, states), cols]) * (-LOG2E)
        decay = [jnp.broadcast_to(decay2[n : n + 1], (reqs, LANES)) for n in range(states)]
        skip = vec_ref[pl.ds(6, 1), cols]
        state = [
            moved_ref[step, :, pl.ds(n * BLOCK + tile * LANES, LANES)].astype(jnp.float32)
            for n in range(states)
        ]
        values = conv_ref[:, cols].astype(jnp.float32)
        for t in range(draft):
            at = t * reqs - late
            if at < 0:
                delta = dt_late[step, pl.ds(t * reqs, reqs), cols]
                value = conv_late[step, pl.ds(t * reqs, reqs), cols]
            else:
                delta = dt_ref[pl.ds(at, reqs), cols]
                value = values[at : at + reqs]
            driven = delta * value
            chosen = accepted == t + 1
            totals = [None, None]
            for n in range(states):
                state[n] = jnp.exp2(delta * decay[n]) * state[n] + driven * b_ref[t * states + n]
                term = c_ref[t * states + n] * state[n]
                totals[n % 2] = term if totals[n % 2] is None else totals[n % 2] + term
                pltpu.store(pick_ref.at[pl.ds(n * reqs, reqs), :], state[n], mask=chosen)
            y_ref[pl.ds(t * reqs, reqs), cols] = totals[0] + totals[1] + skip * value
        for r in range(reqs):
            ns_ref[pl.ds(r * states, states), cols] = pick_ref[pl.ds(r, states, stride=reqs), :]
    gated = (y_ref[...] * silu(gate_ref[...].astype(jnp.float32))).astype(jnp.bfloat16)
    added = jnp.dot(gated, ow_ref[...], preferred_element_type=jnp.float32)
    for k in range(sum_ref.shape[0]):
        sum_ref[k] += added[:, k * LANES : (k + 1) * LANES]

    @pl.when(step == pl.num_programs(0) - 1)
    def _():
        for k in range(sum_ref.shape[0]):
            for r in range(reqs):
                rows = sum_ref[k, pl.ds(r, draft, stride=reqs), :]
                out_ref[r, :, pl.ds(k * LANES, LANES)] = rows.astype(jnp.bfloat16)


def scan_layer(q_place, j_place, moved, weights, dt, conv_rows, projected, coeffs, accepted, vectors, out_weight):
    blocks, reqs, _ = moved.shape
    count, inner = dt.shape
    tokens = projected.shape[0]
    late = tokens - count
    draft = tokens // reqs
    states = 16
    width = out_weight.shape[1]
    smem = pl.BlockSpec(memory_space=pltpu.SMEM)
    once = lambda j: (0, 0)
    cols = lambda j: (0, j)
    return pl.pallas_call(
        scan_kernel,
        grid=(blocks,),
        out_shape=(
            jax.ShapeDtypeStruct((reqs, draft, width), jnp.bfloat16),
            jax.ShapeDtypeStruct((reqs * states, inner), jnp.float32),
        ),
        in_specs=[
            smem,
            smem,
            pl.BlockSpec(moved.shape, lambda j: (0, 0, 0)),
            pl.BlockSpec((32, inner), once),
            pl.BlockSpec(weights.shape, lambda j: (0, 0, 0, 0)),
            pl.BlockSpec((count, BLOCK), cols),
            pl.BlockSpec((count, BLOCK), cols),
            pl.BlockSpec((tokens, BLOCK), lambda j: (0, blocks + j)),
            pl.BlockSpec((count, 2 * states), once),
            pl.BlockSpec((reqs, LANES), once),
            pl.BlockSpec((24, BLOCK), cols),
            pl.BlockSpec((BLOCK, width), lambda j: (j, 0)),
        ],
        out_specs=(
            pl.BlockSpec((reqs, draft, width), lambda j: (0, 0, 0)),
            pl.BlockSpec((reqs * states, BLOCK), cols),
        ),
        scratch_shapes=[
            pltpu.VMEM((draft * states, reqs, LANES), jnp.float32),
            pltpu.VMEM((draft * states, reqs, LANES), jnp.float32),
            pltpu.VMEM((states * reqs, LANES), jnp.float32),
            pltpu.VMEM((tokens, BLOCK), jnp.float32),
            pltpu.VMEM((width // LANES, tokens, LANES), jnp.float32),
            pltpu.VMEM((blocks, late, BLOCK), jnp.float32),
            pltpu.VMEM((blocks, late, BLOCK), jnp.float32),
        ],
        compiler_params=pltpu.CompilerParams(vmem_limit_bytes=32 << 20),
        cost_estimate=pl.CostEstimate(
            flops=2 * tokens * inner * width, bytes_accessed=8 << 20, transcendentals=tokens * inner * states
        ),
        name="scan_layer",
    )(q_place, j_place, moved, projected, weights, dt, conv_rows, projected, coeffs, accepted, vectors, out_weight)


def exchange(values):
    return lax.all_to_all(values, "req", split_axis=0, concat_axis=0, tiled=True)


def select_kernel(mask_ref, arrived_ref, out_ref):
    width = arrived_ref.shape[1] // 19
    at = 16 * width
    spans = [(0, 0, at)] + [(e + 1, at + e * width, width) for e in range(3)]
    for which, start, size in spans:
        cols = pl.ds(start, size)
        out_ref[:, cols] = jnp.dot(
            mask_ref[which], arrived_ref[:, cols], preferred_element_type=jnp.float32
        ).astype(jnp.bfloat16)


def select(masks, arrived):
    if arrived.shape[1] % (19 * LANES) == 0:
        return pl.pallas_call(
            select_kernel,
            out_shape=jax.ShapeDtypeStruct(arrived.shape, jnp.bfloat16),
            in_specs=[pl.BlockSpec(memory_space=pltpu.VMEM)] * 2,
            out_specs=pl.BlockSpec(memory_space=pltpu.VMEM),
            compiler_params=pltpu.CompilerParams(vmem_limit_bytes=16 << 20),
            name="select_slots",
        )(masks, arrived)
    width = arrived.shape[1] // 19
    cut = [0] + [(16 + e) * width for e in range(4)]
    return jnp.concatenate(
        [
            jnp.dot(
                masks[i], arrived[:, cut[i] : cut[i + 1]], preferred_element_type=jnp.float32
            ).astype(jnp.bfloat16)
            for i in range(4)
        ],
        axis=1,
    )


def on_device(
    groups,
    hidden,
    norm_gain,
    in_weight,
    conv_weight,
    conv_bias,
    x_weight,
    step_weight,
    step_bias,
    log_decay,
    skip_gain,
    out_weight,
    old_states,
    old_edges,
    anchor,
    fresh_flag,
    accepted,
    request_ages,
):
    local_reqs, draft_len, width = hidden.shape
    inner_width = out_weight.shape[0]
    channels = conv_weight.shape[1]
    state_size = log_decay.shape[0]
    span = old_edges.shape[1]
    all_reqs = anchor.shape[0]
    blocks = inner_width // channels
    tokens = draft_len * local_reqs

    arrived = exchange(
        pack(old_states, old_edges, blocks).reshape(all_reqs, (state_size + span) * channels)
    )
    old_slot = jnp.arange(all_reqs, dtype=jnp.int32)
    chosen = (anchor[:, None] == old_slot[None, :]) & (fresh_flag[:, None] == 0)
    masks = jnp.stack([chosen] + [chosen & (span - e <= request_ages)[:, None] for e in range(span)])
    moved = exchange(select(masks.astype(jnp.bfloat16), arrived))

    share = weight_share(
        groups, x_weight, step_weight, conv_weight, conv_bias, step_bias, skip_gain, log_decay
    )
    weights = doubled(doubled(share[None], "req")[None], "grp")
    q_place, j_place = places("grp"), places("req")
    if channels != BLOCK:
        moved = moved.reshape(blocks, local_reqs, state_size + span, channels).transpose(1, 2, 0, 3)
        moved = moved.reshape(local_reqs, state_size + span, -1, BLOCK).transpose(2, 0, 1, 3)
        weights = jnp.take(weights, j_place, axis=1).swapaxes(1, 2)
        weights = weights.reshape(groups, SHARE, -1, BLOCK).swapaxes(1, 2)
        j_place = jnp.arange(inner_width // BLOCK, dtype=jnp.int32)
    moved = moved.reshape(inner_width // BLOCK, local_reqs, (state_size + span) * BLOCK)

    token_major = jnp.swapaxes(hidden, 0, 1).reshape(tokens, width)
    normed = rms_normed(token_major, norm_gain)
    projected = jnp.dot(normed, in_weight, preferred_element_type=jnp.float32).astype(jnp.bfloat16)
    conv_rows, dt, coeffs, vectors = early(q_place, j_place, projected, weights, span * local_reqs)
    mine = lax.dynamic_slice_in_dim(accepted, lax.axis_index("req") * local_reqs, local_reqs, 0)
    mine = jnp.broadcast_to(mine[:, None], (local_reqs, LANES))
    layer_out, new_states = scan_layer(
        q_place, j_place, moved, weights, dt, conv_rows, projected, coeffs, mine, vectors, out_weight
    )
    return layer_out, new_states.reshape(local_reqs, state_size, inner_width)


def solution(mesh):
    return jax.shard_map(
        functools.partial(on_device, mesh.shape["grp"]),
        mesh=mesh,
        in_specs=(
            P(("grp", "req"), None, None),
            P(),
            P(),
            P(None, "req"),
            P("req"),
            P("req", None),
            P(None, "req"),
            P("req"),
            P(None, "req"),
            P("req"),
            P(),
            P(("grp", "req"), None, None),
            P(("grp", "req"), None, None),
            P("grp"),
            P("grp"),
            P("grp"),
            P("grp"),
        ),
        out_specs=(P(("grp", "req"), None, None), P(("grp", "req"), None, None)),
        check_vma=False,
    )
```

time: 96.8 us -> 70 us (0.72)
  waiting for transfers between devices: 32.7 us -> 17.6 us
  between operations: 14.3 us -> 0.83 us
  Pallas kernels: 10.6 us -> 15.7 us
  matrix products: 7.63 us -> 4.84 us
  other arithmetic: 3.34 us -> 0.65 us
  starting transfers between devices: 18.2 us -> 19.6 us
    all_to_all x4 -> x2, waiting for transfers between devices: 32.4 us -> 3.7 us  [exchange(): lax.all_to_all(values, 'req', split_axis=0, concat_axis=0, tiled=True)]
    ppermute x0 -> x5, waiting for transfers between devices: none -> 13.8 us  [doubled(): other = lax.ppermute(values, axis, [(i, i ^ bit) for i in range(size)])]
    ppermute x0 -> x5, starting transfers between devices: none -> 9.56 us  [doubled(): other = lax.ppermute(values, axis, [(i, i ^ bit) for i in range(size)])]
    all_to_all x4 -> x2, starting transfers between devices: 18.1 us -> 10.1 us  [exchange(): lax.all_to_all(values, 'req', split_axis=0, concat_axis=0, tiled=True)]
    unnamed x23 -> x36, local copies, waits for them, and re-layouts: 3.54 us -> 9.99 us
    pallas_call x0 -> x3, Pallas kernels: none -> 4.46 us  [the longest x1 1.68 us: early(): pl.pallas_call(early_kernel, grid=(1,), out_shape=(jax.ShapeDtypeStruct((...]
    dot_general x6 -> x0, matrix products: 2.84 us -> none  [the longest x4 1.75 us: picked(): jnp.dot(mask.astype(jnp.bfloat16), values, preferred_element_type=jnp.flo...]
    slice x5 -> x0, local copies, waits for them, and re-layouts: 2.69 us -> none  [the longest x4 2.65 us: gather_weights(): part = full[:, at:at + size].reshape(groups * size, blocks * channels)]
  transfers between devices with their start and end apart: 5 -> 7, of which waited for: 4 -> 3; matrix products, arithmetic and copies ran while one was open for 14% -> 8% of each run, Pallas kernels for 1% -> 6%
where the time goes in v2:
time: 70 us; the launch traced here: 69.5 us
  starting transfers between devices  19.6 us (28%)
  waiting for transfers between devices  17.6 us (25%)
  Pallas kernels  15.7 us (22%)
  local copies, waits for them, and re-layouts  10.2 us (15%)
  matrix products  4.84 us (7%)
  between operations  0.83 us (1%)
    ppermute x5, waiting for transfers between devices, doubled(): other = lax.ppermute(values, axis, [(i, i ^ bit) for i in range(size)])  13.8 us
    all_to_all x2, starting transfers between devices, exchange(): lax.all_to_all(values, 'req', split_axis=0, concat_axis=0, tiled=True)  10.1 us
    pallas_call x1, Pallas kernels, scan_layer(): pl.pallas_call(scan_kernel, grid=(blocks,), out_shape=(jax.ShapeDtypeStru...  10 us
    unnamed x36, local copies, waits for them, and re-layouts  9.99 us
    ppermute x5, starting transfers between devices, doubled(): other = lax.ppermute(values, axis, [(i, i ^ bit) for i in range(size)])  9.56 us
    dot_general x1, matrix products, on_device(): jnp.dot(normed, in_weight, preferred_element_type=jnp.float32)  4.84 us
    all_to_all x2, waiting for transfers between devices, exchange(): lax.all_to_all(values, 'req', split_axis=0, concat_axis=0, tiled=True)  3.7 us
    pallas_call x1, Pallas kernels, early(): pl.pallas_call(early_kernel, grid=(1,), out_shape=(jax.ShapeDtypeStruct((...  1.68 us
  transfers between devices with their start and end apart: 7, of which 3 were waited for; matrix products, arithmetic and copies ran while one was open for 8% of the time, Pallas kernels for 6%

profile of v2, /device:TPU:0, one launch (start us, length us, event | category | flops | bytes accessed | tf_op | source)
XLA Modules:
  0.0 69.5 jit_solution(11054589838978917981)
XLA Ops:
  0.7 1.6 %weight_share.1 = bf16[88,256]{1,0:T(8,128)(2,1)} custom-call(s32[1]{0:T(128)} %bitcast.7.group_ref, bf16[160,256]{1,0:T(8,128)(2,1)} %bitcast.34, bf16[128,256]{1,0:T(8,128)(2,1)} %sw_ref.1, f32[4,256]{1,0:T(4,128)} %cw_ref.1, f32[1,256]{1,0:T(1,128)} %bitcast.35, f32[1,256]{1,0:T(1,128)} %bitcast.36, f32[1,256]{1,0:T(1,128)} %bitcast.37, f32[16,256]{1,0:T(8,128)} %ld_ref.1), custom_call_target="tpu_custom_call" | custom-call | tf_op jit(solution)/shard_map/weight_share/pallas_call | solution.py:93
  2.3 4.0 %collective-permute-start = (bf16[1,88,256]{2,1,0:T(8,128)(2,1)}, bf16[1,88,256]{2,1,0:T(8,128)(2,1)S(1)}, u32[]{:S(2)}, u32[]{:S(2)}) collective-permute-start(bf16[1,88,256]{2,1,0:T(8,128)(2,1)} %bitcast.30), channel_id=1, source_target_pairs={{0,16},{4,20},{8,24},{12,28},{16,0},{20,4},{24,8},{28,12},{1,17},{... | collective-permute-start | bytes 135176 | tf_op jit(solution)/shard_map/ppermute | solution.py:129
  6.3 1.2 %copy-done.1 = f32[8,16,2048]{2,1,0:T(8,128)S(1)} copy-done((f32[8,16,2048]{2,1,0:T(8,128)S(1)}, f32[8,16,2048]{2,1,0:T(8,128)}, u32[]{:S(2)}) %copy-start.1) | copy-done | bytes 1048600
  7.6 0.9 %copy-done.6 = bf16[8,3,2048]{2,0,1:T(8,128)(2,1)S(1)} copy-done((bf16[8,3,2048]{2,0,1:T(8,128)(2,1)S(1)}, bf16[8,3,2048]{2,0,1:T(8,128)(2,1)}, u32[]{:S(2)}) %copy-start.6) | copy-done | bytes 98328
  8.5 1.3 %pack_states.1 = bf16[8,8,4864]{2,1,0:T(8,128)(2,1)} custom-call(f32[128,2048]{1,0:T(8,128)S(1)} %bitcast.28, bf16[3,8,2048]{2,1,0:T(8,128)(2,1)S(1)} %bitcast.29), custom_call_target="tpu_custom_call" | custom-call | tf_op jit(solution)/shard_map/pack_states/pallas_call | solution.py:46
  9.7 3.8 %all-to-all-start = ((bf16[8,8,4864]{2,1,0:T(8,128)(2,1)}), bf16[8,8,4864]{2,1,0:T(8,128)(2,1)S(1)}, u32[]{:S(2)}, u32[]{:S(2)}) async-start(bf16[8,8,4864]{2,1,0:T(8,128)(2,1)} %pack_states.1), calls=%async_computation | async-start | bytes 1245184 | tf_op jit(solution)/shard_map/all_to_all | solution.py:382
  13.5 2.1 %collective-permute-start.1 = (bf16[2,88,256]{2,1,0:T(8,128)(2,1)S(1)}, bf16[2,88,256]{2,1,0:T(8,128)(2,1)S(1)}, u32[]{:S(2)}, u32[]{:S(2)}) collective-permute-start(bf16[2,88,256]{2,1,0:T(8,128)(2,1)S(1)} %pad_maximum_fusion.3), channel_id=1, source_target_pairs={{0,8},{4,12},{8,0},{12,4},{16,24},{20,28},{24,16},{28,20},{1,9},{5... | collective-permute-start | bytes 270344 | tf_op jit(solution)/shard_map/ppermute | solution.py:129
  15.6 9.8 %collective-permute-done.1 = bf16[2,88,256]{2,1,0:T(8,128)(2,1)S(1)} collective-permute-done((bf16[2,88,256]{2,1,0:T(8,128)(2,1)S(1)}, bf16[2,88,256]{2,1,0:T(8,128)(2,1)S(1)}, u32[]{:S(2)}, u32[]{:S(2)}) %collective-permute-start.1) | collective-permute-done | bytes 90144 | tf_op jit(solution)/shard_map/ppermute | solution.py:129
  25.4 1.8 %collective-permute-start.2 = (bf16[4,88,256]{2,1,0:T(8,128)(2,1)S(1)}, bf16[4,88,256]{2,1,0:T(8,128)(2,1)S(1)}, u32[]{:S(2)}, u32[]{:S(2)}) collective-permute-start(bf16[4,88,256]{2,1,0:T(8,128)(2,1)S(1)} %pad_maximum_fusion.2), channel_id=1, source_target_pairs={{0,4},{4,0},{8,12},{12,8},{16,20},{20,16},{24,28},{28,24},{1,5},{5... | collective-permute-start | bytes 540680 | tf_op jit(solution)/shard_map/ppermute | solution.py:129
  27.3 4.1 %collective-permute-done.2 = bf16[4,88,256]{2,1,0:T(8,128)(2,1)S(1)} collective-permute-done((bf16[4,88,256]{2,1,0:T(8,128)(2,1)S(1)}, bf16[4,88,256]{2,1,0:T(8,128)(2,1)S(1)}, u32[]{:S(2)}, u32[]{:S(2)}) %collective-permute-start.2) | collective-permute-done | bytes 180256 | tf_op jit(solution)/shard_map/ppermute | solution.py:129
  31.4 1.6 %collective-permute-start.3 = (bf16[1,8,88,256]{3,2,1,0:T(8,128)(2,1)S(1)}, bf16[1,8,88,256]{3,2,1,0:T(8,128)(2,1)S(1)}, u32[]{:S(2)}, u32[]{:S(2)}) collective-permute-start(bf16[1,8,88,256]{3,2,1,0:T(8,128)(2,1)S(1)} %maximum_bitcast_fusion), channel_id=1, source_target_pairs={{0,2},{1,3},{2,0},{3,1},{4,6},{5,7},{6,4},{7,5},{8,10},{9,11},{10,... | collective-permute-start | bytes 1081352 | tf_op jit(solution)/shard_map/ppermute | solution.py:129
  33.3 1.2 %select_slots.1 = bf16[64,4864]{1,0:T(8,128)(2,1)} custom-call(bf16[4,64,64]{2,1,0:T(8,128)(2,1)S(1)} %add_convert_fusion.mask_ref, bf16[64,4864]{1,0:T(8,128)(2,1)S(1)} %bitcast.27), custom_call_target="tpu_custom_call" | custom-call | tf_op jit(solution)/shard_map/select_slots/pallas_call | solution.py:398
  34.5 6.3 %all-to-all-start.1 = ((bf16[8,8,4864]{2,1,0:T(8,128)(2,1)}), bf16[8,8,4864]{2,1,0:T(8,128)(2,1)S(1)}, u32[]{:S(2)}, u32[]{:S(2)}) async-start(bf16[8,8,4864]{2,1,0:T(8,128)(2,1)} %bitcast.3), calls=%async_computation.1 | async-start | bytes 1245184 | tf_op jit(solution)/shard_map/all_to_all | solution.py:382
  41.7 4.8 %convolution_convert_fusion.inner_ref.gate_ref = bf16[128,4096]{1,0:T(8,128)(2,1)S(1)} fusion(bf16[1024,4096]{1,0:T(8,128)(2,1)} %param.19, f32[1024]{0:T(1024)S(1)} %copy-done.13, f32[128]{0:T(128)S(1)} %rsqrt.12, bf16[8,16,1024]{2,1,0:T(8,128)(2,1)S(1)} %copy-done.9), kind=kOutput, calls=%fused_computation | convolution fusion | flops 1074790400 | bytes 9703936 | tf_op jit(solution)/shard_map/dot_general | solution.py:471
  46.7 1.7 %early_tokens.1 = (bf16[104,2048]{1,0:T(8,128)(2,1)S(1)}, f32[104,2048]{1,0:T(8,128)S(1)}, f32[104,32]{1,0:T(8,128)S(1)}, f32[24,2048]{1,0:T(8,128)S(1)}) custom-call(s32[4]{0:T(128)S(1)} %fusion.9.q_ref, s32[8]{0:T(128)S(1)} %fusion.11.j_ref, bf16[128,4096]{1,0:T(8,128)(2,1)S(1)} %convolution_convert_fusion.inner_ref.gate_ref, ...), custom_call_target="tpu_custom_call" | custom-call | flops 140000000 | bytes 4194304 | tf_op jit(solution)/shard_map/early_tokens/pallas_call | solution.py:212
  48.4 0.9 %copy-done.2 = f32[104,2048]{1,0:T(8,128)} copy-done((f32[104,2048]{1,0:T(8,128)}, f32[104,2048]{1,0:T(8,128)S(1)}, u32[]{:S(2)}) %copy-start.2) | copy-done | bytes 851992
  49.3 0.7 copy-done.4
  50.0 0.6 copy-done.7
  50.6 3.7 %all-to-all-done.1.moved_ref = bf16[8,8,4864]{2,1,0:T(8,128)(2,1)S(1)} async-done(((bf16[8,8,4864]{2,1,0:T(8,128)(2,1)}), bf16[8,8,4864]{2,1,0:T(8,128)(2,1)S(1)}, u32[]{:S(2)}, u32[]{:S(2)}) %all-to-all-start.1) | async-done | bytes 622624 | tf_op jit(solution)/shard_map/all_to_all | solution.py:382
  54.4 2.2 %copy-done = bf16[2048,1024]{1,0:T(8,128)(2,1)S(1)} copy-done((bf16[2048,1024]{1,0:T(8,128)(2,1)S(1)}, bf16[2048,1024]{1,0:T(8,128)(2,1)}, u32[]{:S(2)}) %copy-start) | copy-done | bytes 4194328
  56.6 1.2 %copy-done.3 = f32[104,2048]{1,0:T(8,128)S(1)} copy-done((f32[104,2048]{1,0:T(8,128)S(1)}, f32[104,2048]{1,0:T(8,128)}, u32[]{:S(2)}) %copy-start.3) | copy-done | bytes 851992
  57.7 0.9 %copy-done.5 = f32[24,2048]{1,0:T(8,128)S(1)} copy-done((f32[24,2048]{1,0:T(8,128)S(1)}, f32[24,2048]{1,0:T(8,128)}, u32[]{:S(2)}) %copy-start.5) | copy-done | bytes 196632
  58.6 0.8 %copy-done.8 = f32[104,32]{1,0:T(8,128)S(1)} copy-done((f32[104,32]{1,0:T(8,128)S(1)}, f32[104,32]{1,0:T(8,128)}, u32[]{:S(2)}) %copy-start.8) | copy-done | bytes 13336
  59.5 10.0 %scan_layer.1 = (bf16[8,16,1024]{2,1,0:T(8,128)(2,1)}, f32[128,2048]{1,0:T(8,128)}) custom-call(s32[4]{0:T(128)S(1)} %fusion.9.q_ref, s32[8]{0:T(128)S(1)} %fusion.11.j_ref, bf16[8,8,4864]{2,1,0:T(8,128)(2,1)S(1)} %all-to-all-done.1.moved_ref, bf16[128,4096]{1,0:T(8,128)(2,1)S(1)} %convolution_convert_fusion.inner_ref.gate_ref, ...), custom_call_target="tpu_custom_call" | custom-call | flops 536870912 | bytes 8388608 | tf_op jit(solution)/shard_map/scan_layer/pallas_call | solution.py:339
  (47 shorter events, 1.6 us)
Async XLA Ops:
  0.6 15.0 %copy-start.15 = (s32[64]{0:T(128)S(1)}, s32[64]{0:T(128)}, u32[]{:S(2)}) copy-start(s32[64]{0:T(128)} %param.33) | copy-start | bytes 772
  0.6 15.0 %copy-start.16 = (s32[64]{0:T(128)S(1)}, s32[64]{0:T(128)}, u32[]{:S(2)}) copy-start(s32[64]{0:T(128)} %param.31) | copy-start | bytes 772
  0.7 26.5 %copy-start.14 = (s32[64]{0:T(128)S(1)}, s32[64]{0:T(128)}, u32[]{:S(2)}) copy-start(s32[64]{0:T(128)} %param.30) | copy-start | bytes 772
  2.3 11.2 %collective-permute-start = (bf16[1,88,256]{2,1,0:T(8,128)(2,1)}, bf16[1,88,256]{2,1,0:T(8,128)(2,1)S(1)}, u32[]{:S(2)}, u32[]{:S(2)}) collective-permute-start(bf16[1,88,256]{2,1,0:T(8,128)(2,1)} %bitcast.30), channel_id=1, source_target_pairs={{0,16},{4,20},{8,24},{12,28},{16,0},{20,4},{24,8},{28,12},{1,17},{... | collective-permute-start | bytes 135176 | tf_op jit(solution)/shard_map/ppermute | solution.py:129
  6.3 1.2 %copy-start.1 = (f32[8,16,2048]{2,1,0:T(8,128)S(1)}, f32[8,16,2048]{2,1,0:T(8,128)}, u32[]{:S(2)}) copy-start(f32[8,16,2048]{2,1,0:T(8,128)} %param.28) | copy-start | bytes 3145732
  7.6 0.9 %copy-start.6 = (bf16[8,3,2048]{2,0,1:T(8,128)(2,1)S(1)}, bf16[8,3,2048]{2,0,1:T(8,128)(2,1)}, u32[]{:S(2)}) copy-start(bf16[8,3,2048]{2,0,1:T(8,128)(2,1)} %param.29) | copy-start | bytes 294916
  8.4 5.1 %copy-start.12 = (bf16[88,256]{1,0:T(8,128)(2,1)S(1)}, bf16[88,256]{1,0:T(8,128)(2,1)}, u32[]{:S(2)}) copy-start(bf16[88,256]{1,0:T(8,128)(2,1)} %weight_share.1) | copy-start | bytes 135172
  8.4 24.6 %copy-start.9 = (bf16[8,16,1024]{2,1,0:T(8,128)(2,1)S(1)}, bf16[8,16,1024]{2,1,0:T(8,128)(2,1)}, u32[]{:S(2)}) copy-start(bf16[8,16,1024]{2,1,0:T(8,128)(2,1)} %param.17) | copy-start | bytes 786436
  9.7 23.6 %all-to-all-start = ((bf16[8,8,4864]{2,1,0:T(8,128)(2,1)}), bf16[8,8,4864]{2,1,0:T(8,128)(2,1)S(1)}, u32[]{:S(2)}, u32[]{:S(2)}) async-start(bf16[8,8,4864]{2,1,0:T(8,128)(2,1)} %pack_states.1), calls=%async_computation | async-start | bytes 1245184 | tf_op jit(solution)/shard_map/all_to_all | solution.py:382
  13.5 27.4 %copy-start.17 = (s32[64]{0:T(128)S(1)}, s32[64]{0:T(128)}, u32[]{:S(2)}) copy-start(s32[64]{0:T(128)} %param.32) | copy-start | bytes 772
  13.5 11.8 %collective-permute-start.1 = (bf16[2,88,256]{2,1,0:T(8,128)(2,1)S(1)}, bf16[2,88,256]{2,1,0:T(8,128)(2,1)S(1)}, u32[]{:S(2)}, u32[]{:S(2)}) collective-permute-start(bf16[2,88,256]{2,1,0:T(8,128)(2,1)S(1)} %pad_maximum_fusion.3), channel_id=1, source_target_pairs={{0,8},{4,12},{8,0},{12,4},{16,24},{20,28},{24,16},{28,20},{1,9},{5... | collective-permute-start | bytes 270344 | tf_op jit(solution)/shard_map/ppermute | solution.py:129
  25.4 6.0 %collective-permute-start.2 = (bf16[4,88,256]{2,1,0:T(8,128)(2,1)S(1)}, bf16[4,88,256]{2,1,0:T(8,128)(2,1)S(1)}, u32[]{:S(2)}, u32[]{:S(2)}) collective-permute-start(bf16[4,88,256]{2,1,0:T(8,128)(2,1)S(1)} %pad_maximum_fusion.2), channel_id=1, source_target_pairs={{0,4},{4,0},{8,12},{12,8},{16,20},{20,16},{24,28},{28,24},{1,5},{5... | collective-permute-start | bytes 540680 | tf_op jit(solution)/shard_map/ppermute | solution.py:129
  31.4 9.5 %collective-permute-start.3 = (bf16[1,8,88,256]{3,2,1,0:T(8,128)(2,1)S(1)}, bf16[1,8,88,256]{3,2,1,0:T(8,128)(2,1)S(1)}, u32[]{:S(2)}, u32[]{:S(2)}) collective-permute-start(bf16[1,8,88,256]{3,2,1,0:T(8,128)(2,1)S(1)} %maximum_bitcast_fusion), channel_id=1, source_target_pairs={{0,2},{1,3},{2,0},{3,1},{4,6},{5,7},{6,4},{7,5},{8,10},{9,11},{10,... | collective-permute-start | bytes 1081352 | tf_op jit(solution)/shard_map/ppermute | solution.py:129
  33.1 8.6 %copy-start.13 = (f32[1024]{0:T(1024)S(1)}, f32[1024]{0:T(1024)}, u32[]{:S(2)}) copy-start(f32[1024]{0:T(1024)} %param.18) | copy-start | bytes 12292
  34.5 19.9 %all-to-all-start.1 = ((bf16[8,8,4864]{2,1,0:T(8,128)(2,1)}), bf16[8,8,4864]{2,1,0:T(8,128)(2,1)S(1)}, u32[]{:S(2)}, u32[]{:S(2)}) async-start(bf16[8,8,4864]{2,1,0:T(8,128)(2,1)} %bitcast.3), calls=%async_computation.1 | async-start | bytes 1245184 | tf_op jit(solution)/shard_map/all_to_all | solution.py:382
  40.9 0.7 %copy-start.10 = (bf16[1,8,88,256]{3,2,1,0:T(8,128)(2,1)}, bf16[1,8,88,256]{3,2,1,0:T(8,128)(2,1)S(1)}, u32[]{:S(2)}) copy-start(bf16[1,8,88,256]{3,2,1,0:T(8,128)(2,1)S(1)} %collective-permute-done.3) | copy-start | bytes 1081348
  41.0 5.5 %collective-permute-start.4 = (bf16[2,8,88,256]{3,2,1,0:T(8,128)(2,1)S(1)}, bf16[2,8,88,256]{3,2,1,0:T(8,128)(2,1)S(1)}, u32[]{:S(2)}, u32[]{:S(2)}) collective-permute-start(bf16[2,8,88,256]{3,2,1,0:T(8,128)(2,1)S(1)} %pad_maximum_fusion.1), channel_id=1, source_target_pairs={{0,1},{1,0},{2,3},{3,2},{4,5},{5,4},{6,7},{7,6},{8,9},{9,8},{10,11... | collective-permute-start | bytes 2162696 | tf_op jit(solution)/shard_map/ppermute | solution.py:129
  41.7 4.9 %copy-start.11 = (bf16[1,8,88,256]{3,2,1,0:T(8,128)(2,1)S(1)}, bf16[1,8,88,256]{3,2,1,0:T(8,128)(2,1)}, u32[]{:S(2)}) copy-start(bf16[1,8,88,256]{3,2,1,0:T(8,128)(2,1)} %copy-done.10) | copy-start | bytes 1081348
  48.4 0.9 %copy-start.2 = (f32[104,2048]{1,0:T(8,128)}, f32[104,2048]{1,0:T(8,128)S(1)}, u32[]{:S(2)}) copy-start(f32[104,2048]{1,0:T(8,128)S(1)} %get-tuple-element.8.dt_ref) | copy-start | bytes 2555908
  49.3 0.7 copy-start.4
  54.4 2.2 %copy-start = (bf16[2048,1024]{1,0:T(8,128)(2,1)S(1)}, bf16[2048,1024]{1,0:T(8,128)(2,1)}, u32[]{:S(2)}) copy-start(bf16[2048,1024]{1,0:T(8,128)(2,1)} %ow_ref.1) | copy-start | bytes 12582916
  56.6 1.2 %copy-start.3 = (f32[104,2048]{1,0:T(8,128)S(1)}, f32[104,2048]{1,0:T(8,128)}, u32[]{:S(2)}) copy-start(f32[104,2048]{1,0:T(8,128)} %copy-done.2) | copy-start | bytes 2555908
  57.7 0.9 %copy-start.5 = (f32[24,2048]{1,0:T(8,128)S(1)}, f32[24,2048]{1,0:T(8,128)}, u32[]{:S(2)}) copy-start(f32[24,2048]{1,0:T(8,128)} %copy-done.4) | copy-start | bytes 589828
  58.6 0.8 %copy-start.8 = (f32[104,32]{1,0:T(8,128)S(1)}, f32[104,32]{1,0:T(8,128)}, u32[]{:S(2)}) copy-start(f32[104,32]{1,0:T(8,128)} %copy-done.7) | copy-start | bytes 39940
  (1 other events, 0.6 us)

commit v3 on v2

v3 whole, which is shorter than its diff:
```python
import functools

import jax
import jax.numpy as jnp
from jax import lax
from jax.experimental import pallas as pl
from jax.experimental.pallas import tpu as pltpu
from jax.sharding import PartitionSpec as P

EPS = 1e-05
LOG2E = 1.4426950408889634
LANES = 128
BLOCK = 256
SHARE = 88


def rms_normed(values_in, norm_gain):
    values = values_in.astype(jnp.float32)
    factor = lax.rsqrt(jnp.mean(values * values, axis=-1, keepdims=True) + EPS)
    return (values * factor * norm_gain).astype(jnp.bfloat16)


def in_hbm(values):
    return pltpu.with_memory_space_constraint(values, pltpu.HBM)


def pack_kernel(state_ref, edge_ref, out_ref, tile_ref, held_ref, send_ref, sems):
    blocks, slots, _ = out_ref.shape
    width = state_ref.shape[1] // blocks
    states = state_ref.shape[0] // slots
    per = width // LANES

    def load(tile):
        cols = pl.ds(tile * LANES, LANES)
        return pltpu.make_async_copy(state_ref.at[:, cols], tile_ref.at[tile], sems.at[0, tile])

    def store(dest):
        return pltpu.make_async_copy(send_ref.at[dest], out_ref.at[dest], sems.at[1, dest])

    edges = pltpu.make_async_copy(edge_ref, held_ref, sems.at[1, blocks])
    edges.start()
    for tile in range(blocks * per):
        load(tile).start()
    edges.wait()
    for dest in range(blocks):
        for e in range(edge_ref.shape[0]):
            at = (states + e) * width
            send_ref[dest, :, pl.ds(at, width)] = held_ref[e, :, pl.ds(dest * width, width)]
        for part in range(per):
            tile = dest * per + part
            load(tile).wait()
            for n in range(states):
                rows = tile_ref[tile, pl.ds(n, slots, stride=states), :]
                send_ref[dest, :, pl.ds(n * width + part * LANES, LANES)] = rows.astype(jnp.bfloat16)
        store(dest).start()
    for dest in range(blocks):
        store(dest).wait()


def pack(old_states, old_edges, blocks):
    slots, states, inner = old_states.shape
    span = old_edges.shape[1]
    width = inner // blocks
    edges = jnp.swapaxes(old_edges, 0, 1)
    if width % LANES == 0 and slots == 8:
        tiles = inner // LANES
        return pl.pallas_call(
            pack_kernel,
            out_shape=pltpu.HBM((blocks, slots, (states + span) * width), jnp.bfloat16),
            in_specs=[pl.BlockSpec(memory_space=pltpu.HBM)] * 2,
            out_specs=pl.BlockSpec(memory_space=pltpu.HBM),
            scratch_shapes=[
                pltpu.VMEM((tiles, slots * states, LANES), jnp.float32),
                pltpu.VMEM((span, slots, inner), jnp.bfloat16),
                pltpu.VMEM((blocks, slots, (states + span) * width), jnp.bfloat16),
                pltpu.SemaphoreType.DMA((2, max(tiles, blocks + 1))),
            ],
            compiler_params=pltpu.CompilerParams(vmem_limit_bytes=16 << 20),
            name="pack_states",
        )(in_hbm(old_states.reshape(slots * states, inner)), in_hbm(edges))
    lead = jnp.swapaxes(old_states.astype(jnp.bfloat16), 0, 1)
    both = jnp.concatenate([lead, edges], axis=0)
    both = both.reshape(states + span, slots, blocks, width)
    return both.transpose(2, 1, 0, 3).reshape(blocks, slots, (states + span) * width)


def share_kernel(group_ref, xt_ref, sw_ref, cw_ref, cb_ref, sb_ref, sk_ref, ld_ref, out_ref, vec_ref):
    rank = sw_ref.shape[0]
    groups = rank // 32
    vec_ref[...] = jnp.zeros_like(vec_ref)
    vec_ref[pl.ds(0, 4), :] = cw_ref[...]
    vec_ref[pl.ds(4, 1), :] = cb_ref[...]
    vec_ref[pl.ds(5, 1), :] = sb_ref[...]
    vec_ref[pl.ds(6, 1), :] = sk_ref[...]
    vec_ref[pl.ds(8, 16), :] = ld_ref[...]
    for k in range(groups):

        @pl.when(group_ref[0] == k)
        def _():
            vec = vec_ref[pl.ds(16 * (k % 2), 16), :]
            high = vec.astype(jnp.bfloat16).astype(jnp.float32)
            part = high if k < 2 else vec - high
            rows = [
                xt_ref[pl.ds(32 * k, 32), :].astype(jnp.float32),
                xt_ref[pl.ds(rank + 8 * k, 8), :].astype(jnp.float32),
                part[:8],
                sw_ref[pl.ds(32 * k, 32), :].astype(jnp.float32),
                part[8:],
            ]
            out_ref[...] = jnp.concatenate(rows, axis=0).astype(jnp.bfloat16)


def weight_share(groups, x_weight, step_weight, conv_weight, conv_bias, step_bias, skip_gain, log_decay):
    channels = x_weight.shape[0]
    rank = step_weight.shape[0]
    xt = x_weight.T
    group = lax.axis_index("grp").astype(jnp.int32)
    if channels % LANES == 0:
        return pl.pallas_call(
            share_kernel,
            out_shape=jax.ShapeDtypeStruct((SHARE, channels), jnp.bfloat16),
            in_specs=[pl.BlockSpec(memory_space=pltpu.SMEM)] + [pl.BlockSpec(memory_space=pltpu.VMEM)] * 7,
            out_specs=pl.BlockSpec(memory_space=pltpu.VMEM),
            scratch_shapes=[pltpu.VMEM((32, channels), jnp.float32)],
            name="weight_share",
        )(
            group[None], xt, step_weight, conv_weight, conv_bias[None], step_bias[None],
            skip_gain[None], log_decay,
        )
    vec = jnp.concatenate(
        [conv_weight, conv_bias[None], step_bias[None], skip_gain[None], jnp.zeros_like(conv_bias)[None], log_decay],
        axis=0,
    )
    vec = jnp.pad(vec, ((0, 8), (0, 0)))
    high = vec.astype(jnp.bfloat16)
    both = jnp.concatenate([high, (vec - high.astype(jnp.float32)).astype(jnp.bfloat16)], axis=0)
    both = both.reshape(4, 16, channels)
    stacked = jnp.concatenate(
        [
            xt[:rank].reshape(4, 32, channels),
            xt[rank:].reshape(4, 8, channels),
            both[:, :8],
            step_weight.reshape(4, 32, channels),
            both[:, 8:],
        ],
        axis=1,
    )
    return lax.dynamic_index_in_dim(stacked, group, 0, keepdims=False)


def doubled(values, axis):
    size = lax.axis_size(axis)
    bit = size // 2
    while bit:
        other = lax.ppermute(values, axis, [(i, i ^ bit) for i in range(size)])
        values = jnp.concatenate([values, other], axis=0)
        bit //= 2
    return values


def places(axis):
    size = lax.axis_size(axis)
    offset = jnp.arange(size, dtype=jnp.int32) ^ lax.axis_index(axis).astype(jnp.int32)
    place = jnp.zeros_like(offset)
    bit, top = 1, size // 2
    while top:
        place = place | jnp.where((offset & bit) != 0, top, 0)
        bit, top = bit * 2, top // 2
    return place


def block_weights(w_ref, q_ref, j_ref, j):
    at = j_ref[j]
    quarters = [w_ref.at[q_ref[q], at] for q in range(4)]
    f32 = jnp.float32
    xw = jnp.concatenate(
        [w[pl.ds(0, 32), :].astype(f32) for w in quarters] + [w[pl.ds(32, 8), :].astype(f32) for w in quarters],
        axis=0,
    ).astype(jnp.bfloat16)
    sw = jnp.concatenate([w[pl.ds(48, 32), :] for w in quarters], axis=0)
    first = [w[pl.ds(40, 8), :].astype(f32) for w in quarters]
    second = [w[pl.ds(80, 8), :].astype(f32) for w in quarters]
    high = jnp.concatenate([first[0], second[0], first[1]], axis=0)
    low = jnp.concatenate([first[2], second[2], first[3]], axis=0)
    return xw, sw, high + low


def silu(values):
    return values / (1.0 + jnp.exp(-values))


def convolved(sequence, vec, count):
    reqs = (sequence.shape[0] - count) // 3
    running = vec[4:5]
    for k in range(4):
        running = running + vec[k : k + 1] * sequence[k * reqs : k * reqs + count]
    return silu(running).astype(jnp.bfloat16)


def softplus(values):
    return jnp.maximum(values, 0.0) + jnp.log1p(jnp.exp(-jnp.abs(values)))


def mixed_of(conv, xw):
    return lax.dot_general(conv, xw, (((1,), (1,)), ((), ())), preferred_element_type=jnp.float32)


def spread(rows, t, b_ref, c_ref):
    reqs, both = rows.shape
    states = both // 2
    for n in range(states):
        b_ref[t * states + n] = jnp.broadcast_to(rows[:, n : n + 1], (reqs, LANES))
        c_ref[t * states + n] = jnp.broadcast_to(rows[:, states + n : states + n + 1], (reqs, LANES))


def before_kernel(q_ref, j_ref, proj_ref, w_ref, acc_ref, *refs):
    results, kept, (dt_ref, cv_ref, b_ref, dec_ref, sems) = refs[:10], refs[10:20], refs[20:]
    y_ref, sg_ref, sum_ref, at_ref, ga_ref, c_ref, xw_ref, sw_ref, vec_ref, x_ref = kept
    blocks = w_ref.shape[1]
    tiles, count, _ = y_ref.shape
    tokens = sg_ref.shape[1]
    late = tokens - count
    reqs = late // 3
    states = b_ref.shape[0] * reqs // count
    inner = blocks * BLOCK
    rank = sw_ref.shape[1]
    per = BLOCK // LANES
    copies = [pltpu.make_async_copy(kept[i], results[i], sems.at[i]) for i in range(len(kept))]
    mixed = jnp.zeros((count, rank + 2 * states), jnp.float32)
    for j in range(blocks):
        xw, sw, vec = block_weights(w_ref, q_ref, j_ref, j)
        values = proj_ref[:, pl.ds(j * BLOCK, BLOCK)].astype(jnp.float32)
        conv = convolved(values, vec, count)
        mixed = mixed + mixed_of(conv, xw)
        xw_ref[j] = xw
        sw_ref[j] = sw
        x_ref[j] = values[:late]
        vec_ref[j, pl.ds(0, 8), :] = vec[:8]
        decay2 = jnp.exp(vec[8:]) * (-LOG2E)
        vec_ref[j, pl.ds(8, states), :] = decay2
        full = conv.astype(jnp.float32)
        gate = silu(proj_ref[:, pl.ds(inner + j * BLOCK, BLOCK)].astype(jnp.float32))
        for k in range(per):
            tile = j * per + k
            lanes = slice(k * LANES, (k + 1) * LANES)
            cv_ref[tile] = full[:, lanes]
            sg_ref[tile] = gate[:, lanes]
            y_ref[tile] = vec[6:7, lanes] * full[:, lanes]
            for n in range(states):
                dec_ref[tile, n] = jnp.broadcast_to(decay2[n : n + 1, lanes], (reqs, LANES))
    for i in (1, 6, 7, 8, 9):
        copies[i].start()
    rounded = mixed.astype(jnp.bfloat16)
    for j in range(blocks):
        dt = softplus(
            jnp.dot(rounded[:, :rank], sw_ref[j], preferred_element_type=jnp.float32)
            + vec_ref[j, pl.ds(5, 1), :]
        )
        for k in range(per):
            dt_ref[j * per + k] = dt[:, k * LANES : (k + 1) * LANES]
    coefs = rounded[:, rank:].astype(jnp.float32)
    for t in range(count // reqs):
        spread(coefs[t * reqs : (t + 1) * reqs], t, b_ref, c_ref)
    copies[5].start()
    accepted = acc_ref[...]
    ga_ref[...] = jnp.zeros_like(ga_ref)
    at_ref[...] = jnp.zeros_like(at_ref)

    @pl.loop(0, tiles)
    def _(tile):
        state = [None] * states
        passed = None
        for t in range(count // reqs):
            rows = pl.ds(t * reqs, reqs)
            delta = dt_ref[tile, rows, :]
            passed = delta if t == 0 else passed + delta
            sum_ref[tile, rows, :] = passed
            driven = delta * cv_ref[tile, rows, :]
            chosen = accepted == t + 4
            pltpu.store(at_ref.at[tile], passed, mask=chosen)
            totals = [None, None]
            for n in range(states):
                at = t * states + n
                added = driven * b_ref[at]
                state[n] = added if t == 0 else jnp.exp2(delta * dec_ref[tile, n]) * state[n] + added
                term = c_ref[at] * state[n]
                totals[n % 2] = term if totals[n % 2] is None else totals[n % 2] + term
                pltpu.store(ga_ref.at[tile, pl.ds(n * reqs, reqs), :], state[n], mask=chosen)
            y_ref[tile, rows, :] = y_ref[tile, rows, :] + (totals[0] + totals[1])

    for i in (0, 2, 3, 4):
        copies[i].start()
    for copy in copies:
        copy.wait()


def before(q_place, j_place, projected, weights, accepted, late, states):
    tokens = projected.shape[0]
    blocks = weights.shape[1]
    tiles = blocks * (BLOCK // LANES)
    count = tokens - late
    reqs = accepted.shape[0]
    rank = 4 * 32
    smem = pl.BlockSpec(memory_space=pltpu.SMEM)
    vmem = pl.BlockSpec(memory_space=pltpu.VMEM)
    f32 = jnp.float32
    spots = count // reqs * states
    results = [
        ((tiles, count, LANES), f32),
        ((tiles, tokens, LANES), f32),
        ((tiles, count, LANES), f32),
        ((tiles, reqs, LANES), f32),
        ((tiles, states * reqs, LANES), f32),
        ((spots, reqs, LANES), f32),
        ((blocks, rank + 2 * states, BLOCK), jnp.bfloat16),
        ((blocks, rank, BLOCK), jnp.bfloat16),
        ((blocks, 24, BLOCK), f32),
        ((blocks, late, BLOCK), f32),
    ]
    return pl.pallas_call(
        before_kernel,
        out_shape=tuple(pltpu.HBM(shape, dtype) for shape, dtype in results),
        in_specs=[smem, smem, vmem, vmem, vmem],
        out_specs=(pl.BlockSpec(memory_space=pltpu.HBM),) * len(results),
        scratch_shapes=[pltpu.VMEM(shape, dtype) for shape, dtype in results]
        + [
            pltpu.VMEM((tiles, count, LANES), f32),
            pltpu.VMEM((tiles, count, LANES), f32),
            pltpu.VMEM((spots, reqs, LANES), f32),
            pltpu.VMEM((tiles, states, reqs, LANES), f32),
            pltpu.SemaphoreType.DMA((len(results),)),
        ],
        compiler_params=pltpu.CompilerParams(vmem_limit_bytes=24 << 20),
        cost_estimate=pl.CostEstimate(flops=200_000_000, bytes_accessed=8 << 20, transcendentals=4_000_000),
        name="before_states",
    )(q_place, j_place, projected, weights, accepted)


def after_kernel(moved_ref, acc_ref, *refs):
    given, (out_ref, ns_ref) = refs[:11], refs[11:13]
    held, refs = refs[13:24], refs[24:]
    new_ref, pick_ref, total_ref, dt_ref, cv_ref, b_ref, cl_ref, sems, ns_sem = refs
    y_ref, sg_ref, sum_ref, at_ref, ga_ref, c_ref, xw_ref, sw_ref, vec_ref, x_ref, ow_ref = held
    reqs, draft, _ = out_ref.shape
    blocks, late, _ = x_ref.shape
    tiles, count, _ = y_ref.shape
    states = ga_ref.shape[1] // reqs
    rank = sw_ref.shape[1]
    per = BLOCK // LANES

    def state_copy(j):
        return pltpu.make_async_copy(new_ref.at[j], ns_ref.at[:, pl.ds(j * BLOCK, BLOCK)], ns_sem.at[j])

    copies = [pltpu.make_async_copy(given[i], held[i], sems.at[i]) for i in range(len(held))]
    for i in (9, 8, 6, 7, 5, 2, 0, 1, 3, 4, 10):
        copies[i].start()
    for i in (9, 8, 6):
        copies[i].wait()
    mixed = jnp.zeros((late, rank + 2 * states), jnp.float32)
    for j in range(blocks):
        history = [
            moved_ref[j, :, pl.ds((states + e) * BLOCK, BLOCK)].astype(jnp.float32) for e in range(3)
        ]
        conv = convolved(jnp.concatenate(history + [x_ref[j]], axis=0), vec_ref[j], late)
        cv_ref[j] = conv.astype(jnp.float32)
        mixed = mixed + mixed_of(conv, xw_ref[j])
    rounded = mixed.astype(jnp.bfloat16)
    copies[7].wait()
    for j in range(blocks):
        dt_ref[j] = softplus(
            jnp.dot(rounded[:, :rank], sw_ref[j], preferred_element_type=jnp.float32)
            + vec_ref[j, pl.ds(5, 1), :]
        )
    coefs = rounded[:, rank:].astype(jnp.float32)
    for t in range(late // reqs):
        spread(coefs[t * reqs : (t + 1) * reqs], t, b_ref, cl_ref)
    accepted = acc_ref[...]
    for i in (5, 2, 0, 1, 3, 4, 10):
        copies[i].wait()
    for j in range(blocks):
        gated = []
        for k in range(per):
            tile = j * per + k
            lanes = pl.ds(k * LANES, LANES)
            skip = vec_ref[j, pl.ds(6, 1), lanes]
            state = [
                moved_ref[j, :, pl.ds(n * BLOCK + k * LANES, LANES)].astype(jnp.float32)
                for n in range(states)
            ]
            decay = [
                jnp.broadcast_to(vec_ref[j, pl.ds(8 + n, 1), lanes], (reqs, LANES))
                for n in range(states)
            ]
            outs = []
            for t in range(late // reqs):
                rows = pl.ds(t * reqs, reqs)
                delta = dt_ref[j, rows, lanes]
                value = cv_ref[j, rows, lanes]
                driven = delta * value
                chosen = accepted == t + 1
                totals = [skip * value, None]
                for n in range(states):
                    at = t * states + n
                    state[n] = jnp.exp2(delta * decay[n]) * state[n] + driven * b_ref[at]
                    term = cl_ref[at] * state[n]
                    totals[n % 2] = term if totals[n % 2] is None else totals[n % 2] + term
                    pltpu.store(pick_ref.at[tile, pl.ds(n * reqs, reqs), :], state[n], mask=chosen)
                outs.append(totals[0] + totals[1])
            beyond = accepted > late // reqs
            passed = at_ref[tile]
            for n in range(states):
                keep = pl.ds(n * reqs, reqs)
                value = jnp.exp2(passed * decay[n]) * state[n] + ga_ref[tile, keep, :]
                pltpu.store(pick_ref.at[tile, keep, :], value, mask=beyond)
            for t in range(count // reqs):
                rows = pl.ds(t * reqs, reqs)
                passed = sum_ref[tile, rows, :]
                totals = [y_ref[tile, rows, :], None]
                for n in range(states):
                    term = c_ref[t * states + n] * (jnp.exp2(passed * decay[n]) * state[n])
                    totals[n % 2] = term if totals[n % 2] is None else totals[n % 2] + term
                outs.append(totals[0] + totals[1])
            for r in range(reqs):
                new_ref[j, pl.ds(r * states, states), lanes] = pick_ref[
                    tile, pl.ds(r, states, stride=reqs), :
                ]
            gated.append(jnp.concatenate(outs, axis=0) * sg_ref[tile])
        state_copy(j).start()
        added = jnp.dot(
            jnp.concatenate(gated, axis=1).astype(jnp.bfloat16),
            ow_ref[pl.ds(j * BLOCK, BLOCK), :],
            preferred_element_type=jnp.float32,
        )
        for k in range(total_ref.shape[0]):
            part = added[:, k * LANES : (k + 1) * LANES]
            total_ref[k] = part if j == 0 else total_ref[k] + part
    for k in range(total_ref.shape[0]):
        for r in range(reqs):
            rows = total_ref[k, pl.ds(r, draft, stride=reqs), :]
            out_ref[r, :, pl.ds(k * LANES, LANES)] = rows.astype(jnp.bfloat16)
    for j in range(blocks):
        state_copy(j).wait()


def after(moved, accepted, early, out_weight):
    blocks, reqs, _ = moved.shape
    tiles, tokens, _ = early[1].shape
    states = early[4].shape[1] // reqs
    late = early[9].shape[1]
    draft = tokens // reqs
    inner, width = out_weight.shape
    vmem = pl.BlockSpec(memory_space=pltpu.VMEM)
    hbm = pl.BlockSpec(memory_space=pltpu.HBM)
    f32 = jnp.float32
    spots = late // reqs * states
    given = tuple(in_hbm(x) for x in (*early, out_weight))
    return pl.pallas_call(
        after_kernel,
        out_shape=(
            jax.ShapeDtypeStruct((reqs, draft, width), jnp.bfloat16),
            jax.ShapeDtypeStruct((reqs * states, inner), f32),
        ),
        in_specs=[vmem] * 2 + [hbm] * len(given),
        out_specs=(vmem, hbm),
        scratch_shapes=[pltpu.VMEM(x.shape, x.dtype) for x in given]
        + [
            pltpu.VMEM((blocks, reqs * states, BLOCK), f32),
            pltpu.VMEM((tiles, states * reqs, LANES), f32),
            pltpu.VMEM((width // LANES, tokens, LANES), f32),
            pltpu.VMEM((blocks, late, BLOCK), f32),
            pltpu.VMEM((blocks, late, BLOCK), f32),
            pltpu.VMEM((spots, reqs, LANES), f32),
            pltpu.VMEM((spots, reqs, LANES), f32),
            pltpu.SemaphoreType.DMA((len(given),)),
            pltpu.SemaphoreType.DMA((blocks,)),
        ],
        compiler_params=pltpu.CompilerParams(vmem_limit_bytes=24 << 20),
        cost_estimate=pl.CostEstimate(
            flops=2 * tokens * inner * width, bytes_accessed=12 << 20, transcendentals=4_000_000
        ),
        name="after_states",
    )(moved, accepted, *given)


def exchange(values):
    return lax.all_to_all(values, "req", split_axis=0, concat_axis=0, tiled=True)


def select_kernel(mask_ref, arrived_ref, out_ref):
    width = arrived_ref.shape[1] // 19
    at = 16 * width
    spans = [(0, 0, at)] + [(e + 1, at + e * width, width) for e in range(3)]
    for which, start, size in spans:
        cols = pl.ds(start, size)
        out_ref[:, cols] = jnp.dot(
            mask_ref[which], arrived_ref[:, cols], preferred_element_type=jnp.float32
        ).astype(jnp.bfloat16)


def select(masks, arrived):
    if arrived.shape[1] % (19 * LANES) == 0:
        return pl.pallas_call(
            select_kernel,
            out_shape=jax.ShapeDtypeStruct(arrived.shape, jnp.bfloat16),
            in_specs=[pl.BlockSpec(memory_space=pltpu.VMEM)] * 2,
            out_specs=pl.BlockSpec(memory_space=pltpu.VMEM),
            compiler_params=pltpu.CompilerParams(vmem_limit_bytes=16 << 20),
            name="select_slots",
        )(masks, arrived)
    width = arrived.shape[1] // 19
    cut = [0] + [(16 + e) * width for e in range(4)]
    return jnp.concatenate(
        [
            jnp.dot(
                masks[i], arrived[:, cut[i] : cut[i + 1]], preferred_element_type=jnp.float32
            ).astype(jnp.bfloat16)
            for i in range(4)
        ],
        axis=1,
    )


def on_device(
    groups,
    hidden,
    norm_gain,
    in_weight,
    conv_weight,
    conv_bias,
    x_weight,
    step_weight,
    step_bias,
    log_decay,
    skip_gain,
    out_weight,
    old_states,
    old_edges,
    anchor,
    fresh_flag,
    accepted,
    request_ages,
):
    local_reqs, draft_len, width = hidden.shape
    inner_width = out_weight.shape[0]
    channels = conv_weight.shape[1]
    state_size = log_decay.shape[0]
    span = old_edges.shape[1]
    all_reqs = anchor.shape[0]
    blocks = inner_width // channels
    tokens = draft_len * local_reqs

    arrived = exchange(
        pack(old_states, old_edges, blocks).reshape(all_reqs, (state_size + span) * channels)
    )
    old_slot = jnp.arange(all_reqs, dtype=jnp.int32)
    chosen = (anchor[:, None] == old_slot[None, :]) & (fresh_flag[:, None] == 0)
    masks = jnp.stack([chosen] + [chosen & (span - e <= request_ages)[:, None] for e in range(span)])
    token_major = jnp.swapaxes(hidden, 0, 1).reshape(tokens, width)
    normed = rms_normed(token_major, norm_gain)
    projected = jnp.dot(normed, in_weight, preferred_element_type=jnp.float32).astype(jnp.bfloat16)
    masks, projected = lax.optimization_barrier((masks.astype(jnp.bfloat16), projected))
    moved = exchange(select(masks, arrived))

    share = weight_share(
        groups, x_weight, step_weight, conv_weight, conv_bias, step_bias, skip_gain, log_decay
    )
    weights = doubled(doubled(share[None], "req")[None], "grp")
    q_place, j_place = places("grp"), places("req")
    if channels != BLOCK:
        moved = moved.reshape(blocks, local_reqs, state_size + span, channels).transpose(1, 2, 0, 3)
        moved = moved.reshape(local_reqs, state_size + span, -1, BLOCK).transpose(2, 0, 1, 3)
        weights = jnp.take(weights, j_place, axis=1).swapaxes(1, 2)
        weights = weights.reshape(groups, SHARE, -1, BLOCK).swapaxes(1, 2)
        j_place = jnp.arange(inner_width // BLOCK, dtype=jnp.int32)
    moved = moved.reshape(inner_width // BLOCK, local_reqs, (state_size + span) * BLOCK)

    mine = lax.dynamic_slice_in_dim(accepted, lax.axis_index("req") * local_reqs, local_reqs, 0)
    mine = jnp.broadcast_to(mine[:, None], (local_reqs, LANES))
    early = before(q_place, j_place, projected, weights, mine, span * local_reqs, state_size)
    layer_out, new_states = after(moved, mine, early, out_weight)
    return layer_out, new_states.reshape(local_reqs, state_size, inner_width)


def solution(mesh):
    return jax.shard_map(
        functools.partial(on_device, mesh.shape["grp"]),
        mesh=mesh,
        in_specs=(
            P(("grp", "req"), None, None),
            P(),
            P(),
            P(None, "req"),
            P("req"),
            P("req", None),
            P(None, "req"),
            P("req"),
            P(None, "req"),
            P("req"),
            P(),
            P(("grp", "req"), None, None),
            P(("grp", "req"), None, None),
            P("grp"),
            P("grp"),
            P("grp"),
            P("grp"),
        ),
        out_specs=(P(("grp", "req"), None, None), P(("grp", "req"), None, None)),
        check_vma=False,
    )
```

time: 70 us -> 63.3 us (0.904)
  local copies, waits for them, and re-layouts: 10.2 us -> 0.27 us
  Pallas kernels: 15.7 us -> 22.1 us
  waiting for transfers between devices: 17.6 us -> 13.4 us
  other arithmetic: 0.65 us -> 1.77 us
    unnamed x36 -> x14, local copies, waits for them, and re-layouts: 9.99 us -> 0.04 us
    pallas_call x3, Pallas kernels: 13 us -> 19.3 us  [the longest x1 9.75 us: after(): pl.pallas_call(after_kernel, out_shape=(jax.ShapeDtypeStruct((reqs, draft...]
    ppermute x5, waiting for transfers between devices: 13.8 us -> 11 us  [doubled(): other = lax.ppermute(values, axis, [(i, i ^ bit) for i in range(size)])]
    all_to_all x2, waiting for transfers between devices: 3.7 us -> 2.4 us  [exchange(): lax.all_to_all(values, 'req', split_axis=0, concat_axis=0, tiled=True)]
    concatenate x4, other arithmetic: 0.24 us -> 1.35 us  [doubled(): values = jnp.concatenate([values, other], axis=0)]
  transfers between devices with their start and end apart: 7 -> 7, of which waited for: 3 -> 4; matrix products, arithmetic and copies ran while one was open for 8% -> 11% of each run, Pallas kernels for 6% -> 17%
where the time goes in v3:
time: 63.3 us; the launch traced here: 62.8 us
  Pallas kernels  22.1 us (35%)
  starting transfers between devices  19.7 us (31%)
  waiting for transfers between devices  13.4 us (21%)
  matrix products  4.78 us (8%)
  other arithmetic  1.77 us (3%)
  between operations  0.82 us (1%)
    ppermute x5, waiting for transfers between devices, doubled(): other = lax.ppermute(values, axis, [(i, i ^ bit) for i in range(size)])  11 us
    all_to_all x2, starting transfers between devices, exchange(): lax.all_to_all(values, 'req', split_axis=0, concat_axis=0, tiled=True)  10.1 us
    pallas_call x1, Pallas kernels, after(): pl.pallas_call(after_kernel, out_shape=(jax.ShapeDtypeStruct((reqs, draft...  9.75 us
    ppermute x5, starting transfers between devices, doubled(): other = lax.ppermute(values, axis, [(i, i ^ bit) for i in range(size)])  9.57 us
    pallas_call x1, Pallas kernels, before(): pl.pallas_call(before_kernel, out_shape=tuple((pltpu.HBM(shape, dtype) fo...  7.34 us
    dot_general x1, matrix products, on_device(): jnp.dot(normed, in_weight, preferred_element_type=jnp.float32)  4.78 us
    all_to_all x2, waiting for transfers between devices, exchange(): lax.all_to_all(values, 'req', split_axis=0, concat_axis=0, tiled=True)  2.4 us
    pallas_call x1, Pallas kernels, pack(): pl.pallas_call(pack_kernel, out_shape=pltpu.HBM((blocks, slots, (states +...  2.26 us
  transfers between devices with their start and end apart: 7, of which 4 were waited for; matrix products, arithmetic and copies ran while one was open for 11% of the time, Pallas kernels for 17%

profile of v3, /device:TPU:0, one launch (start us, length us, event | category | flops | bytes accessed | tf_op | source)
XLA Modules:
  0.0 62.8 jit_solution(17046034058633498201)
XLA Ops:
  0.7 1.6 %weight_share.1 = bf16[88,256]{1,0:T(8,128)(2,1)} custom-call(s32[1]{0:T(128)} %bitcast.7.group_ref, bf16[160,256]{1,0:T(8,128)(2,1)} %bitcast.34, bf16[128,256]{1,0:T(8,128)(2,1)} %sw_ref.1, f32[4,256]{1,0:T(4,128)} %cw_ref.1, f32[1,256]{1,0:T(1,128)} %bitcast.35, f32[1,256]{1,0:T(1,128)} %bitcast.36, f32[1,256]{1,0:T(1,128)} %bitcast.37, f32[16,256]{1,0:T(8,128)} %ld_ref.1), custom_call_target="tpu_custom_call" | custom-call | tf_op jit(solution)/shard_map/weight_share/pallas_call | solution.py:119
  2.3 4.0 %collective-permute-start = (bf16[1,88,256]{2,1,0:T(8,128)(2,1)}, bf16[1,88,256]{2,1,0:T(8,128)(2,1)S(1)}, u32[]{:S(2)}, u32[]{:S(2)}) collective-permute-start(bf16[1,88,256]{2,1,0:T(8,128)(2,1)} %bitcast.29), channel_id=1, source_target_pairs={{0,16},{4,20},{8,24},{12,28},{16,0},{20,4},{24,8},{28,12},{1,17},{... | collective-permute-start | bytes 135176 | tf_op jit(solution)/shard_map/ppermute | solution.py:155
  6.3 2.3 %pack_states.1 = bf16[8,8,4864]{2,1,0:T(8,128)(2,1)} custom-call(f32[128,2048]{1,0:T(8,128)} %bitcast.28, bf16[3,8,2048]{2,1,0:T(8,128)(2,1)} %bitcast.33), custom_call_target="tpu_custom_call" | custom-call | tf_op jit(solution)/shard_map/pack_states/pallas_call | solution.py:67
  8.6 3.8 %all-to-all-start = ((bf16[8,8,4864]{2,1,0:T(8,128)(2,1)}), bf16[8,8,4864]{2,1,0:T(8,128)(2,1)S(1)}, u32[]{:S(2)}, u32[]{:S(2)}) async-start(bf16[8,8,4864]{2,1,0:T(8,128)(2,1)} %pack_states.1), calls=%async_computation | async-start | bytes 1245184 | tf_op jit(solution)/shard_map/all_to_all | solution.py:486
  12.4 0.2 fusion.3
  12.6 0.1 rsqrt.12
  12.8 2.1 %collective-permute-start.1 = (bf16[2,88,256]{2,1,0:T(8,128)(2,1)S(1)}, bf16[2,88,256]{2,1,0:T(8,128)(2,1)S(1)}, u32[]{:S(2)}, u32[]{:S(2)}) collective-permute-start(bf16[2,88,256]{2,1,0:T(8,128)(2,1)S(1)} %pad_maximum_fusion.3), channel_id=1, source_target_pairs={{0,8},{4,12},{8,0},{12,4},{16,24},{20,28},{24,16},{28,20},{1,9},{5... | collective-permute-start | bytes 270344 | tf_op jit(solution)/shard_map/ppermute | solution.py:155
  14.9 4.8 %convolution_convert_fusion.proj_ref = bf16[128,4096]{1,0:T(8,128)(2,1)S(1)} fusion(bf16[1024,4096]{1,0:T(8,128)(2,1)} %param.19, f32[1024]{0:T(1024)S(1)} %copy-done.2, f32[128]{0:T(128)S(1)} %rsqrt.12, bf16[8,16,1024]{2,1,0:T(8,128)(2,1)S(1)} %copy-done), kind=kOutput, calls=%fused_computation | convolution fusion | flops 1074790400 | bytes 9703936 | tf_op jit(solution)/shard_map/dot_general | solution.py:560
  19.7 4.6 %collective-permute-done.1 = bf16[2,88,256]{2,1,0:T(8,128)(2,1)S(1)} collective-permute-done((bf16[2,88,256]{2,1,0:T(8,128)(2,1)S(1)}, bf16[2,88,256]{2,1,0:T(8,128)(2,1)S(1)}, u32[]{:S(2)}, u32[]{:S(2)}) %collective-permute-start.1) | collective-permute-done | bytes 90144 | tf_op jit(solution)/shard_map/ppermute | solution.py:155
  24.3 1.8 %collective-permute-start.2 = (bf16[4,88,256]{2,1,0:T(8,128)(2,1)S(1)}, bf16[4,88,256]{2,1,0:T(8,128)(2,1)S(1)}, u32[]{:S(2)}, u32[]{:S(2)}) collective-permute-start(bf16[4,88,256]{2,1,0:T(8,128)(2,1)S(1)} %pad_maximum_fusion.2), channel_id=1, source_target_pairs={{0,4},{4,0},{8,12},{12,8},{16,20},{20,16},{24,28},{28,24},{1,5},{5... | collective-permute-start | bytes 540680 | tf_op jit(solution)/shard_map/ppermute | solution.py:155
  26.1 4.2 %collective-permute-done.2 = bf16[4,88,256]{2,1,0:T(8,128)(2,1)S(1)} collective-permute-done((bf16[4,88,256]{2,1,0:T(8,128)(2,1)S(1)}, bf16[4,88,256]{2,1,0:T(8,128)(2,1)S(1)}, u32[]{:S(2)}, u32[]{:S(2)}) %collective-permute-start.2) | collective-permute-done | bytes 180256 | tf_op jit(solution)/shard_map/ppermute | solution.py:155
  30.4 1.6 %collective-permute-start.3 = (bf16[1,8,88,256]{3,2,1,0:T(8,128)(2,1)S(1)}, bf16[1,8,88,256]{3,2,1,0:T(8,128)(2,1)S(1)}, u32[]{:S(2)}, u32[]{:S(2)}) collective-permute-start(bf16[1,8,88,256]{3,2,1,0:T(8,128)(2,1)S(1)} %maximum_bitcast_fusion), channel_id=1, source_target_pairs={{0,2},{1,3},{2,0},{3,1},{4,6},{5,7},{6,4},{7,5},{8,10},{9,11},{10,... | collective-permute-start | bytes 1081352 | tf_op jit(solution)/shard_map/ppermute | solution.py:155
  32.0 0.1 fusion.8
  32.1 1.1 %select_slots.1 = bf16[64,4864]{1,0:T(8,128)(2,1)} custom-call(bf16[4,64,64]{2,1,0:T(8,128)(2,1)S(1)} %add_convert_fusion.mask_ref, bf16[64,4864]{1,0:T(8,128)(2,1)S(1)} %bitcast.27), custom_call_target="tpu_custom_call" | custom-call | tf_op jit(solution)/shard_map/select_slots/pallas_call | solution.py:502
  33.2 6.3 %all-to-all-start.1 = ((bf16[8,8,4864]{2,1,0:T(8,128)(2,1)}), bf16[8,8,4864]{2,1,0:T(8,128)(2,1)S(1)}, u32[]{:S(2)}, u32[]{:S(2)}) async-start(bf16[8,8,4864]{2,1,0:T(8,128)(2,1)} %bitcast.6), calls=%async_computation.1 | async-start | bytes 1245184 | tf_op jit(solution)/shard_map/all_to_all | solution.py:486
  39.5 0.1 pad_maximum_fusion.1
  39.6 0.1 collective-permute-start.4
  39.7 0.1 dynamic_slice.3
  39.8 2.2 %collective-permute-done.4 = bf16[2,8,88,256]{3,2,1,0:T(8,128)(2,1)} collective-permute-done((bf16[2,8,88,256]{3,2,1,0:T(8,128)(2,1)S(1)}, bf16[2,8,88,256]{3,2,1,0:T(8,128)(2,1)}, u32[]{:S(2)}, u32[]{:S(2)}) %collective-permute-start.4) | collective-permute-done | bytes 720928 | tf_op jit(solution)/shard_map/ppermute | solution.py:155
  42.0 1.3 %pad_maximum_fusion.w_ref = bf16[4,8,88,256]{3,2,1,0:T(8,128)(2,1)S(1)} fusion(bf16[2,8,88,256]{3,2,1,0:T(8,128)(2,1)} %collective-permute-done.4, bf16[1,8,88,256]{3,2,1,0:T(8,128)(2,1)S(1)} %collective-permute-done.3, bf16[1,8,88,256]{3,2,1,0:T(8,128)(2,1)S(1)} %maximum_bitcast_fusion), kind=kLoop, calls=%fused_computation.1 | loop fusion | flops 1441792 | bytes 2883584 | tf_op jit(solution)/shard_map/concatenate | solution.py:156
  43.3 0.1 broadcast_in_dim.50.acc_ref
  43.3 7.3 %before_states.1 = (f32[16,104,128]{2,1,0:T(8,128)}, f32[16,128,128]{2,1,0:T(8,128)}, f32[16,104,128]{2,1,0:T(8,128)}, f32[16,8,128]{2,1,0:T(8,128)}, f32[16,128...) custom-call(s32[4]{0:T(128)S(1)} %fusion.9.q_ref, ...), custom_call_target="tpu_custom_call" | custom-call | flops 200000000 | bytes 8388608 | tf_op jit(solution)/shard_map/before_states/pallas_call | solution.py:320
  50.7 2.4 %all-to-all-done.1.moved_ref = bf16[8,8,4864]{2,1,0:T(8,128)(2,1)S(1)} async-done(((bf16[8,8,4864]{2,1,0:T(8,128)(2,1)}), bf16[8,8,4864]{2,1,0:T(8,128)(2,1)S(1)}, u32[]{:S(2)}, u32[]{:S(2)}) %all-to-all-start.1) | async-done | bytes 622624 | tf_op jit(solution)/shard_map/all_to_all | solution.py:486
  53.1 9.7 %after_states.1 = (bf16[8,16,1024]{2,1,0:T(8,128)(2,1)}, f32[128,2048]{1,0:T(8,128)}) custom-call(bf16[8,8,4864]{2,1,0:T(8,128)(2,1)S(1)} %all-to-all-done.1.moved_ref, s32[8,128]{1,0:T(8,128)S(1)} %broadcast_in_dim.50.acc_ref, f32[16,104,128]{2,1,0:T(8,128)} %get-tuple-element.18.refs_0_, f32[16,128,128]{2,1,0:T(8,128)} %get-tuple-element.19.refs_1_, ...), custom_call_target="tpu_custom_call" | custom-call | flops 536870912 | bytes 12582912 | tf_op jit(solution)/shard_map/after_states/pallas_call | solution.py:457
  (25 shorter events, 0.2 us)
Async XLA Ops:
  0.6 11.8 %copy-start = (bf16[8,16,1024]{2,1,0:T(8,128)(2,1)S(1)}, bf16[8,16,1024]{2,1,0:T(8,128)(2,1)}, u32[]{:S(2)}) copy-start(bf16[8,16,1024]{2,1,0:T(8,128)(2,1)} %param.17) | copy-start | bytes 786436
  0.6 14.3 %copy-start.2 = (f32[1024]{0:T(1024)S(1)}, f32[1024]{0:T(1024)}, u32[]{:S(2)}) copy-start(f32[1024]{0:T(1024)} %param.18) | copy-start | bytes 12292
  2.3 10.4 %copy-start.1 = (bf16[88,256]{1,0:T(8,128)(2,1)S(1)}, bf16[88,256]{1,0:T(8,128)(2,1)}, u32[]{:S(2)}) copy-start(bf16[88,256]{1,0:T(8,128)(2,1)} %weight_share.1) | copy-start | bytes 135172
  2.3 10.4 %collective-permute-start = (bf16[1,88,256]{2,1,0:T(8,128)(2,1)}, bf16[1,88,256]{2,1,0:T(8,128)(2,1)S(1)}, u32[]{:S(2)}, u32[]{:S(2)}) collective-permute-start(bf16[1,88,256]{2,1,0:T(8,128)(2,1)} %bitcast.29), channel_id=1, source_target_pairs={{0,16},{4,20},{8,24},{12,28},{16,0},{20,4},{24,8},{28,12},{1,17},{... | collective-permute-start | bytes 135176 | tf_op jit(solution)/shard_map/ppermute | solution.py:155
  8.6 23.5 %all-to-all-start = ((bf16[8,8,4864]{2,1,0:T(8,128)(2,1)}), bf16[8,8,4864]{2,1,0:T(8,128)(2,1)S(1)}, u32[]{:S(2)}, u32[]{:S(2)}) async-start(bf16[8,8,4864]{2,1,0:T(8,128)(2,1)} %pack_states.1), calls=%async_computation | async-start | bytes 1245184 | tf_op jit(solution)/shard_map/all_to_all | solution.py:486
  12.8 13.3 %copy-start.4 = (s32[64]{0:T(128)S(1)}, s32[64]{0:T(128)}, u32[]{:S(2)}) copy-start(s32[64]{0:T(128)} %param.33) | copy-start | bytes 772
  12.8 13.3 %copy-start.5 = (s32[64]{0:T(128)S(1)}, s32[64]{0:T(128)}, u32[]{:S(2)}) copy-start(s32[64]{0:T(128)} %param.31) | copy-start | bytes 772
  12.8 19.2 %copy-start.3 = (s32[64]{0:T(128)S(1)}, s32[64]{0:T(128)}, u32[]{:S(2)}) copy-start(s32[64]{0:T(128)} %param.30) | copy-start | bytes 772
  12.8 11.5 %collective-permute-start.1 = (bf16[2,88,256]{2,1,0:T(8,128)(2,1)S(1)}, bf16[2,88,256]{2,1,0:T(8,128)(2,1)S(1)}, u32[]{:S(2)}, u32[]{:S(2)}) collective-permute-start(bf16[2,88,256]{2,1,0:T(8,128)(2,1)S(1)} %pad_maximum_fusion.3), channel_id=1, source_target_pairs={{0,8},{4,12},{8,0},{12,4},{16,24},{20,28},{24,16},{28,20},{1,9},{5... | collective-permute-start | bytes 270344 | tf_op jit(solution)/shard_map/ppermute | solution.py:155
  24.3 6.0 %collective-permute-start.2 = (bf16[4,88,256]{2,1,0:T(8,128)(2,1)S(1)}, bf16[4,88,256]{2,1,0:T(8,128)(2,1)S(1)}, u32[]{:S(2)}, u32[]{:S(2)}) collective-permute-start(bf16[4,88,256]{2,1,0:T(8,128)(2,1)S(1)} %pad_maximum_fusion.2), channel_id=1, source_target_pairs={{0,4},{4,0},{8,12},{12,8},{16,20},{20,16},{24,28},{28,24},{1,5},{5... | collective-permute-start | bytes 540680 | tf_op jit(solution)/shard_map/ppermute | solution.py:155
  30.3 9.4 %copy-start.6 = (s32[64]{0:T(128)S(1)}, s32[64]{0:T(128)}, u32[]{:S(2)}) copy-start(s32[64]{0:T(128)} %param.32) | copy-start | bytes 772
  30.4 9.2 %collective-permute-start.3 = (bf16[1,8,88,256]{3,2,1,0:T(8,128)(2,1)S(1)}, bf16[1,8,88,256]{3,2,1,0:T(8,128)(2,1)S(1)}, u32[]{:S(2)}, u32[]{:S(2)}) collective-permute-start(bf16[1,8,88,256]{3,2,1,0:T(8,128)(2,1)S(1)} %maximum_bitcast_fusion), channel_id=1, source_target_pairs={{0,2},{1,3},{2,0},{3,1},{4,6},{5,7},{6,4},{7,5},{8,10},{9,11},{10,... | collective-permute-start | bytes 1081352 | tf_op jit(solution)/shard_map/ppermute | solution.py:155
  33.2 19.9 %all-to-all-start.1 = ((bf16[8,8,4864]{2,1,0:T(8,128)(2,1)}), bf16[8,8,4864]{2,1,0:T(8,128)(2,1)S(1)}, u32[]{:S(2)}, u32[]{:S(2)}) async-start(bf16[8,8,4864]{2,1,0:T(8,128)(2,1)} %bitcast.6), calls=%async_computation.1 | async-start | bytes 1245184 | tf_op jit(solution)/shard_map/all_to_all | solution.py:486
  39.6 2.4 %collective-permute-start.4 = (bf16[2,8,88,256]{3,2,1,0:T(8,128)(2,1)S(1)}, bf16[2,8,88,256]{3,2,1,0:T(8,128)(2,1)}, u32[]{:S(2)}, u32[]{:S(2)}) collective-permute-start(bf16[2,8,88,256]{3,2,1,0:T(8,128)(2,1)S(1)} %pad_maximum_fusion.1), channel_id=1, source_target_pairs={{0,1},{1,0},{2,3},{3,2},{4,5},{5,4},{6,7},{7,6},{8,9},{9,8},{10,11... | collective-permute-start | bytes 2162696 | tf_op jit(solution)/shard_map/ppermute | solution.py:155

commit v4 on v3

--- a/solution.py
+++ b/solution.py
@@ -24,11 +24,16 @@
     return pltpu.with_memory_space_constraint(values, pltpu.HBM)
 
 
-def pack_kernel(state_ref, edge_ref, out_ref, tile_ref, held_ref, send_ref, sems):
+def send_kernel(
+    group_ref, state_ref, edge_ref, xt_ref, sw_ref, cw_ref, cb_ref, sb_ref, sk_ref, ld_ref,
+    out_ref, share_ref,
+    tile_ref, held_ref, send_ref, xt_in, sw_in, vec_ref, sems, few,
+):
     blocks, slots, _ = out_ref.shape
     width = state_ref.shape[1] // blocks
     states = state_ref.shape[0] // slots
     per = width // LANES
+    rank = sw_ref.shape[0]
 
     def load(tile):
         cols = pl.ds(tile * LANES, LANES)
@@ -37,11 +42,41 @@
     def store(dest):
         return pltpu.make_async_copy(send_ref.at[dest], out_ref.at[dest], sems.at[1, dest])
 
-    edges = pltpu.make_async_copy(edge_ref, held_ref, sems.at[1, blocks])
-    edges.start()
+    small = [
+        (edge_ref, held_ref),
+        (xt_ref, xt_in),
+        (sw_ref, sw_in),
+        (cw_ref, vec_ref.at[pl.ds(0, 4), :]),
+        (cb_ref, vec_ref.at[pl.ds(4, 1), :]),
+        (sb_ref, vec_ref.at[pl.ds(5, 1), :]),
+        (sk_ref, vec_ref.at[pl.ds(6, 1), :]),
+        (ld_ref, vec_ref.at[pl.ds(8, 16), :]),
+    ]
+    copies = [pltpu.make_async_copy(x, y, few.at[i]) for i, (x, y) in enumerate(small)]
+    vec_ref[pl.ds(7, 1), :] = jnp.zeros((1, width), jnp.float32)
+    vec_ref[pl.ds(24, 8), :] = jnp.zeros((8, width), jnp.float32)
+    for copy in copies:
+        copy.start()
     for tile in range(blocks * per):
         load(tile).start()
-    edges.wait()
+    for copy in copies:
+        copy.wait()
+    for k in range(4):
+
+        @pl.when(group_ref[0] == k)
+        def _():
+            vec = vec_ref[pl.ds(16 * (k % 2), 16), :]
+            high = vec.astype(jnp.bfloat16).astype(jnp.float32)
+            part = high if k < 2 else vec - high
+            rows = [
+                xt_in[pl.ds(32 * k, 32), :].astype(jnp.float32),
+                xt_in[pl.ds(rank + 8 * k, 8), :].astype(jnp.float32),
+                part[:8],
+                sw_in[pl.ds(32 * k, 32), :].astype(jnp.float32),
+                part[8:],
+            ]
+            share_ref[...] = jnp.concatenate(rows, axis=0).astype(jnp.bfloat16)
+
     for dest in range(blocks):
         for e in range(edge_ref.shape[0]):
             at = (states + e) * width
@@ -57,103 +92,78 @@
         store(dest).wait()
 
 
-def pack(old_states, old_edges, blocks):
+def prepared(
+    old_states, old_edges, x_weight, step_weight, conv_weight, conv_bias, step_bias, skip_gain, log_decay
+):
     slots, states, inner = old_states.shape
     span = old_edges.shape[1]
-    width = inner // blocks
+    width = x_weight.shape[0]
+    blocks = inner // width
+    rank = step_weight.shape[0]
     edges = jnp.swapaxes(old_edges, 0, 1)
+    xt = x_weight.T
+    group = lax.axis_index("grp").astype(jnp.int32)
     if width % LANES == 0 and slots == 8:
         tiles = inner // LANES
+        vmem = pl.BlockSpec(memory_space=pltpu.VMEM)
+        hbm = pl.BlockSpec(memory_space=pltpu.HBM)
+        given = (
+            old_states.reshape(slots * states, inner), edges, xt, step_weight, conv_weight,
+            conv_bias[None], step_bias[None], skip_gain[None], log_decay,
+        )
         return pl.pallas_call(
-            pack_kernel,
-            out_shape=pltpu.HBM((blocks, slots, (states + span) * width), jnp.bfloat16),
-            in_specs=[pl.BlockSpec(memory_space=pltpu.HBM)] * 2,
-            out_specs=pl.BlockSpec(memory_space=pltpu.HBM),
+            send_kernel,
+            out_shape=(
+                pltpu.HBM((blocks, slots, (states + span) * width), jnp.bfloat16),
+                jax.ShapeDtypeStruct((SHARE, width), jnp.bfloat16),
+            ),
+            in_specs=[pl.BlockSpec(memory_space=pltpu.SMEM)] + [hbm] * len(given),
+            out_specs=(hbm, vmem),
             scratch_shapes=[
                 pltpu.VMEM((tiles, slots * states, LANES), jnp.float32),
                 pltpu.VMEM((span, slots, inner), jnp.bfloat16),
                 pltpu.VMEM((blocks, slots, (states + span) * width), jnp.bfloat16),
-                pltpu.SemaphoreType.DMA((2, max(tiles, blocks + 1))),
+                pltpu.VMEM(xt.shape, jnp.bfloat16),
+                pltpu.VMEM(step_weight.shape, jnp.bfloat16),
+                pltpu.VMEM((32, width), jnp.float32),
+                pltpu.SemaphoreType.DMA((2, tiles)),
+                pltpu.SemaphoreType.DMA((8,)),
             ],
             compiler_params=pltpu.CompilerParams(vmem_limit_bytes=16 << 20),
-            name="pack_states",
-        )(in_hbm(old_states.reshape(slots * states, inner)), in_hbm(edges))
+            name="send_states",
+        )(group[None], *[in_hbm(x) for x in given])
     lead = jnp.swapaxes(old_states.astype(jnp.bfloat16), 0, 1)
     both = jnp.concatenate([lead, edges], axis=0)
     both = both.reshape(states + span, slots, blocks, width)
-    return both.transpose(2, 1, 0, 3).reshape(blocks, slots, (states + span) * width)
-
-
-def share_kernel(group_ref, xt_ref, sw_ref, cw_ref, cb_ref, sb_ref, sk_ref, ld_ref, out_ref, vec_ref):
-    rank = sw_ref.shape[0]
-    groups = rank // 32
-    vec_ref[...] = jnp.zeros_like(vec_ref)
-    vec_ref[pl.ds(0, 4), :] = cw_ref[...]
-    vec_ref[pl.ds(4, 1), :] = cb_ref[...]
-    vec_ref[pl.ds(5, 1), :] = sb_ref[...]
-    vec_ref[pl.ds(6, 1), :] = sk_ref[...]
-    vec_ref[pl.ds(8, 16), :] = ld_ref[...]
-    for k in range(groups):
-
-        @pl.when(group_ref[0] == k)
-        def _():
-            vec = vec_ref[pl.ds(16 * (k % 2), 16), :]
-            high = vec.astype(jnp.bfloat16).astype(jnp.float32)
-            part = high if k < 2 else vec - high
-            rows = [
-                xt_ref[pl.ds(32 * k, 32), :].astype(jnp.float32),
-                xt_ref[pl.ds(rank + 8 * k, 8), :].astype(jnp.float32),
-                part[:8],
-                sw_ref[pl.ds(32 * k, 32), :].astype(jnp.float32),
-                part[8:],
-            ]
-            out_ref[...] = jnp.concatenate(rows, axis=0).astype(jnp.bfloat16)
-
-
-def weight_share(groups, x_weight, step_weight, conv_weight, conv_bias, step_bias, skip_gain, log_decay):
-    channels = x_weight.shape[0]
-    rank = step_weight.shape[0]
-    xt = x_weight.T
-    group = lax.axis_index("grp").astype(jnp.int32)
-    if channels % LANES == 0:
-        return pl.pallas_call(
-            share_kernel,
-            out_shape=jax.ShapeDtypeStruct((SHARE, channels), jnp.bfloat16),
-            in_specs=[pl.BlockSpec(memory_space=pltpu.SMEM)] + [pl.BlockSpec(memory_space=pltpu.VMEM)] * 7,
-            out_specs=pl.BlockSpec(memory_space=pltpu.VMEM),
-            scratch_shapes=[pltpu.VMEM((32, channels), jnp.float32)],
-            name="weight_share",
-        )(
-            group[None], xt, step_weight, conv_weight, conv_bias[None], step_bias[None],
-            skip_gain[None], log_decay,
-        )
+    packed = both.transpose(2, 1, 0, 3).reshape(blocks, slots, (states + span) * width)
+    none = jnp.zeros_like(conv_bias)[None]
     vec = jnp.concatenate(
-        [conv_weight, conv_bias[None], step_bias[None], skip_gain[None], jnp.zeros_like(conv_bias)[None], log_decay],
-        axis=0,
+        [conv_weight, conv_bias[None], step_bias[None], skip_gain[None], none, log_decay], axis=0
     )
     vec = jnp.pad(vec, ((0, 8), (0, 0)))
     high = vec.astype(jnp.bfloat16)
-    both = jnp.concatenate([high, (vec - high.astype(jnp.float32)).astype(jnp.bfloat16)], axis=0)
-    both = both.reshape(4, 16, channels)
+    halves = jnp.concatenate([high, (vec - high.astype(jnp.float32)).astype(jnp.bfloat16)], axis=0)
+    halves = halves.reshape(4, 16, width)
     stacked = jnp.concatenate(
         [
-            xt[:rank].reshape(4, 32, channels),
-            xt[rank:].reshape(4, 8, channels),
-            both[:, :8],
-            step_weight.reshape(4, 32, channels),
-            both[:, 8:],
+            xt[:rank].reshape(4, 32, width),
+            xt[rank:].reshape(4, 8, width),
+            halves[:, :8],
+            step_weight.reshape(4, 32, width),
+            halves[:, 8:],
         ],
         axis=1,
     )
-    return lax.dynamic_index_in_dim(stacked, group, 0, keepdims=False)
-
-
-def doubled(values, axis):
-    size = lax.axis_size(axis)
-    bit = size // 2
+    return packed, lax.dynamic_index_in_dim(stacked, group, 0, keepdims=False)
+
+
+def moved_by(values, axis, bits):
+    return lax.ppermute(values, axis, [(i, i ^ bits) for i in range(lax.axis_size(axis))])
+
+
+def doubled(values, axis, bit):
     while bit:
-        other = lax.ppermute(values, axis, [(i, i ^ bit) for i in range(size)])
-        values = jnp.concatenate([values, other], axis=0)
+        values = jnp.concatenate([values, moved_by(values, axis, bit)], axis=0)
         bit //= 2
     return values
 
@@ -213,19 +223,26 @@
         c_ref[t * states + n] = jnp.broadcast_to(rows[:, states + n : states + n + 1], (reqs, LANES))
 
 
-def before_kernel(q_ref, j_ref, proj_ref, w_ref, acc_ref, *refs):
-    results, kept, (dt_ref, cv_ref, b_ref, dec_ref, sems) = refs[:10], refs[10:20], refs[20:]
-    y_ref, sg_ref, sum_ref, at_ref, ga_ref, c_ref, xw_ref, sw_ref, vec_ref, x_ref = kept
+def before_kernel(
+    q_ref, j_ref, proj_ref, w_ref, acc_ref,
+    rows_out, at_ref, coef_ref, xw_ref, sw_ref, vec_ref, x_ref,
+    rows_ref, dt_ref, cv_ref, b_ref, c_ref, dec_ref, sems,
+):
     blocks = w_ref.shape[1]
-    tiles, count, _ = y_ref.shape
-    tokens = sg_ref.shape[1]
+    tiles, count, _ = dt_ref.shape
+    tokens = proj_ref.shape[0]
     late = tokens - count
     reqs = late // 3
     states = b_ref.shape[0] * reqs // count
     inner = blocks * BLOCK
     rank = sw_ref.shape[1]
     per = BLOCK // LANES
-    copies = [pltpu.make_async_copy(kept[i], results[i], sems.at[i]) for i in range(len(kept))]
+    y_at, sum_at, gate_at, state_at = row_offsets(count, tokens)
+
+    def copy(j):
+        some = pl.ds(j * per, per)
+        return pltpu.make_async_copy(rows_ref.at[some], rows_out.at[some], sems.at[j])
+
     mixed = jnp.zeros((count, rank + 2 * states), jnp.float32)
     for j in range(blocks):
         xw, sw, vec = block_weights(w_ref, q_ref, j_ref, j)
@@ -244,12 +261,10 @@
             tile = j * per + k
             lanes = slice(k * LANES, (k + 1) * LANES)
             cv_ref[tile] = full[:, lanes]
-            sg_ref[tile] = gate[:, lanes]
-            y_ref[tile] = vec[6:7, lanes] * full[:, lanes]
+            rows_ref[tile, pl.ds(gate_at, tokens), :] = gate[:, lanes]
+            rows_ref[tile, pl.ds(y_at, count), :] = vec[6:7, lanes] * full[:, lanes]
             for n in range(states):
                 dec_ref[tile, n] = jnp.broadcast_to(decay2[n : n + 1, lanes], (reqs, LANES))
-    for i in (1, 6, 7, 8, 9):
-        copies[i].start()
     rounded = mixed.astype(jnp.bfloat16)
     for j in range(blocks):
         dt = softplus(
@@ -259,39 +274,46 @@
         for k in range(per):
             dt_ref[j * per + k] = dt[:, k * LANES : (k + 1) * LANES]
     coefs = rounded[:, rank:].astype(jnp.float32)
+    coef_ref[...] = coefs
     for t in range(count // reqs):
         spread(coefs[t * reqs : (t + 1) * reqs], t, b_ref, c_ref)
-    copies[5].start()
     accepted = acc_ref[...]
-    ga_ref[...] = jnp.zeros_like(ga_ref)
     at_ref[...] = jnp.zeros_like(at_ref)
 
     @pl.loop(0, tiles)
     def _(tile):
         state = [None] * states
         passed = None
+        rows_ref[tile, pl.ds(state_at, states * reqs), :] = jnp.zeros((states * reqs, LANES), jnp.float32)
         for t in range(count // reqs):
-            rows = pl.ds(t * reqs, reqs)
-            delta = dt_ref[tile, rows, :]
+            delta = dt_ref[tile, pl.ds(t * reqs, reqs), :]
             passed = delta if t == 0 else passed + delta
-            sum_ref[tile, rows, :] = passed
-            driven = delta * cv_ref[tile, rows, :]
-            chosen = accepted == t + 4
+            rows_ref[tile, pl.ds(sum_at + t * reqs, reqs), :] = passed
+            driven = delta * cv_ref[tile, pl.ds(t * reqs, reqs), :]
+            chosen = accepted == t + late // reqs + 1
             pltpu.store(at_ref.at[tile], passed, mask=chosen)
-            totals = [None, None]
+            totals = [rows_ref[tile, pl.ds(y_at + t * reqs, reqs), :], None]
             for n in range(states):
                 at = t * states + n
                 added = driven * b_ref[at]
                 state[n] = added if t == 0 else jnp.exp2(delta * dec_ref[tile, n]) * state[n] + added
                 term = c_ref[at] * state[n]
                 totals[n % 2] = term if totals[n % 2] is None else totals[n % 2] + term
-                pltpu.store(ga_ref.at[tile, pl.ds(n * reqs, reqs), :], state[n], mask=chosen)
-            y_ref[tile, rows, :] = y_ref[tile, rows, :] + (totals[0] + totals[1])
-
-    for i in (0, 2, 3, 4):
-        copies[i].start()
-    for copy in copies:
-        copy.wait()
+                pltpu.store(
+                    rows_ref.at[tile, pl.ds(state_at + n * reqs, reqs), :], state[n], mask=chosen
+                )
+            rows_ref[tile, pl.ds(y_at + t * reqs, reqs), :] = totals[0] + totals[1]
+
+        @pl.when(tile % per == per - 1)
+        def _():
+            copy(tile // per).start()
+
+    for j in range(blocks):
+        copy(j).wait()
+
+
+def row_offsets(count, tokens):
+    return 0, count, 2 * count, 2 * count + tokens
 
 
 def before(q_place, j_place, projected, weights, accepted, late, states):
@@ -305,30 +327,28 @@
     vmem = pl.BlockSpec(memory_space=pltpu.VMEM)
     f32 = jnp.float32
     spots = count // reqs * states
-    results = [
-        ((tiles, count, LANES), f32),
-        ((tiles, tokens, LANES), f32),
-        ((tiles, count, LANES), f32),
-        ((tiles, reqs, LANES), f32),
-        ((tiles, states * reqs, LANES), f32),
-        ((spots, reqs, LANES), f32),
-        ((blocks, rank + 2 * states, BLOCK), jnp.bfloat16),
-        ((blocks, rank, BLOCK), jnp.bfloat16),
-        ((blocks, 24, BLOCK), f32),
-        ((blocks, late, BLOCK), f32),
-    ]
+    rows = (tiles, 2 * count + tokens + states * reqs, LANES)
     return pl.pallas_call(
         before_kernel,
-        out_shape=tuple(pltpu.HBM(shape, dtype) for shape, dtype in results),
+        out_shape=(
+            pltpu.HBM(rows, f32),
+            jax.ShapeDtypeStruct((tiles, reqs, LANES), f32),
+            jax.ShapeDtypeStruct((count, 2 * states), f32),
+            jax.ShapeDtypeStruct((blocks, rank + 2 * states, BLOCK), jnp.bfloat16),
+            jax.ShapeDtypeStruct((blocks, rank, BLOCK), jnp.bfloat16),
+            jax.ShapeDtypeStruct((blocks, 24, BLOCK), f32),
+            jax.ShapeDtypeStruct((blocks, late, BLOCK), f32),
+        ),
         in_specs=[smem, smem, vmem, vmem, vmem],
-        out_specs=(pl.BlockSpec(memory_space=pltpu.HBM),) * len(results),
-        scratch_shapes=[pltpu.VMEM(shape, dtype) for shape, dtype in results]
-        + [
+        out_specs=(pl.BlockSpec(memory_space=pltpu.HBM),) + (vmem,) * 6,
+        scratch_shapes=[
+            pltpu.VMEM(rows, f32),
             pltpu.VMEM((tiles, count, LANES), f32),
             pltpu.VMEM((tiles, count, LANES), f32),
             pltpu.VMEM((spots, reqs, LANES), f32),
+            pltpu.VMEM((spots, reqs, LANES), f32),
             pltpu.VMEM((tiles, states, reqs, LANES), f32),
-            pltpu.SemaphoreType.DMA((len(results),)),
+            pltpu.SemaphoreType.DMA((blocks,)),
         ],
         compiler_params=pltpu.CompilerParams(vmem_limit_bytes=24 << 20),
         cost_estimate=pl.CostEstimate(flops=200_000_000, bytes_accessed=8 << 20, transcendentals=4_000_000),
@@ -336,26 +356,32 @@
     )(q_place, j_place, projected, weights, accepted)
 
 
-def after_kernel(moved_ref, acc_ref, *refs):
-    given, (out_ref, ns_ref) = refs[:11], refs[11:13]
-    held, refs = refs[13:24], refs[24:]
-    new_ref, pick_ref, total_ref, dt_ref, cv_ref, b_ref, cl_ref, sems, ns_sem = refs
-    y_ref, sg_ref, sum_ref, at_ref, ga_ref, c_ref, xw_ref, sw_ref, vec_ref, x_ref, ow_ref = held
+def after_kernel(
+    moved_ref, acc_ref, at_ref, coef_ref, xw_ref, sw_ref, vec_ref, x_ref, rows_in, ow_in,
+    out_ref, ns_ref,
+    rows_ref, ow_ref, new_ref, pick_ref, total_ref, dt_ref, cv_ref, b_ref, c_ref, sems,
+):
     reqs, draft, _ = out_ref.shape
     blocks, late, _ = x_ref.shape
-    tiles, count, _ = y_ref.shape
-    states = ga_ref.shape[1] // reqs
+    tiles = rows_ref.shape[0]
+    tokens = reqs * draft
+    count = tokens - late
+    states = coef_ref.shape[1] // 2
     rank = sw_ref.shape[1]
     per = BLOCK // LANES
-
-    def state_copy(j):
-        return pltpu.make_async_copy(new_ref.at[j], ns_ref.at[:, pl.ds(j * BLOCK, BLOCK)], ns_sem.at[j])
-
-    copies = [pltpu.make_async_copy(given[i], held[i], sems.at[i]) for i in range(len(held))]
-    for i in (9, 8, 6, 7, 5, 2, 0, 1, 3, 4, 10):
-        copies[i].start()
-    for i in (9, 8, 6):
-        copies[i].wait()
+    y_at, sum_at, gate_at, state_at = row_offsets(count, tokens)
+
+    def copies(j):
+        some, cols = pl.ds(j * per, per), pl.ds(j * BLOCK, BLOCK)
+        return [
+            pltpu.make_async_copy(rows_in.at[some], rows_ref.at[some], sems.at[0, j]),
+            pltpu.make_async_copy(ow_in.at[cols, :], ow_ref.at[cols, :], sems.at[1, j]),
+            pltpu.make_async_copy(new_ref.at[j], ns_ref.at[:, cols], sems.at[2, j]),
+        ]
+
+    for j in range(blocks):
+        for copy in copies(j)[:2]:
+            copy.start()
     mixed = jnp.zeros((late, rank + 2 * states), jnp.float32)
     for j in range(blocks):
         history = [
@@ -365,20 +391,26 @@
         cv_ref[j] = conv.astype(jnp.float32)
         mixed = mixed + mixed_of(conv, xw_ref[j])
     rounded = mixed.astype(jnp.bfloat16)
-    copies[7].wait()
     for j in range(blocks):
         dt_ref[j] = softplus(
             jnp.dot(rounded[:, :rank], sw_ref[j], preferred_element_type=jnp.float32)
             + vec_ref[j, pl.ds(5, 1), :]
         )
     coefs = rounded[:, rank:].astype(jnp.float32)
-    for t in range(late // reqs):
-        spread(coefs[t * reqs : (t + 1) * reqs], t, b_ref, cl_ref)
+    for t in range(draft):
+        if t * reqs < late:
+            rows = coefs[t * reqs : (t + 1) * reqs]
+        else:
+            rows = coef_ref[pl.ds(t * reqs - late, reqs), :]
+        for n in range(states):
+            at = t * states + n
+            if t * reqs < late:
+                b_ref[at] = jnp.broadcast_to(rows[:, n : n + 1], (reqs, LANES))
+            c_ref[at] = jnp.broadcast_to(rows[:, states + n : states + n + 1], (reqs, LANES))
     accepted = acc_ref[...]
-    for i in (5, 2, 0, 1, 3, 4, 10):
-        copies[i].wait()
     for j in range(blocks):
         gated = []
+        copies(j)[0].wait()
         for k in range(per):
             tile = j * per + k
             lanes = pl.ds(k * LANES, LANES)
@@ -402,7 +434,7 @@
                 for n in range(states):
                     at = t * states + n
                     state[n] = jnp.exp2(delta * decay[n]) * state[n] + driven * b_ref[at]
-                    term = cl_ref[at] * state[n]
+                    term = c_ref[at] * state[n]
                     totals[n % 2] = term if totals[n % 2] is None else totals[n % 2] + term
                     pltpu.store(pick_ref.at[tile, pl.ds(n * reqs, reqs), :], state[n], mask=chosen)
                 outs.append(totals[0] + totals[1])
@@ -410,12 +442,13 @@
             passed = at_ref[tile]
             for n in range(states):
                 keep = pl.ds(n * reqs, reqs)
-                value = jnp.exp2(passed * decay[n]) * state[n] + ga_ref[tile, keep, :]
+                ahead = rows_ref[tile, pl.ds(state_at + n * reqs, reqs), :]
+                value = jnp.exp2(passed * decay[n]) * state[n] + ahead
                 pltpu.store(pick_ref.at[tile, keep, :], value, mask=beyond)
-            for t in range(count // reqs):
-                rows = pl.ds(t * reqs, reqs)
-                passed = sum_ref[tile, rows, :]
-                totals = [y_ref[tile, rows, :], None]
+            for t in range(late // reqs, draft):
+                row = t * reqs - late
+                passed = rows_ref[tile, pl.ds(sum_at + row, reqs), :]
+                totals = [rows_ref[tile, pl.ds(y_at + row, reqs), :], None]
                 for n in range(states):
                     term = c_ref[t * states + n] * (jnp.exp2(passed * decay[n]) * state[n])
                     totals[n % 2] = term if totals[n % 2] is None else totals[n % 2] + term
@@ -424,8 +457,9 @@
                 new_ref[j, pl.ds(r * states, states), lanes] = pick_ref[
                     tile, pl.ds(r, states, stride=reqs), :
                 ]
-            gated.append(jnp.concatenate(outs, axis=0) * sg_ref[tile])
-        state_copy(j).start()
+            gated.append(jnp.concatenate(outs, axis=0) * rows_ref[tile, pl.ds(gate_at, tokens), :])
+        copies(j)[2].start()
+        copies(j)[1].wait()
         added = jnp.dot(
             jnp.concatenate(gated, axis=1).astype(jnp.bfloat16),
             ow_ref[pl.ds(j * BLOCK, BLOCK), :],
@@ -439,47 +473,47 @@
             rows = total_ref[k, pl.ds(r, draft, stride=reqs), :]
             out_ref[r, :, pl.ds(k * LANES, LANES)] = rows.astype(jnp.bfloat16)
     for j in range(blocks):
-        state_copy(j).wait()
+        copies(j)[2].wait()
 
 
 def after(moved, accepted, early, out_weight):
+    rows, at, coefs, xw, sw, vec, x = early
     blocks, reqs, _ = moved.shape
-    tiles, tokens, _ = early[1].shape
-    states = early[4].shape[1] // reqs
-    late = early[9].shape[1]
+    tiles = at.shape[0]
+    states = coefs.shape[1] // 2
+    late = x.shape[1]
+    tokens = coefs.shape[0] + late
     draft = tokens // reqs
     inner, width = out_weight.shape
     vmem = pl.BlockSpec(memory_space=pltpu.VMEM)
     hbm = pl.BlockSpec(memory_space=pltpu.HBM)
     f32 = jnp.float32
-    spots = late // reqs * states
-    given = tuple(in_hbm(x) for x in (*early, out_weight))
     return pl.pallas_call(
         after_kernel,
         out_shape=(
             jax.ShapeDtypeStruct((reqs, draft, width), jnp.bfloat16),
             jax.ShapeDtypeStruct((reqs * states, inner), f32),
         ),
-        in_specs=[vmem] * 2 + [hbm] * len(given),
+        in_specs=[vmem] * 8 + [hbm] * 2,
         out_specs=(vmem, hbm),
-        scratch_shapes=[pltpu.VMEM(x.shape, x.dtype) for x in given]
-        + [
+        scratch_shapes=[
+            pltpu.VMEM(rows.shape, f32),
+            pltpu.VMEM(out_weight.shape, jnp.bfloat16),
             pltpu.VMEM((blocks, reqs * states, BLOCK), f32),
             pltpu.VMEM((tiles, states * reqs, LANES), f32),
             pltpu.VMEM((width // LANES, tokens, LANES), f32),
             pltpu.VMEM((blocks, late, BLOCK), f32),
             pltpu.VMEM((blocks, late, BLOCK), f32),
-            pltpu.VMEM((spots, reqs, LANES), f32),
-            pltpu.VMEM((spots, reqs, LANES), f32),
-            pltpu.SemaphoreType.DMA((len(given),)),
-            pltpu.SemaphoreType.DMA((blocks,)),
+            pltpu.VMEM((late // reqs * states, reqs, LANES), f32),
+            pltpu.VMEM((draft * states, reqs, LANES), f32),
+            pltpu.SemaphoreType.DMA((3, blocks)),
         ],
         compiler_params=pltpu.CompilerParams(vmem_limit_bytes=24 << 20),
         cost_estimate=pl.CostEstimate(
             flops=2 * tokens * inner * width, bytes_accessed=12 << 20, transcendentals=4_000_000
         ),
         name="after_states",
-    )(moved, accepted, *given)
+    )(moved, accepted, at, coefs, xw, sw, vec, x, in_hbm(rows), in_hbm(out_weight))
 
 
 def exchange(values):
@@ -549,9 +583,10 @@
     blocks = inner_width // channels
     tokens = draft_len * local_reqs
 
-    arrived = exchange(
-        pack(old_states, old_edges, blocks).reshape(all_reqs, (state_size + span) * channels)
+    packed, share = prepared(
+        old_states, old_edges, x_weight, step_weight, conv_weight, conv_bias, step_bias, skip_gain, log_decay
     )
+    arrived = exchange(packed.reshape(all_reqs, (state_size + span) * channels))
     old_slot = jnp.arange(all_reqs, dtype=jnp.int32)
     chosen = (anchor[:, None] == old_slot[None, :]) & (fresh_flag[:, None] == 0)
     masks = jnp.stack([chosen] + [chosen & (span - e <= request_ages)[:, None] for e in range(span)])
@@ -561,10 +596,11 @@
     masks, projected = lax.optimization_barrier((masks.astype(jnp.bfloat16), projected))
     moved = exchange(select(masks, arrived))
 
-    share = weight_share(
-        groups, x_weight, step_weight, conv_weight, conv_bias, step_bias, skip_gain, log_decay
+    top = blocks // 2
+    weights = jnp.concatenate(
+        [share[None]] + [moved_by(share[None], "req", bits) for bits in (top, top // 2, top + top // 2)]
     )
-    weights = doubled(doubled(share[None], "req")[None], "grp")
+    weights = doubled(doubled(weights, "req", top // 4)[None], "grp", groups // 2)
     q_place, j_place = places("grp"), places("req")
     if channels != BLOCK:
         moved = moved.reshape(blocks, local_reqs, state_size + span, channels).transpose(1, 2, 0, 3)

time: 63.3 us -> 60.4 us (0.954)
  Pallas kernels: 22.1 us -> 18.4 us
  waiting for transfers between devices: 13.4 us -> 14.8 us
    all_to_all x2, waiting for transfers between devices: 2.4 us -> 4.6 us  [exchange(): lax.all_to_all(values, 'req', split_axis=0, concat_axis=0, tiled=True)]
    pallas_call x3 -> x2, Pallas kernels: 11.2 us -> 9.22 us  [the longest x1 6.54 us: before(): pl.pallas_call(before_kernel, out_shape=(pltpu.HBM(rows, f32), jax.ShapeD...]
    pallas_call x1, Pallas kernels: 9.75 us -> 8.09 us  [after(): pl.pallas_call(after_kernel, out_shape=(jax.ShapeDtypeStruct((reqs, draft...]
    ppermute x5 -> x6, waiting for transfers between devices: 11 us -> 10.2 us  [moved_by(): lax.ppermute(values, axis, [(i, i ^ bits) for i in range(lax.axis_size(ax...]
    ppermute x5 -> x6, starting transfers between devices: 9.57 us -> 9.48 us  [moved_by(): lax.ppermute(values, axis, [(i, i ^ bits) for i in range(lax.axis_size(ax...]
    concatenate x4 -> x3, other arithmetic: 1.35 us -> 1.35 us  [the longest x2 1.32 us: doubled(): values = jnp.concatenate([values, moved_by(values, axis, bit)], axis=0)]
  transfers between devices with their start and end apart: 7 -> 8, of which waited for: 4 -> 5; matrix products, arithmetic and copies ran while one was open for 11% -> 11% of each run, Pallas kernels for 17% -> 13%
where the time goes in v4:
time: 60.4 us; the launch traced here: 60 us
  starting transfers between devices  19.1 us (32%)
  Pallas kernels  18.4 us (30%)
  waiting for transfers between devices  14.8 us (25%)
  matrix products  4.8 us (8%)
  other arithmetic  1.73 us (3%)
  between operations  0.85 us (1%)
    ppermute x6, waiting for transfers between devices, moved_by(): lax.ppermute(values, axis, [(i, i ^ bits) for i in range(lax.axis_size(ax...  10.2 us
    all_to_all x2, starting transfers between devices, exchange(): lax.all_to_all(values, 'req', split_axis=0, concat_axis=0, tiled=True)  9.63 us
    ppermute x6, starting transfers between devices, moved_by(): lax.ppermute(values, axis, [(i, i ^ bits) for i in range(lax.axis_size(ax...  9.48 us
    pallas_call x1, Pallas kernels, after(): pl.pallas_call(after_kernel, out_shape=(jax.ShapeDtypeStruct((reqs, draft...  8.09 us
    pallas_call x1, Pallas kernels, before(): pl.pallas_call(before_kernel, out_shape=(pltpu.HBM(rows, f32), jax.ShapeD...  6.54 us
    dot_general x1, matrix products, on_device(): jnp.dot(normed, in_weight, preferred_element_type=jnp.float32)  4.8 us
    all_to_all x2, waiting for transfers between devices, exchange(): lax.all_to_all(values, 'req', split_axis=0, concat_axis=0, tiled=True)  4.6 us
    pallas_call x1, Pallas kernels, prepared(): pl.pallas_call(send_kernel, out_shape=(pltpu.HBM((blocks, slots, (states...  2.68 us
  transfers between devices with their start and end apart: 8, of which 5 were waited for; matrix products, arithmetic and copies ran while one was open for 11% of the time, Pallas kernels for 13%

profile of v4, /device:TPU:0, one launch (start us, length us, event | category | flops | bytes accessed | tf_op | source)
XLA Modules:
  0.0 60.0 jit_solution(13801099001281657891)
XLA Ops:
  0.7 2.7 %send_states.1 = (bf16[8,8,4864]{2,1,0:T(8,128)(2,1)}, bf16[88,256]{1,0:T(8,128)(2,1)S(1)}) custom-call(s32[1]{0:T(128)} %bitcast.3.group_ref, f32[128,2048]{1,0:T(8,128)} %bitcast.35, bf16[3,8,2048]{2,1,0:T(8,128)(2,1)} %bitcast.36, bf16[160,256]{1,0:T(8,128)(2,1)} %bitcast.37, bf16[128,256]{1,0:T(8,128)(2,1)} %sw_ref.1, f32[4,256]{1,0:T(4,128)} %cw_ref.1, ...), custom_call_target="tpu_custom_call" | custom-call | tf_op jit(solution)/shard_map/send_states/pallas_call | solution.py:114
  3.3 5.1 %collective-permute-start.2 = (bf16[1,88,256]{2,1,0:T(8,128)(2,1)S(1)}, bf16[1,88,256]{2,1,0:T(8,128)(2,1)S(1)}, u32[]{:S(2)}, u32[]{:S(2)}) collective-permute-start(bf16[1,88,256]{2,1,0:T(8,128)(2,1)S(1)} %bitcast.28), channel_id=1, source_target_pairs={{0,24},{4,28},{8,16},{12,20},{16,8},{20,12},{24,0},{28,4},{1,25},{... | collective-permute-start | bytes 135176 | tf_op jit(solution)/shard_map/ppermute | solution.py:161
  8.5 0.6 %collective-permute-start = (bf16[1,88,256]{2,1,0:T(8,128)(2,1)S(1)}, bf16[1,88,256]{2,1,0:T(8,128)(2,1)S(1)}, u32[]{:S(2)}, u32[]{:S(2)}) collective-permute-start(bf16[1,88,256]{2,1,0:T(8,128)(2,1)S(1)} %bitcast.30), channel_id=1, source_target_pairs={{0,16},{4,20},{8,24},{12,28},{16,0},{20,4},{24,8},{28,12},{1,17},{... | collective-permute-start | bytes 135176 | tf_op jit(solution)/shard_map/ppermute | solution.py:161
  9.1 5.9 %all-to-all-start = ((bf16[8,8,4864]{2,1,0:T(8,128)(2,1)}), bf16[8,8,4864]{2,1,0:T(8,128)(2,1)S(1)}, u32[]{:S(2)}, u32[]{:S(2)}) async-start(bf16[8,8,4864]{2,1,0:T(8,128)(2,1)} %get-tuple-element.16), calls=%async_computation | async-start | bytes 1245184 | tf_op jit(solution)/shard_map/all_to_all | solution.py:520
  15.1 0.2 fusion.3
  15.3 0.1 rsqrt.12
  15.4 4.8 %convolution_convert_fusion.proj_ref = bf16[128,4096]{1,0:T(8,128)(2,1)S(1)} fusion(bf16[1024,4096]{1,0:T(8,128)(2,1)} %param.19, f32[1024]{0:T(1024)S(1)} %copy-done.1, f32[128]{0:T(128)S(1)} %rsqrt.12, bf16[8,16,1024]{2,1,0:T(8,128)(2,1)S(1)} %copy-done), kind=kOutput, calls=%fused_computation | convolution fusion | flops 1074790400 | bytes 9703936 | tf_op jit(solution)/shard_map/dot_general | solution.py:595
  20.4 2.1 %collective-permute-start.3 = (bf16[4,88,256]{2,1,0:T(8,128)(2,1)S(1)}, bf16[4,88,256]{2,1,0:T(8,128)(2,1)S(1)}, u32[]{:S(2)}, u32[]{:S(2)}) collective-permute-start(bf16[4,88,256]{2,1,0:T(8,128)(2,1)S(1)} %pad_maximum_fusion.2), channel_id=1, source_target_pairs={{0,4},{4,0},{8,12},{12,8},{16,20},{20,16},{24,28},{28,24},{1,5},{5... | collective-permute-start | bytes 540680 | tf_op jit(solution)/shard_map/ppermute | solution.py:161
  22.5 6.2 %collective-permute-done.3 = bf16[4,88,256]{2,1,0:T(8,128)(2,1)S(1)} collective-permute-done((bf16[4,88,256]{2,1,0:T(8,128)(2,1)S(1)}, bf16[4,88,256]{2,1,0:T(8,128)(2,1)S(1)}, u32[]{:S(2)}, u32[]{:S(2)}) %collective-permute-start.3) | collective-permute-done | bytes 180256 | tf_op jit(solution)/shard_map/ppermute | solution.py:161
  28.7 1.6 %collective-permute-start.4 = (bf16[1,8,88,256]{3,2,1,0:T(8,128)(2,1)S(1)}, bf16[1,8,88,256]{3,2,1,0:T(8,128)(2,1)S(1)}, u32[]{:S(2)}, u32[]{:S(2)}) collective-permute-start(bf16[1,8,88,256]{3,2,1,0:T(8,128)(2,1)S(1)} %bitcast.32), channel_id=1, source_target_pairs={{0,2},{1,3},{2,0},{3,1},{4,6},{5,7},{6,4},{7,5},{8,10},{9,11},{10,... | collective-permute-start | bytes 1081352 | tf_op jit(solution)/shard_map/ppermute | solution.py:161
  30.2 0.1 fusion.8
  30.4 0.5 all-to-all-done
  30.8 1.1 %select_slots.1 = bf16[64,4864]{1,0:T(8,128)(2,1)} custom-call(bf16[4,64,64]{2,1,0:T(8,128)(2,1)S(1)} %add_convert_fusion.mask_ref, bf16[64,4864]{1,0:T(8,128)(2,1)S(1)} %bitcast.27), custom_call_target="tpu_custom_call" | custom-call | tf_op jit(solution)/shard_map/select_slots/pallas_call | solution.py:536
  32.0 3.7 %all-to-all-start.1 = ((bf16[8,8,4864]{2,1,0:T(8,128)(2,1)}), bf16[8,8,4864]{2,1,0:T(8,128)(2,1)S(1)}, u32[]{:S(2)}, u32[]{:S(2)}) async-start(bf16[8,8,4864]{2,1,0:T(8,128)(2,1)} %bitcast.11), calls=%async_computation.1 | async-start | bytes 1245184 | tf_op jit(solution)/shard_map/all_to_all | solution.py:520
  35.7 1.8 %collective-permute-done.4 = bf16[1,8,88,256]{3,2,1,0:T(8,128)(2,1)S(1)} collective-permute-done((bf16[1,8,88,256]{3,2,1,0:T(8,128)(2,1)S(1)}, bf16[1,8,88,256]{3,2,1,0:T(8,128)(2,1)S(1)}, u32[]{:S(2)}, u32[]{:S(2)}) %collective-permute-start.4) | collective-permute-done | bytes 360480 | tf_op jit(solution)/shard_map/ppermute | solution.py:161
  37.4 0.1 pad_maximum_fusion.1
  37.5 0.1 collective-permute-start.5
  37.6 0.1 dynamic_slice.3
  37.7 2.2 %collective-permute-done.5 = bf16[2,8,88,256]{3,2,1,0:T(8,128)(2,1)} collective-permute-done((bf16[2,8,88,256]{3,2,1,0:T(8,128)(2,1)S(1)}, bf16[2,8,88,256]{3,2,1,0:T(8,128)(2,1)}, u32[]{:S(2)}, u32[]{:S(2)}) %collective-permute-start.5) | collective-permute-done | bytes 720928 | tf_op jit(solution)/shard_map/ppermute | solution.py:161
  39.9 1.3 %pad_maximum_fusion.w_ref = bf16[4,8,88,256]{3,2,1,0:T(8,128)(2,1)S(1)} fusion(bf16[2,8,88,256]{3,2,1,0:T(8,128)(2,1)} %collective-permute-done.5, bf16[1,8,88,256]{3,2,1,0:T(8,128)(2,1)S(1)} %collective-permute-done.4, bf16[1,8,88,256]{3,2,1,0:T(8,128)(2,1)S(1)} %bitcast.34), kind=kLoop, calls=%fused_computation.1 | loop fusion | flops 1441792 | bytes 2883584 | tf_op jit(solution)/shard_map/concatenate | solution.py:166
  41.2 0.1 broadcast_in_dim.57.acc_ref
  41.2 6.5 %before_states.1 = (f32[16,464,128]{2,1,0:T(8,128)}, f32[16,8,128]{2,1,0:T(8,128)S(1)}, f32[104,32]{1,0:T(8,128)S(1)}, bf16[8,160,256]{2,1,0:T(8,128)(2,1)S(1)},...) custom-call(s32[4]{0:T(128)S(1)} %fusion.9.q_ref, s32[8]{0:T(128)S(1)} %fusion.11.j_ref, ...), custom_call_target="tpu_custom_call" | custom-call | flops 200000000 | bytes 8388608 | tf_op jit(solution)/shard_map/before_states/pallas_call | solution.py:331
  47.8 4.1 %all-to-all-done.1.moved_ref = bf16[8,8,4864]{2,1,0:T(8,128)(2,1)S(1)} async-done(((bf16[8,8,4864]{2,1,0:T(8,128)(2,1)}), bf16[8,8,4864]{2,1,0:T(8,128)(2,1)S(1)}, u32[]{:S(2)}, u32[]{:S(2)}) %all-to-all-start.1) | async-done | bytes 622624 | tf_op jit(solution)/shard_map/all_to_all | solution.py:520
  51.9 8.1 %after_states.1 = (bf16[8,16,1024]{2,1,0:T(8,128)(2,1)}, f32[128,2048]{1,0:T(8,128)}) custom-call(bf16[8,8,4864]{2,1,0:T(8,128)(2,1)S(1)} %all-to-all-done.1.moved_ref, s32[8,128]{1,0:T(8,128)S(1)} %broadcast_in_dim.57.acc_ref, f32[16,8,128]{2,1,0:T(8,128)S(1)} %get-tuple-element.19.at_ref, f32[104,32]{1,0:T(8,128)S(1)} %get-tuple-element.20.coef_ref, ...), custom_call_target="tpu_custom_call" | custom-call | flops 536870912 | bytes 12582912 | tf_op jit(solution)/shard_map/after_states/pallas_call | solution.py:491
  (27 shorter events, 0.2 us)
Async XLA Ops:
  0.6 14.4 %copy-start = (bf16[8,16,1024]{2,1,0:T(8,128)(2,1)S(1)}, bf16[8,16,1024]{2,1,0:T(8,128)(2,1)}, u32[]{:S(2)}) copy-start(bf16[8,16,1024]{2,1,0:T(8,128)(2,1)} %param.17) | copy-start | bytes 786436
  0.6 14.8 %copy-start.1 = (f32[1024]{0:T(1024)S(1)}, f32[1024]{0:T(1024)}, u32[]{:S(2)}) copy-start(f32[1024]{0:T(1024)} %param.18) | copy-start | bytes 12292
  3.3 16.9 %collective-permute-start.2 = (bf16[1,88,256]{2,1,0:T(8,128)(2,1)S(1)}, bf16[1,88,256]{2,1,0:T(8,128)(2,1)S(1)}, u32[]{:S(2)}, u32[]{:S(2)}) collective-permute-start(bf16[1,88,256]{2,1,0:T(8,128)(2,1)S(1)} %bitcast.28), channel_id=1, source_target_pairs={{0,24},{4,28},{8,16},{12,20},{16,8},{20,12},{24,0},{28,4},{1,25},{... | collective-permute-start | bytes 135176 | tf_op jit(solution)/shard_map/ppermute | solution.py:161
  8.5 11.8 %collective-permute-start.1 = (bf16[1,88,256]{2,1,0:T(8,128)(2,1)S(1)}, bf16[1,88,256]{2,1,0:T(8,128)(2,1)S(1)}, u32[]{:S(2)}, u32[]{:S(2)}) collective-permute-start(bf16[1,88,256]{2,1,0:T(8,128)(2,1)S(1)} %bitcast.29), channel_id=1, source_target_pairs={{0,8},{4,12},{8,0},{12,4},{16,24},{20,28},{24,16},{28,20},{1,9},{5... | collective-permute-start | bytes 135176 | tf_op jit(solution)/shard_map/ppermute | solution.py:161
  8.5 11.8 %collective-permute-start = (bf16[1,88,256]{2,1,0:T(8,128)(2,1)S(1)}, bf16[1,88,256]{2,1,0:T(8,128)(2,1)S(1)}, u32[]{:S(2)}, u32[]{:S(2)}) collective-permute-start(bf16[1,88,256]{2,1,0:T(8,128)(2,1)S(1)} %bitcast.30), channel_id=1, source_target_pairs={{0,16},{4,20},{8,24},{12,28},{16,0},{20,4},{24,8},{28,12},{1,17},{... | collective-permute-start | bytes 135176 | tf_op jit(solution)/shard_map/ppermute | solution.py:161
  9.1 21.7 %all-to-all-start = ((bf16[8,8,4864]{2,1,0:T(8,128)(2,1)}), bf16[8,8,4864]{2,1,0:T(8,128)(2,1)S(1)}, u32[]{:S(2)}, u32[]{:S(2)}) async-start(bf16[8,8,4864]{2,1,0:T(8,128)(2,1)} %get-tuple-element.16), calls=%async_computation | async-start | bytes 1245184 | tf_op jit(solution)/shard_map/all_to_all | solution.py:520
  15.4 4.9 %copy-start.3 = (s32[64]{0:T(128)S(1)}, s32[64]{0:T(128)}, u32[]{:S(2)}) copy-start(s32[64]{0:T(128)} %param.33) | copy-start | bytes 772
  15.4 4.8 %copy-start.4 = (s32[64]{0:T(128)S(1)}, s32[64]{0:T(128)}, u32[]{:S(2)}) copy-start(s32[64]{0:T(128)} %param.31) | copy-start | bytes 772
  15.4 14.8 %copy-start.2 = (s32[64]{0:T(128)S(1)}, s32[64]{0:T(128)}, u32[]{:S(2)}) copy-start(s32[64]{0:T(128)} %param.30) | copy-start | bytes 772
  20.4 8.3 %collective-permute-start.3 = (bf16[4,88,256]{2,1,0:T(8,128)(2,1)S(1)}, bf16[4,88,256]{2,1,0:T(8,128)(2,1)S(1)}, u32[]{:S(2)}, u32[]{:S(2)}) collective-permute-start(bf16[4,88,256]{2,1,0:T(8,128)(2,1)S(1)} %pad_maximum_fusion.2), channel_id=1, source_target_pairs={{0,4},{4,0},{8,12},{12,8},{16,20},{20,16},{24,28},{28,24},{1,5},{5... | collective-permute-start | bytes 540680 | tf_op jit(solution)/shard_map/ppermute | solution.py:161
  28.6 9.0 %copy-start.5 = (s32[64]{0:T(128)S(1)}, s32[64]{0:T(128)}, u32[]{:S(2)}) copy-start(s32[64]{0:T(128)} %param.32) | copy-start | bytes 772
  28.7 8.8 %collective-permute-start.4 = (bf16[1,8,88,256]{3,2,1,0:T(8,128)(2,1)S(1)}, bf16[1,8,88,256]{3,2,1,0:T(8,128)(2,1)S(1)}, u32[]{:S(2)}, u32[]{:S(2)}) collective-permute-start(bf16[1,8,88,256]{3,2,1,0:T(8,128)(2,1)S(1)} %bitcast.32), channel_id=1, source_target_pairs={{0,2},{1,3},{2,0},{3,1},{4,6},{5,7},{6,4},{7,5},{8,10},{9,11},{10,... | collective-permute-start | bytes 1081352 | tf_op jit(solution)/shard_map/ppermute | solution.py:161
  32.0 19.9 %all-to-all-start.1 = ((bf16[8,8,4864]{2,1,0:T(8,128)(2,1)}), bf16[8,8,4864]{2,1,0:T(8,128)(2,1)S(1)}, u32[]{:S(2)}, u32[]{:S(2)}) async-start(bf16[8,8,4864]{2,1,0:T(8,128)(2,1)} %bitcast.11), calls=%async_computation.1 | async-start | bytes 1245184 | tf_op jit(solution)/shard_map/all_to_all | solution.py:520
  37.5 2.4 %collective-permute-start.5 = (bf16[2,8,88,256]{3,2,1,0:T(8,128)(2,1)S(1)}, bf16[2,8,88,256]{3,2,1,0:T(8,128)(2,1)}, u32[]{:S(2)}, u32[]{:S(2)}) collective-permute-start(bf16[2,8,88,256]{3,2,1,0:T(8,128)(2,1)S(1)} %pad_maximum_fusion.1), channel_id=1, source_target_pairs={{0,1},{1,0},{2,3},{3,2},{4,5},{5,4},{6,7},{7,6},{8,9},{9,8},{10,11... | collective-permute-start | bytes 2162696 | tf_op jit(solution)/shard_map/ppermute | solution.py:161

commit v5 on v4

--- a/solution.py
+++ b/solution.py
@@ -12,6 +12,7 @@
 LANES = 128
 BLOCK = 256
 SHARE = 88
+AHEAD = 6
 
 
 def rms_normed(values_in, norm_gain):
@@ -161,8 +162,8 @@
     return lax.ppermute(values, axis, [(i, i ^ bits) for i in range(lax.axis_size(axis))])
 
 
-def doubled(values, axis, bit):
-    while bit:
+def doubled(values, axis, bit, stop=0):
+    while bit > stop:
         values = jnp.concatenate([values, moved_by(values, axis, bit)], axis=0)
         bit //= 2
     return values
@@ -179,17 +180,22 @@
     return place
 
 
-def block_weights(w_ref, q_ref, j_ref, j):
+def block_weights(near_ref, far_ref, q_ref, j_ref, j):
     at = j_ref[j]
-    quarters = [w_ref.at[q_ref[q], at] for q in range(4)]
     f32 = jnp.float32
+
+    def rows(q, start, size):
+        place = q_ref[q]
+        some = pl.ds(start, size)
+        near = near_ref[place % 2, at, some, :].astype(f32)
+        return jnp.where(place < 2, near, far_ref[place % 2, at, some, :].astype(f32))
+
     xw = jnp.concatenate(
-        [w[pl.ds(0, 32), :].astype(f32) for w in quarters] + [w[pl.ds(32, 8), :].astype(f32) for w in quarters],
-        axis=0,
+        [rows(q, 0, 32) for q in range(4)] + [rows(q, 32, 8) for q in range(4)], axis=0
     ).astype(jnp.bfloat16)
-    sw = jnp.concatenate([w[pl.ds(48, 32), :] for w in quarters], axis=0)
-    first = [w[pl.ds(40, 8), :].astype(f32) for w in quarters]
-    second = [w[pl.ds(80, 8), :].astype(f32) for w in quarters]
+    sw = jnp.concatenate([rows(q, 48, 32) for q in range(4)], axis=0).astype(jnp.bfloat16)
+    first = [rows(q, 40, 8) for q in range(4)]
+    second = [rows(q, 80, 8) for q in range(4)]
     high = jnp.concatenate([first[0], second[0], first[1]], axis=0)
     low = jnp.concatenate([first[2], second[2], first[3]], axis=0)
     return xw, sw, high + low
@@ -224,11 +230,11 @@
 
 
 def before_kernel(
-    q_ref, j_ref, proj_ref, w_ref, acc_ref,
+    q_ref, j_ref, proj_ref, near_ref, far_ref, acc_ref,
     rows_out, at_ref, coef_ref, xw_ref, sw_ref, vec_ref, x_ref,
     rows_ref, dt_ref, cv_ref, b_ref, c_ref, dec_ref, sems,
 ):
-    blocks = w_ref.shape[1]
+    blocks = near_ref.shape[1]
     tiles, count, _ = dt_ref.shape
     tokens = proj_ref.shape[0]
     late = tokens - count
@@ -245,7 +251,7 @@
 
     mixed = jnp.zeros((count, rank + 2 * states), jnp.float32)
     for j in range(blocks):
-        xw, sw, vec = block_weights(w_ref, q_ref, j_ref, j)
+        xw, sw, vec = block_weights(near_ref, far_ref, q_ref, j_ref, j)
         values = proj_ref[:, pl.ds(j * BLOCK, BLOCK)].astype(jnp.float32)
         conv = convolved(values, vec, count)
         mixed = mixed + mixed_of(conv, xw)
@@ -318,7 +324,7 @@
 
 def before(q_place, j_place, projected, weights, accepted, late, states):
     tokens = projected.shape[0]
-    blocks = weights.shape[1]
+    blocks = weights[0].shape[1]
     tiles = blocks * (BLOCK // LANES)
     count = tokens - late
     reqs = accepted.shape[0]
@@ -339,7 +345,7 @@
             jax.ShapeDtypeStruct((blocks, 24, BLOCK), f32),
             jax.ShapeDtypeStruct((blocks, late, BLOCK), f32),
         ),
-        in_specs=[smem, smem, vmem, vmem, vmem],
+        in_specs=[smem, smem, vmem, vmem, vmem, vmem],
         out_specs=(pl.BlockSpec(memory_space=pltpu.HBM),) + (vmem,) * 6,
         scratch_shapes=[
             pltpu.VMEM(rows, f32),
@@ -353,13 +359,13 @@
         compiler_params=pltpu.CompilerParams(vmem_limit_bytes=24 << 20),
         cost_estimate=pl.CostEstimate(flops=200_000_000, bytes_accessed=8 << 20, transcendentals=4_000_000),
         name="before_states",
-    )(q_place, j_place, projected, weights, accepted)
+    )(q_place, j_place, projected, *weights, accepted)
 
 
 def after_kernel(
     moved_ref, acc_ref, at_ref, coef_ref, xw_ref, sw_ref, vec_ref, x_ref, rows_in, ow_in,
     out_ref, ns_ref,
-    rows_ref, ow_ref, new_ref, pick_ref, total_ref, dt_ref, cv_ref, b_ref, c_ref, sems,
+    rows_ref, ow_ref, new_ref, pick_ref, total_ref, dt_ref, cv_ref, b_ref, c_ref, done_ref, sems, out_sem,
 ):
     reqs, draft, _ = out_ref.shape
     blocks, late, _ = x_ref.shape
@@ -379,9 +385,13 @@
             pltpu.make_async_copy(new_ref.at[j], ns_ref.at[:, cols], sems.at[2, j]),
         ]
 
-    for j in range(blocks):
-        for copy in copies(j)[:2]:
-            copy.start()
+    def result(k):
+        cols = pl.ds(k * LANES, LANES)
+        return pltpu.make_async_copy(done_ref.at[k], out_ref.at[:, :, cols], out_sem.at[k])
+
+    queue = [copies(j)[i] for j in range(blocks) for i in range(2)]
+    for copy in queue[:AHEAD]:
+        copy.start()
     mixed = jnp.zeros((late, rank + 2 * states), jnp.float32)
     for j in range(blocks):
         history = [
@@ -408,9 +418,24 @@
                 b_ref[at] = jnp.broadcast_to(rows[:, n : n + 1], (reqs, LANES))
             c_ref[at] = jnp.broadcast_to(rows[:, states + n : states + n + 1], (reqs, LANES))
     accepted = acc_ref[...]
+    def project(j, gated):
+        added = jnp.dot(
+            gated, ow_ref[pl.ds(j * BLOCK, BLOCK), :], preferred_element_type=jnp.float32
+        )
+        for k in range(total_ref.shape[0]):
+            part = added[:, k * LANES : (k + 1) * LANES]
+            total_ref[k] = part if j == 0 else total_ref[k] + part
+
+    ready = None
     for j in range(blocks):
+        for at in (2 * j - 1, 2 * j):
+            if at >= 0:
+                queue[at].wait()
+                if at + AHEAD < len(queue):
+                    queue[at + AHEAD].start()
+        if ready is not None:
+            project(j - 1, ready)
         gated = []
-        copies(j)[0].wait()
         for k in range(per):
             tile = j * per + k
             lanes = pl.ds(k * LANES, LANES)
@@ -459,21 +484,18 @@
                 ]
             gated.append(jnp.concatenate(outs, axis=0) * rows_ref[tile, pl.ds(gate_at, tokens), :])
         copies(j)[2].start()
-        copies(j)[1].wait()
-        added = jnp.dot(
-            jnp.concatenate(gated, axis=1).astype(jnp.bfloat16),
-            ow_ref[pl.ds(j * BLOCK, BLOCK), :],
-            preferred_element_type=jnp.float32,
-        )
-        for k in range(total_ref.shape[0]):
-            part = added[:, k * LANES : (k + 1) * LANES]
-            total_ref[k] = part if j == 0 else total_ref[k] + part
+        ready = jnp.concatenate(gated, axis=1).astype(jnp.bfloat16)
+    queue[-1].wait()
+    project(blocks - 1, ready)
     for k in range(total_ref.shape[0]):
         for r in range(reqs):
             rows = total_ref[k, pl.ds(r, draft, stride=reqs), :]
-            out_ref[r, :, pl.ds(k * LANES, LANES)] = rows.astype(jnp.bfloat16)
+            done_ref[k, r] = rows.astype(jnp.bfloat16)
+        result(k).start()
     for j in range(blocks):
         copies(j)[2].wait()
+    for k in range(total_ref.shape[0]):
+        result(k).wait()
 
 
 def after(moved, accepted, early, out_weight):
@@ -495,7 +517,7 @@
             jax.ShapeDtypeStruct((reqs * states, inner), f32),
         ),
         in_specs=[vmem] * 8 + [hbm] * 2,
-        out_specs=(vmem, hbm),
+        out_specs=(hbm, hbm),
         scratch_shapes=[
             pltpu.VMEM(rows.shape, f32),
             pltpu.VMEM(out_weight.shape, jnp.bfloat16),
@@ -506,7 +528,9 @@
             pltpu.VMEM((blocks, late, BLOCK), f32),
             pltpu.VMEM((late // reqs * states, reqs, LANES), f32),
             pltpu.VMEM((draft * states, reqs, LANES), f32),
+            pltpu.VMEM((width // LANES, reqs, draft, LANES), jnp.bfloat16),
             pltpu.SemaphoreType.DMA((3, blocks)),
+            pltpu.SemaphoreType.DMA((width // LANES,)),
         ],
         compiler_params=pltpu.CompilerParams(vmem_limit_bytes=24 << 20),
         cost_estimate=pl.CostEstimate(
@@ -596,17 +620,16 @@
     masks, projected = lax.optimization_barrier((masks.astype(jnp.bfloat16), projected))
     moved = exchange(select(masks, arrived))
 
-    top = blocks // 2
-    weights = jnp.concatenate(
-        [share[None]] + [moved_by(share[None], "req", bits) for bits in (top, top // 2, top + top // 2)]
-    )
-    weights = doubled(doubled(weights, "req", top // 4)[None], "grp", groups // 2)
+    near = doubled(doubled(share[None], "req", blocks // 2)[None], "grp", groups // 2, 1)
+    weights = (near, moved_by(near, "grp", 1))
     q_place, j_place = places("grp"), places("req")
     if channels != BLOCK:
         moved = moved.reshape(blocks, local_reqs, state_size + span, channels).transpose(1, 2, 0, 3)
         moved = moved.reshape(local_reqs, state_size + span, -1, BLOCK).transpose(2, 0, 1, 3)
-        weights = jnp.take(weights, j_place, axis=1).swapaxes(1, 2)
-        weights = weights.reshape(groups, SHARE, -1, BLOCK).swapaxes(1, 2)
+        weights = tuple(
+            jnp.take(w, j_place, axis=1).swapaxes(1, 2).reshape(-1, SHARE, inner_width // BLOCK, BLOCK).swapaxes(1, 2)
+            for w in weights
+        )
         j_place = jnp.arange(inner_width // BLOCK, dtype=jnp.int32)
     moved = moved.reshape(inner_width // BLOCK, local_reqs, (state_size + span) * BLOCK)
 

time: 60.4 us -> 72.6 us (1.20)
  waiting for transfers between devices: 14.8 us -> 23.3 us
  local copies, waits for them, and re-layouts: 0.3 us -> 5.49 us
    ppermute x6 -> x5, waiting for transfers between devices: 10.2 us -> 20.7 us  [moved_by(): lax.ppermute(values, axis, [(i, i ^ bits) for i in range(lax.axis_size(ax...]
    unnamed x16 -> x20, local copies, waits for them, and re-layouts: 0.05 us -> 5.25 us
    ppermute x6 -> x5, starting transfers between devices: 9.48 us -> 6.18 us  [moved_by(): lax.ppermute(values, axis, [(i, i ^ bits) for i in range(lax.axis_size(ax...]
    all_to_all x2, starting transfers between devices: 9.63 us -> 12.3 us  [exchange(): lax.all_to_all(values, 'req', split_axis=0, concat_axis=0, tiled=True)]
    all_to_all x2, waiting for transfers between devices: 4.6 us -> 2.59 us  [exchange(): lax.all_to_all(values, 'req', split_axis=0, concat_axis=0, tiled=True)]
    concatenate x2 -> x3, other arithmetic: 1.32 us -> 0.1 us  [doubled(): values = jnp.concatenate([values, moved_by(values, axis, bit)], axis=0)]
    pallas_call x1, Pallas kernels: 8.09 us -> 7.14 us  [after(): pl.pallas_call(after_kernel, out_shape=(jax.ShapeDtypeStruct((reqs, draft...]
    reduce_sum x1, other arithmetic: 0.22 us -> 1.17 us  [rms_normed(): factor = lax.rsqrt(jnp.mean(values * values, axis=-1, keepdims=True) + EPS)]
  transfers between devices with their start and end apart: 8 -> 7, of which waited for: 5 -> 5; matrix products, arithmetic and copies ran while one was open for 11% -> 9% of each run, Pallas kernels for 13% -> 11%
where the time goes in v5:
time: 72.6 us; the launch traced here: 72.1 us
  waiting for transfers between devices  23.3 us (32%)
  starting transfers between devices  18.5 us (25%)
  Pallas kernels  17.7 us (24%)
  local copies, waits for them, and re-layouts  5.49 us (8%)
  matrix products  4.91 us (7%)
  other arithmetic  1.47 us (2%)
  between operations  0.8 us (1%)
    ppermute x5, waiting for transfers between devices, moved_by(): lax.ppermute(values, axis, [(i, i ^ bits) for i in range(lax.axis_size(ax...  20.7 us
    all_to_all x2, starting transfers between devices, exchange(): lax.all_to_all(values, 'req', split_axis=0, concat_axis=0, tiled=True)  12.3 us
    pallas_call x1, Pallas kernels, after(): pl.pallas_call(after_kernel, out_shape=(jax.ShapeDtypeStruct((reqs, draft...  7.14 us
    pallas_call x1, Pallas kernels, before(): pl.pallas_call(before_kernel, out_shape=(pltpu.HBM(rows, f32), jax.ShapeD...  6.75 us
    ppermute x5, starting transfers between devices, moved_by(): lax.ppermute(values, axis, [(i, i ^ bits) for i in range(lax.axis_size(ax...  6.18 us
    unnamed x20, local copies, waits for them, and re-layouts  5.25 us
    dot_general x1, matrix products, on_device(): jnp.dot(normed, in_weight, preferred_element_type=jnp.float32)  4.91 us
    pallas_call x1, Pallas kernels, prepared(): pl.pallas_call(send_kernel, out_shape=(pltpu.HBM((blocks, slots, (states...  2.65 us
  transfers between devices with their start and end apart: 7, of which 5 were waited for; matrix products, arithmetic and copies ran while one was open for 9% of the time, Pallas kernels for 11%

profile of v5, /device:TPU:0, one launch (start us, length us, event | category | flops | bytes accessed | tf_op | source)
XLA Modules:
  0.0 72.1 jit_solution(11259732950037442896)
XLA Ops:
  0.6 2.6 %send_states.1 = (bf16[8,8,4864]{2,1,0:T(8,128)(2,1)}, bf16[88,256]{1,0:T(8,128)(2,1)S(1)}) custom-call(s32[1]{0:T(128)} %bitcast.3.group_ref, f32[128,2048]{1,0:T(8,128)} %bitcast.32, bf16[3,8,2048]{2,1,0:T(8,128)(2,1)} %bitcast.33, bf16[160,256]{1,0:T(8,128)(2,1)} %bitcast.34, bf16[128,256]{1,0:T(8,128)(2,1)} %sw_ref.1, f32[4,256]{1,0:T(4,128)} %cw_ref.1, ...), custom_call_target="tpu_custom_call" | custom-call | tf_op jit(solution)/shard_map/send_states/pallas_call | solution.py:115
  3.3 7.4 %all-to-all-start = ((bf16[8,8,4864]{2,1,0:T(8,128)(2,1)}), bf16[8,8,4864]{2,1,0:T(8,128)(2,1)S(1)}, u32[]{:S(2)}, u32[]{:S(2)}) async-start(bf16[8,8,4864]{2,1,0:T(8,128)(2,1)} %get-tuple-element.16), calls=%async_computation | async-start | bytes 1245184 | tf_op jit(solution)/shard_map/all_to_all | solution.py:544
  10.7 2.9 %collective-permute-start = (bf16[1,88,256]{2,1,0:T(8,128)(2,1)S(1)}, bf16[1,88,256]{2,1,0:T(8,128)(2,1)S(1)}, u32[]{:S(2)}, u32[]{:S(2)}) collective-permute-start(bf16[1,88,256]{2,1,0:T(8,128)(2,1)S(1)} %bitcast.28), channel_id=1, source_target_pairs={{0,16},{4,20},{8,24},{12,28},{16,0},{20,4},{24,8},{28,12},{1,17},{... | collective-permute-start | bytes 135176 | tf_op jit(solution)/shard_map/ppermute | solution.py:162
  13.6 1.2 %fusion.3 = f32[8,16]{0,1:T(8,128)S(1)} fusion(bf16[8,16,1024]{2,1,0:T(8,128)(2,1)} %param.17), kind=kLoop, calls=%fused_computation.7 | loop fusion | flops 393088 | bytes 262656 | tf_op jit(solution)/shard_map/reduce_sum | solution.py:20
  14.8 0.1 rsqrt.12
  14.9 14.3 %collective-permute-done = bf16[1,88,256]{2,1,0:T(8,128)(2,1)S(1)} collective-permute-done((bf16[1,88,256]{2,1,0:T(8,128)(2,1)S(1)}, bf16[1,88,256]{2,1,0:T(8,128)(2,1)S(1)}, u32[]{:S(2)}, u32[]{:S(2)}) %collective-permute-start) | collective-permute-done | bytes 45088 | tf_op jit(solution)/shard_map/ppermute | solution.py:162
  29.3 4.9 %convolution_convert_fusion.proj_ref = bf16[128,4096]{1,0:T(8,128)(2,1)S(1)} fusion(bf16[1024,4096]{1,0:T(8,128)(2,1)} %param.19, f32[1024]{0:T(1024)} %param.18, f32[128]{0:T(128)S(1)} %rsqrt.12, bf16[8,16,1024]{2,1,0:T(8,128)(2,1)} %param.17), kind=kOutput, calls=%fused_computation | convolution fusion | flops 1074790400 | bytes 9703936 | tf_op jit(solution)/shard_map/dot_general | solution.py:619
  34.3 1.5 %collective-permute-start.2 = (bf16[4,88,256]{2,1,0:T(8,128)(2,1)S(1)}, bf16[4,88,256]{2,1,0:T(8,128)(2,1)S(1)}, u32[]{:S(2)}, u32[]{:S(2)}) collective-permute-start(bf16[4,88,256]{2,1,0:T(8,128)(2,1)S(1)} %pad_maximum_fusion.1), channel_id=1, source_target_pairs={{0,4},{4,0},{8,12},{12,8},{16,20},{20,16},{24,28},{28,24},{1,5},{5... | collective-permute-start | bytes 540680 | tf_op jit(solution)/shard_map/ppermute | solution.py:162
  35.9 4.0 %collective-permute-done.2 = bf16[4,88,256]{2,1,0:T(8,128)(2,1)S(1)} collective-permute-done((bf16[4,88,256]{2,1,0:T(8,128)(2,1)S(1)}, bf16[4,88,256]{2,1,0:T(8,128)(2,1)S(1)}, u32[]{:S(2)}, u32[]{:S(2)}) %collective-permute-start.2) | collective-permute-done | bytes 180256 | tf_op jit(solution)/shard_map/ppermute | solution.py:162
  39.9 1.6 %collective-permute-start.3 = (bf16[1,8,88,256]{3,2,1,0:T(8,128)(2,1)S(1)}, bf16[1,8,88,256]{3,2,1,0:T(8,128)(2,1)S(1)}, u32[]{:S(2)}, u32[]{:S(2)}) collective-permute-start(bf16[1,8,88,256]{3,2,1,0:T(8,128)(2,1)S(1)} %maximum_bitcast_fusion), channel_id=1, source_target_pairs={{0,2},{1,3},{2,0},{3,1},{4,6},{5,7},{6,4},{7,5},{8,10},{9,11},{10,... | collective-permute-start | bytes 1081352 | tf_op jit(solution)/shard_map/ppermute | solution.py:162
  41.5 0.1 fusion.8
  41.7 1.1 %select_slots.1 = bf16[64,4864]{1,0:T(8,128)(2,1)} custom-call(bf16[4,64,64]{2,1,0:T(8,128)(2,1)S(1)} %add_convert_fusion.mask_ref, bf16[64,4864]{1,0:T(8,128)(2,1)S(1)} %bitcast.27), custom_call_target="tpu_custom_call" | custom-call | tf_op jit(solution)/shard_map/select_slots/pallas_call | solution.py:560
  42.8 4.9 %all-to-all-start.1 = ((bf16[8,8,4864]{2,1,0:T(8,128)(2,1)}), bf16[8,8,4864]{2,1,0:T(8,128)(2,1)S(1)}, u32[]{:S(2)}, u32[]{:S(2)}) async-start(bf16[8,8,4864]{2,1,0:T(8,128)(2,1)} %bitcast.11), calls=%async_computation.1 | async-start | bytes 1245184 | tf_op jit(solution)/shard_map/all_to_all | solution.py:544
  47.7 0.3 collective-permute-done.3
  48.2 2.1 %collective-permute-done.4.far_ref = bf16[2,8,88,256]{3,2,1,0:T(8,128)(2,1)S(1)} collective-permute-done((bf16[2,8,88,256]{3,2,1,0:T(8,128)(2,1)S(1)}, bf16[2,8,88,256]{3,2,1,0:T(8,128)(2,1)S(1)}, u32[]{:S(2)}, u32[]{:S(2)}) %collective-permute-start.4) | collective-permute-done | bytes 720928 | tf_op jit(solution)/shard_map/ppermute | solution.py:162
  50.3 0.9 %copy-done.4 = bf16[2,8,88,256]{3,2,1,0:T(8,128)(2,1)} copy-done((bf16[2,8,88,256]{3,2,1,0:T(8,128)(2,1)}, bf16[2,8,88,256]{3,2,1,0:T(8,128)(2,1)S(1)}, u32[]{:S(2)}) %copy-start.4) | copy-done | bytes 720920
  51.2 1.1 %copy-done.5 = bf16[2,8,88,256]{3,2,1,0:T(8,128)(2,1)S(1)} copy-done((bf16[2,8,88,256]{3,2,1,0:T(8,128)(2,1)S(1)}, bf16[2,8,88,256]{3,2,1,0:T(8,128)(2,1)}, u32[]{:S(2)}) %copy-start.5) | copy-done | bytes 720920
  52.3 6.7 %before_states.1 = (f32[16,464,128]{2,1,0:T(8,128)}, f32[16,8,128]{2,1,0:T(8,128)S(1)}, f32[104,32]{1,0:T(8,128)S(1)}, bf16[8,160,256]{2,1,0:T(8,128)(2,1)S(1)},...) custom-call(s32[4]{0:T(128)S(1)} %fusion.9.q_ref, s32[8]{0:T(128)S(1)} %fusion.11.j_ref, ...), custom_call_target="tpu_custom_call" | custom-call | flops 200000000 | bytes 8388608 | tf_op jit(solution)/shard_map/before_states/pallas_call | solution.py:337
  59.1 0.8 %copy-done = bf16[8,128,256]{2,1,0:T(8,128)(2,1)} copy-done((bf16[8,128,256]{2,1,0:T(8,128)(2,1)}, bf16[8,128,256]{2,1,0:T(8,128)(2,1)S(1)}, u32[]{:S(2)}) %copy-start) | copy-done | bytes 524312
  59.9 0.6 copy-done.2
  60.5 2.6 %all-to-all-done.1.moved_ref = bf16[8,8,4864]{2,1,0:T(8,128)(2,1)S(1)} async-done(((bf16[8,8,4864]{2,1,0:T(8,128)(2,1)}), bf16[8,8,4864]{2,1,0:T(8,128)(2,1)S(1)}, u32[]{:S(2)}, u32[]{:S(2)}) %all-to-all-start.1) | async-done | bytes 622624 | tf_op jit(solution)/shard_map/all_to_all | solution.py:544
  63.1 1.0 %copy-done.1 = bf16[8,128,256]{2,1,0:T(8,128)(2,1)S(1)} copy-done((bf16[8,128,256]{2,1,0:T(8,128)(2,1)S(1)}, bf16[8,128,256]{2,1,0:T(8,128)(2,1)}, u32[]{:S(2)}) %copy-start.1) | copy-done | bytes 524312
  64.1 0.8 %copy-done.3 = f32[104,32]{1,0:T(8,128)S(1)} copy-done((f32[104,32]{1,0:T(8,128)S(1)}, f32[104,32]{1,0:T(8,128)}, u32[]{:S(2)}) %copy-start.3) | copy-done | bytes 13336
  64.9 7.1 %after_states.1 = (bf16[8,16,1024]{2,1,0:T(8,128)(2,1)}, f32[128,2048]{1,0:T(8,128)}) custom-call(bf16[8,8,4864]{2,1,0:T(8,128)(2,1)S(1)} %all-to-all-done.1.moved_ref, s32[8,128]{1,0:T(8,128)S(1)} %broadcast_in_dim.54.acc_ref, f32[16,8,128]{2,1,0:T(8,128)S(1)} %get-tuple-element.19.at_ref, f32[104,32]{1,0:T(8,128)S(1)} %copy-done.3, ...), custom_call_target="tpu_custom_call" | custom-call | flops 536870912 | bytes 12582912 | tf_op jit(solution)/shard_map/after_states/pallas_call | solution.py:513
  (29 shorter events, 0.5 us)
Async XLA Ops:
  3.3 32.5 %copy-start.7 = (s32[64]{0:T(128)S(1)}, s32[64]{0:T(128)}, u32[]{:S(2)}) copy-start(s32[64]{0:T(128)} %param.33) | copy-start | bytes 772
  3.3 32.5 %copy-start.8 = (s32[64]{0:T(128)S(1)}, s32[64]{0:T(128)}, u32[]{:S(2)}) copy-start(s32[64]{0:T(128)} %param.31) | copy-start | bytes 772
  3.3 38.2 %copy-start.6 = (s32[64]{0:T(128)S(1)}, s32[64]{0:T(128)}, u32[]{:S(2)}) copy-start(s32[64]{0:T(128)} %param.30) | copy-start | bytes 772
  3.3 38.3 %all-to-all-start = ((bf16[8,8,4864]{2,1,0:T(8,128)(2,1)}), bf16[8,8,4864]{2,1,0:T(8,128)(2,1)S(1)}, u32[]{:S(2)}, u32[]{:S(2)}) async-start(bf16[8,8,4864]{2,1,0:T(8,128)(2,1)} %get-tuple-element.16), calls=%async_computation | async-start | bytes 1245184 | tf_op jit(solution)/shard_map/all_to_all | solution.py:544
  10.7 18.5 %collective-permute-start = (bf16[1,88,256]{2,1,0:T(8,128)(2,1)S(1)}, bf16[1,88,256]{2,1,0:T(8,128)(2,1)S(1)}, u32[]{:S(2)}, u32[]{:S(2)}) collective-permute-start(bf16[1,88,256]{2,1,0:T(8,128)(2,1)S(1)} %bitcast.28), channel_id=1, source_target_pairs={{0,16},{4,20},{8,24},{12,28},{16,0},{20,4},{24,8},{28,12},{1,17},{... | collective-permute-start | bytes 135176 | tf_op jit(solution)/shard_map/ppermute | solution.py:162
  29.3 18.8 %copy-start.9 = (s32[64]{0:T(128)S(1)}, s32[64]{0:T(128)}, u32[]{:S(2)}) copy-start(s32[64]{0:T(128)} %param.32) | copy-start | bytes 772
  29.3 5.0 %collective-permute-start.1 = (bf16[2,88,256]{2,1,0:T(8,128)(2,1)S(1)}, bf16[2,88,256]{2,1,0:T(8,128)(2,1)S(1)}, u32[]{:S(2)}, u32[]{:S(2)}) collective-permute-start(bf16[2,88,256]{2,1,0:T(8,128)(2,1)S(1)} %pad_maximum_fusion.2), channel_id=1, source_target_pairs={{0,8},{4,12},{8,0},{12,4},{16,24},{20,28},{24,16},{28,20},{1,9},{5... | collective-permute-start | bytes 270344 | tf_op jit(solution)/shard_map/ppermute | solution.py:162
  34.3 5.6 %collective-permute-start.2 = (bf16[4,88,256]{2,1,0:T(8,128)(2,1)S(1)}, bf16[4,88,256]{2,1,0:T(8,128)(2,1)S(1)}, u32[]{:S(2)}, u32[]{:S(2)}) collective-permute-start(bf16[4,88,256]{2,1,0:T(8,128)(2,1)S(1)} %pad_maximum_fusion.1), channel_id=1, source_target_pairs={{0,4},{4,0},{8,12},{12,8},{16,20},{20,16},{24,28},{28,24},{1,5},{5... | collective-permute-start | bytes 540680 | tf_op jit(solution)/shard_map/ppermute | solution.py:162
  39.9 8.0 %collective-permute-start.3 = (bf16[1,8,88,256]{3,2,1,0:T(8,128)(2,1)S(1)}, bf16[1,8,88,256]{3,2,1,0:T(8,128)(2,1)S(1)}, u32[]{:S(2)}, u32[]{:S(2)}) collective-permute-start(bf16[1,8,88,256]{3,2,1,0:T(8,128)(2,1)S(1)} %maximum_bitcast_fusion), channel_id=1, source_target_pairs={{0,2},{1,3},{2,0},{3,1},{4,6},{5,7},{6,4},{7,5},{8,10},{9,11},{10,... | collective-permute-start | bytes 1081352 | tf_op jit(solution)/shard_map/ppermute | solution.py:162
  42.8 20.3 %all-to-all-start.1 = ((bf16[8,8,4864]{2,1,0:T(8,128)(2,1)}), bf16[8,8,4864]{2,1,0:T(8,128)(2,1)S(1)}, u32[]{:S(2)}, u32[]{:S(2)}) async-start(bf16[8,8,4864]{2,1,0:T(8,128)(2,1)} %bitcast.11), calls=%async_computation.1 | async-start | bytes 1245184 | tf_op jit(solution)/shard_map/all_to_all | solution.py:544
  48.0 2.3 %collective-permute-start.4 = (bf16[2,8,88,256]{3,2,1,0:T(8,128)(2,1)S(1)}, bf16[2,8,88,256]{3,2,1,0:T(8,128)(2,1)S(1)}, u32[]{:S(2)}, u32[]{:S(2)}) collective-permute-start(bf16[2,8,88,256]{3,2,1,0:T(8,128)(2,1)S(1)} %pad_maximum_fusion.near_ref), channel_id=1, source_target_pairs={{0,1},{1,0},{2,3},{3,2},{4,5},{5,4},{6,7},{7,6},{8,9},{9,8},{10,11... | collective-permute-start | bytes 2162696 | tf_op jit(solution)/shard_map/ppermute | solution.py:162
  50.3 0.9 %copy-start.4 = (bf16[2,8,88,256]{3,2,1,0:T(8,128)(2,1)}, bf16[2,8,88,256]{3,2,1,0:T(8,128)(2,1)S(1)}, u32[]{:S(2)}) copy-start(bf16[2,8,88,256]{3,2,1,0:T(8,128)(2,1)S(1)} %collective-permute-done.4.far_ref) | copy-start | bytes 2162692
  51.2 1.1 %copy-start.5 = (bf16[2,8,88,256]{3,2,1,0:T(8,128)(2,1)S(1)}, bf16[2,8,88,256]{3,2,1,0:T(8,128)(2,1)}, u32[]{:S(2)}) copy-start(bf16[2,8,88,256]{3,2,1,0:T(8,128)(2,1)} %copy-done.4) | copy-start | bytes 2162692
  59.1 0.8 %copy-start = (bf16[8,128,256]{2,1,0:T(8,128)(2,1)}, bf16[8,128,256]{2,1,0:T(8,128)(2,1)S(1)}, u32[]{:S(2)}) copy-start(bf16[8,128,256]{2,1,0:T(8,128)(2,1)S(1)} %get-tuple-element.22.sw_ref) | copy-start | bytes 1572868
  59.9 0.6 copy-start.2
  63.1 1.0 %copy-start.1 = (bf16[8,128,256]{2,1,0:T(8,128)(2,1)S(1)}, bf16[8,128,256]{2,1,0:T(8,128)(2,1)}, u32[]{:S(2)}) copy-start(bf16[8,128,256]{2,1,0:T(8,128)(2,1)} %copy-done) | copy-start | bytes 1572868
  64.1 0.8 %copy-start.3 = (f32[104,32]{1,0:T(8,128)S(1)}, f32[104,32]{1,0:T(8,128)}, u32[]{:S(2)}) copy-start(f32[104,32]{1,0:T(8,128)} %copy-done.2) | copy-start | bytes 39940

commit v6 on v5

--- a/solution.py
+++ b/solution.py
@@ -56,11 +56,24 @@
     copies = [pltpu.make_async_copy(x, y, few.at[i]) for i, (x, y) in enumerate(small)]
     vec_ref[pl.ds(7, 1), :] = jnp.zeros((1, width), jnp.float32)
     vec_ref[pl.ds(24, 8), :] = jnp.zeros((8, width), jnp.float32)
-    for copy in copies:
-        copy.start()
+    copies[0].start()
     for tile in range(blocks * per):
         load(tile).start()
-    for copy in copies:
+    for copy in copies[1:]:
+        copy.start()
+    copies[0].wait()
+    for dest in range(blocks):
+        for e in range(edge_ref.shape[0]):
+            at = (states + e) * width
+            send_ref[dest, :, pl.ds(at, width)] = held_ref[e, :, pl.ds(dest * width, width)]
+        for part in range(per):
+            tile = dest * per + part
+            load(tile).wait()
+            for n in range(states):
+                rows = tile_ref[tile, pl.ds(n, slots, stride=states), :]
+                send_ref[dest, :, pl.ds(n * width + part * LANES, LANES)] = rows.astype(jnp.bfloat16)
+        store(dest).start()
+    for copy in copies[1:]:
         copy.wait()
     for k in range(4):
 
@@ -78,17 +91,6 @@
             ]
             share_ref[...] = jnp.concatenate(rows, axis=0).astype(jnp.bfloat16)
 
-    for dest in range(blocks):
-        for e in range(edge_ref.shape[0]):
-            at = (states + e) * width
-            send_ref[dest, :, pl.ds(at, width)] = held_ref[e, :, pl.ds(dest * width, width)]
-        for part in range(per):
-            tile = dest * per + part
-            load(tile).wait()
-            for n in range(states):
-                rows = tile_ref[tile, pl.ds(n, slots, stride=states), :]
-                send_ref[dest, :, pl.ds(n * width + part * LANES, LANES)] = rows.astype(jnp.bfloat16)
-        store(dest).start()
     for dest in range(blocks):
         store(dest).wait()
 
@@ -162,8 +164,8 @@
     return lax.ppermute(values, axis, [(i, i ^ bits) for i in range(lax.axis_size(axis))])
 
 
-def doubled(values, axis, bit, stop=0):
-    while bit > stop:
+def doubled(values, axis, bit):
+    while bit:
         values = jnp.concatenate([values, moved_by(values, axis, bit)], axis=0)
         bit //= 2
     return values
@@ -180,22 +182,17 @@
     return place
 
 
-def block_weights(near_ref, far_ref, q_ref, j_ref, j):
+def block_weights(w_ref, q_ref, j_ref, j):
     at = j_ref[j]
+    quarters = [w_ref.at[q_ref[q], at] for q in range(4)]
     f32 = jnp.float32
-
-    def rows(q, start, size):
-        place = q_ref[q]
-        some = pl.ds(start, size)
-        near = near_ref[place % 2, at, some, :].astype(f32)
-        return jnp.where(place < 2, near, far_ref[place % 2, at, some, :].astype(f32))
-
     xw = jnp.concatenate(
-        [rows(q, 0, 32) for q in range(4)] + [rows(q, 32, 8) for q in range(4)], axis=0
+        [w[pl.ds(0, 32), :].astype(f32) for w in quarters] + [w[pl.ds(32, 8), :].astype(f32) for w in quarters],
+        axis=0,
     ).astype(jnp.bfloat16)
-    sw = jnp.concatenate([rows(q, 48, 32) for q in range(4)], axis=0).astype(jnp.bfloat16)
-    first = [rows(q, 40, 8) for q in range(4)]
-    second = [rows(q, 80, 8) for q in range(4)]
+    sw = jnp.concatenate([w[pl.ds(48, 32), :] for w in quarters], axis=0)
+    first = [w[pl.ds(40, 8), :].astype(f32) for w in quarters]
+    second = [w[pl.ds(80, 8), :].astype(f32) for w in quarters]
     high = jnp.concatenate([first[0], second[0], first[1]], axis=0)
     low = jnp.concatenate([first[2], second[2], first[3]], axis=0)
     return xw, sw, high + low
@@ -230,11 +227,11 @@
 
 
 def before_kernel(
-    q_ref, j_ref, proj_ref, near_ref, far_ref, acc_ref,
+    q_ref, j_ref, proj_ref, w_ref, acc_ref,
     rows_out, at_ref, coef_ref, xw_ref, sw_ref, vec_ref, x_ref,
     rows_ref, dt_ref, cv_ref, b_ref, c_ref, dec_ref, sems,
 ):
-    blocks = near_ref.shape[1]
+    blocks = w_ref.shape[1]
     tiles, count, _ = dt_ref.shape
     tokens = proj_ref.shape[0]
     late = tokens - count
@@ -251,7 +248,7 @@
 
     mixed = jnp.zeros((count, rank + 2 * states), jnp.float32)
     for j in range(blocks):
-        xw, sw, vec = block_weights(near_ref, far_ref, q_ref, j_ref, j)
+        xw, sw, vec = block_weights(w_ref, q_ref, j_ref, j)
         values = proj_ref[:, pl.ds(j * BLOCK, BLOCK)].astype(jnp.float32)
         conv = convolved(values, vec, count)
         mixed = mixed + mixed_of(conv, xw)
@@ -324,7 +321,7 @@
 
 def before(q_place, j_place, projected, weights, accepted, late, states):
     tokens = projected.shape[0]
-    blocks = weights[0].shape[1]
+    blocks = weights.shape[1]
     tiles = blocks * (BLOCK // LANES)
     count = tokens - late
     reqs = accepted.shape[0]
@@ -345,7 +342,7 @@
             jax.ShapeDtypeStruct((blocks, 24, BLOCK), f32),
             jax.ShapeDtypeStruct((blocks, late, BLOCK), f32),
         ),
-        in_specs=[smem, smem, vmem, vmem, vmem, vmem],
+        in_specs=[smem, smem, vmem, vmem, vmem],
         out_specs=(pl.BlockSpec(memory_space=pltpu.HBM),) + (vmem,) * 6,
         scratch_shapes=[
             pltpu.VMEM(rows, f32),
@@ -359,7 +356,7 @@
         compiler_params=pltpu.CompilerParams(vmem_limit_bytes=24 << 20),
         cost_estimate=pl.CostEstimate(flops=200_000_000, bytes_accessed=8 << 20, transcendentals=4_000_000),
         name="before_states",
-    )(q_place, j_place, projected, *weights, accepted)
+    )(q_place, j_place, projected, weights, accepted)
 
 
 def after_kernel(
@@ -544,24 +541,33 @@
     return lax.all_to_all(values, "req", split_axis=0, concat_axis=0, tiled=True)
 
 
-def select_kernel(mask_ref, arrived_ref, out_ref):
+def select_kernel(mask_ref, arrived_ref, out_ref, kept_ref, sems):
     width = arrived_ref.shape[1] // 19
-    at = 16 * width
-    spans = [(0, 0, at)] + [(e + 1, at + e * width, width) for e in range(3)]
-    for which, start, size in spans:
-        cols = pl.ds(start, size)
-        out_ref[:, cols] = jnp.dot(
-            mask_ref[which], arrived_ref[:, cols], preferred_element_type=jnp.float32
-        ).astype(jnp.bfloat16)
+    copies = []
+    for at in range(0, 19, 4):
+        parts = [(0, 4)] if at < 16 else [(e + 1, 1) for e in range(3)]
+        start = at
+        for which, size in parts:
+            cols = pl.ds(start * width, size * width)
+            kept_ref[:, cols] = jnp.dot(
+                mask_ref[which], arrived_ref[:, cols], preferred_element_type=jnp.float32
+            ).astype(jnp.bfloat16)
+            start += size
+        cols = pl.ds(at * width, (start - at) * width)
+        copies.append(pltpu.make_async_copy(kept_ref.at[:, cols], out_ref.at[:, cols], sems.at[at // 4]))
+        copies[-1].start()
+    for copy in copies:
+        copy.wait()
 
 
 def select(masks, arrived):
     if arrived.shape[1] % (19 * LANES) == 0:
         return pl.pallas_call(
             select_kernel,
-            out_shape=jax.ShapeDtypeStruct(arrived.shape, jnp.bfloat16),
+            out_shape=pltpu.HBM(arrived.shape, jnp.bfloat16),
             in_specs=[pl.BlockSpec(memory_space=pltpu.VMEM)] * 2,
-            out_specs=pl.BlockSpec(memory_space=pltpu.VMEM),
+            out_specs=pl.BlockSpec(memory_space=pltpu.HBM),
+            scratch_shapes=[pltpu.VMEM(arrived.shape, jnp.bfloat16), pltpu.SemaphoreType.DMA((5,))],
             compiler_params=pltpu.CompilerParams(vmem_limit_bytes=16 << 20),
             name="select_slots",
         )(masks, arrived)
@@ -620,16 +626,17 @@
     masks, projected = lax.optimization_barrier((masks.astype(jnp.bfloat16), projected))
     moved = exchange(select(masks, arrived))
 
-    near = doubled(doubled(share[None], "req", blocks // 2)[None], "grp", groups // 2, 1)
-    weights = (near, moved_by(near, "grp", 1))
+    top = blocks // 2
+    weights = jnp.concatenate(
+        [share[None]] + [moved_by(share[None], "req", bits) for bits in (top, top // 2, top + top // 2)]
+    )
+    weights = doubled(doubled(weights, "req", top // 4)[None], "grp", groups // 2)
     q_place, j_place = places("grp"), places("req")
     if channels != BLOCK:
         moved = moved.reshape(blocks, local_reqs, state_size + span, channels).transpose(1, 2, 0, 3)
         moved = moved.reshape(local_reqs, state_size + span, -1, BLOCK).transpose(2, 0, 1, 3)
-        weights = tuple(
-            jnp.take(w, j_place, axis=1).swapaxes(1, 2).reshape(-1, SHARE, inner_width // BLOCK, BLOCK).swapaxes(1, 2)
-            for w in weights
-        )
+        weights = jnp.take(weights, j_place, axis=1).swapaxes(1, 2)
+        weights = weights.reshape(groups, SHARE, -1, BLOCK).swapaxes(1, 2)
         j_place = jnp.arange(inner_width // BLOCK, dtype=jnp.int32)
     moved = moved.reshape(inner_width // BLOCK, local_reqs, (state_size + span) * BLOCK)
 

time: 72.6 us -> 59.3 us (0.82)
  waiting for transfers between devices: 23.3 us -> 14.8 us
  local copies, waits for them, and re-layouts: 5.49 us -> 0.3 us
    ppermute x5 -> x6, waiting for transfers between devices: 20.7 us -> 10.2 us  [moved_by(): lax.ppermute(values, axis, [(i, i ^ bits) for i in range(lax.axis_size(ax...]
    unnamed x20 -> x16, local copies, waits for them, and re-layouts: 5.25 us -> 0.05 us
    ppermute x5 -> x6, starting transfers between devices: 6.18 us -> 9.49 us  [moved_by(): lax.ppermute(values, axis, [(i, i ^ bits) for i in range(lax.axis_size(ax...]
    all_to_all x2, starting transfers between devices: 12.3 us -> 9.65 us  [exchange(): lax.all_to_all(values, 'req', split_axis=0, concat_axis=0, tiled=True)]
    all_to_all x2, waiting for transfers between devices: 2.59 us -> 4.52 us  [exchange(): lax.all_to_all(values, 'req', split_axis=0, concat_axis=0, tiled=True)]
    concatenate x3 -> x2, other arithmetic: 0.1 us -> 1.32 us  [doubled(): values = jnp.concatenate([values, moved_by(values, axis, bit)], axis=0)]
    reduce_sum x1, other arithmetic: 1.17 us -> 0.22 us  [rms_normed(): factor = lax.rsqrt(jnp.mean(values * values, axis=-1, keepdims=True) + EPS)]
  transfers between devices with their start and end apart: 7 -> 8, of which waited for: 5 -> 5; matrix products, arithmetic and copies ran while one was open for 9% -> 12% of each run, Pallas kernels for 11% -> 13%
where the time goes in v6:
time: 59.3 us; the launch traced here: 58.9 us
  starting transfers between devices  19.1 us (32%)
  Pallas kernels  17.3 us (29%)
  waiting for transfers between devices  14.8 us (25%)
  matrix products  4.8 us (8%)
  other arithmetic  1.73 us (3%)
  between operations  0.86 us (1%)
    ppermute x6, waiting for transfers between devices, moved_by(): lax.ppermute(values, axis, [(i, i ^ bits) for i in range(lax.axis_size(ax...  10.2 us
    all_to_all x2, starting transfers between devices, exchange(): lax.all_to_all(values, 'req', split_axis=0, concat_axis=0, tiled=True)  9.65 us
    ppermute x6, starting transfers between devices, moved_by(): lax.ppermute(values, axis, [(i, i ^ bits) for i in range(lax.axis_size(ax...  9.49 us
    pallas_call x1, Pallas kernels, after(): pl.pallas_call(after_kernel, out_shape=(jax.ShapeDtypeStruct((reqs, draft...  7.14 us
    pallas_call x1, Pallas kernels, before(): pl.pallas_call(before_kernel, out_shape=(pltpu.HBM(rows, f32), jax.ShapeD...  6.54 us
    dot_general x1, matrix products, on_device(): jnp.dot(normed, in_weight, preferred_element_type=jnp.float32)  4.8 us
    all_to_all x2, waiting for transfers between devices, exchange(): lax.all_to_all(values, 'req', split_axis=0, concat_axis=0, tiled=True)  4.52 us
    pallas_call x1, Pallas kernels, prepared(): pl.pallas_call(send_kernel, out_shape=(pltpu.HBM((blocks, slots, (states...  2.6 us
  transfers between devices with their start and end apart: 8, of which 5 were waited for; matrix products, arithmetic and copies ran while one was open for 12% of the time, Pallas kernels for 13%

profile of v6, /device:TPU:0, one launch (start us, length us, event | category | flops | bytes accessed | tf_op | source)
XLA Modules:
  0.0 58.9 jit_solution(3576088093094948412)
XLA Ops:
  0.7 2.6 %send_states.1 = (bf16[8,8,4864]{2,1,0:T(8,128)(2,1)}, bf16[88,256]{1,0:T(8,128)(2,1)S(1)}) custom-call(s32[1]{0:T(128)} %bitcast.3.group_ref, f32[128,2048]{1,0:T(8,128)} %bitcast.36, bf16[3,8,2048]{2,1,0:T(8,128)(2,1)} %bitcast.37, bf16[160,256]{1,0:T(8,128)(2,1)} %bitcast.38, bf16[128,256]{1,0:T(8,128)(2,1)} %sw_ref.1, f32[4,256]{1,0:T(4,128)} %cw_ref.1, ...), custom_call_target="tpu_custom_call" | custom-call | tf_op jit(solution)/shard_map/send_states/pallas_call | solution.py:117
  3.3 5.1 %collective-permute-start.2 = (bf16[1,88,256]{2,1,0:T(8,128)(2,1)S(1)}, bf16[1,88,256]{2,1,0:T(8,128)(2,1)S(1)}, u32[]{:S(2)}, u32[]{:S(2)}) collective-permute-start(bf16[1,88,256]{2,1,0:T(8,128)(2,1)S(1)} %bitcast.28), channel_id=1, source_target_pairs={{0,24},{4,28},{8,16},{12,20},{16,8},{20,12},{24,0},{28,4},{1,25},{... | collective-permute-start | bytes 135176 | tf_op jit(solution)/shard_map/ppermute | solution.py:164
  8.4 0.6 %collective-permute-start = (bf16[1,88,256]{2,1,0:T(8,128)(2,1)S(1)}, bf16[1,88,256]{2,1,0:T(8,128)(2,1)S(1)}, u32[]{:S(2)}, u32[]{:S(2)}) collective-permute-start(bf16[1,88,256]{2,1,0:T(8,128)(2,1)S(1)} %bitcast.30), channel_id=1, source_target_pairs={{0,16},{4,20},{8,24},{12,28},{16,0},{20,4},{24,8},{28,12},{1,17},{... | collective-permute-start | bytes 135176 | tf_op jit(solution)/shard_map/ppermute | solution.py:164
  9.0 5.9 %all-to-all-start = ((bf16[8,8,4864]{2,1,0:T(8,128)(2,1)}), bf16[8,8,4864]{2,1,0:T(8,128)(2,1)S(1)}, u32[]{:S(2)}, u32[]{:S(2)}) async-start(bf16[8,8,4864]{2,1,0:T(8,128)(2,1)} %get-tuple-element.16), calls=%async_computation | async-start | bytes 1245184 | tf_op jit(solution)/shard_map/all_to_all | solution.py:541
  15.0 0.2 fusion.3
  15.2 0.1 rsqrt.12
  15.4 4.8 %convolution_convert_fusion.proj_ref = bf16[128,4096]{1,0:T(8,128)(2,1)S(1)} fusion(bf16[1024,4096]{1,0:T(8,128)(2,1)} %param.19, f32[1024]{0:T(1024)S(1)} %copy-done.1, f32[128]{0:T(128)S(1)} %rsqrt.12, bf16[8,16,1024]{2,1,0:T(8,128)(2,1)S(1)} %copy-done), kind=kOutput, calls=%fused_computation | convolution fusion | flops 1074790400 | bytes 9703936 | tf_op jit(solution)/shard_map/dot_general | solution.py:625
  20.3 2.1 %collective-permute-start.3 = (bf16[4,88,256]{2,1,0:T(8,128)(2,1)S(1)}, bf16[4,88,256]{2,1,0:T(8,128)(2,1)S(1)}, u32[]{:S(2)}, u32[]{:S(2)}) collective-permute-start(bf16[4,88,256]{2,1,0:T(8,128)(2,1)S(1)} %pad_maximum_fusion.2), channel_id=1, source_target_pairs={{0,4},{4,0},{8,12},{12,8},{16,20},{20,16},{24,28},{28,24},{1,5},{5... | collective-permute-start | bytes 540680 | tf_op jit(solution)/shard_map/ppermute | solution.py:164
  22.4 6.2 %collective-permute-done.3 = bf16[4,88,256]{2,1,0:T(8,128)(2,1)S(1)} collective-permute-done((bf16[4,88,256]{2,1,0:T(8,128)(2,1)S(1)}, bf16[4,88,256]{2,1,0:T(8,128)(2,1)S(1)}, u32[]{:S(2)}, u32[]{:S(2)}) %collective-permute-start.3) | collective-permute-done | bytes 180256 | tf_op jit(solution)/shard_map/ppermute | solution.py:164
  28.6 1.6 %collective-permute-start.4 = (bf16[1,8,88,256]{3,2,1,0:T(8,128)(2,1)S(1)}, bf16[1,8,88,256]{3,2,1,0:T(8,128)(2,1)S(1)}, u32[]{:S(2)}, u32[]{:S(2)}) collective-permute-start(bf16[1,8,88,256]{3,2,1,0:T(8,128)(2,1)S(1)} %bitcast.33), channel_id=1, source_target_pairs={{0,2},{1,3},{2,0},{3,1},{4,6},{5,7},{6,4},{7,5},{8,10},{9,11},{10,... | collective-permute-start | bytes 1081352 | tf_op jit(solution)/shard_map/ppermute | solution.py:164
  30.2 0.1 fusion.8
  30.3 0.5 all-to-all-done
  30.8 1.0 %select_slots.1 = bf16[64,4864]{1,0:T(8,128)(2,1)} custom-call(bf16[4,64,64]{2,1,0:T(8,128)(2,1)S(1)} %add_convert_fusion.mask_ref, bf16[64,4864]{1,0:T(8,128)(2,1)S(1)} %bitcast.27), custom_call_target="tpu_custom_call" | custom-call | tf_op jit(solution)/shard_map/select_slots/pallas_call | solution.py:565
  31.8 3.7 %all-to-all-start.1 = ((bf16[8,8,4864]{2,1,0:T(8,128)(2,1)}), bf16[8,8,4864]{2,1,0:T(8,128)(2,1)S(1)}, u32[]{:S(2)}, u32[]{:S(2)}) async-start(bf16[8,8,4864]{2,1,0:T(8,128)(2,1)} %bitcast.32), calls=%async_computation.1 | async-start | bytes 1245184 | tf_op jit(solution)/shard_map/all_to_all | solution.py:541
  35.5 1.9 %collective-permute-done.4 = bf16[1,8,88,256]{3,2,1,0:T(8,128)(2,1)S(1)} collective-permute-done((bf16[1,8,88,256]{3,2,1,0:T(8,128)(2,1)S(1)}, bf16[1,8,88,256]{3,2,1,0:T(8,128)(2,1)S(1)}, u32[]{:S(2)}, u32[]{:S(2)}) %collective-permute-start.4) | collective-permute-done | bytes 360480 | tf_op jit(solution)/shard_map/ppermute | solution.py:164
  37.4 0.1 pad_maximum_fusion.1
  37.4 0.1 collective-permute-start.5
  37.5 0.1 dynamic_slice.3
  37.6 2.2 %collective-permute-done.5 = bf16[2,8,88,256]{3,2,1,0:T(8,128)(2,1)} collective-permute-done((bf16[2,8,88,256]{3,2,1,0:T(8,128)(2,1)S(1)}, bf16[2,8,88,256]{3,2,1,0:T(8,128)(2,1)}, u32[]{:S(2)}, u32[]{:S(2)}) %collective-permute-start.5) | collective-permute-done | bytes 720928 | tf_op jit(solution)/shard_map/ppermute | solution.py:164
  39.8 1.3 %pad_maximum_fusion.w_ref = bf16[4,8,88,256]{3,2,1,0:T(8,128)(2,1)S(1)} fusion(bf16[2,8,88,256]{3,2,1,0:T(8,128)(2,1)} %collective-permute-done.5, bf16[1,8,88,256]{3,2,1,0:T(8,128)(2,1)S(1)} %collective-permute-done.4, bf16[1,8,88,256]{3,2,1,0:T(8,128)(2,1)S(1)} %bitcast.35), kind=kLoop, calls=%fused_computation.1 | loop fusion | flops 1441792 | bytes 2883584 | tf_op jit(solution)/shard_map/concatenate | solution.py:169
  41.1 0.1 broadcast_in_dim.57.acc_ref
  41.2 6.5 %before_states.1 = (f32[16,464,128]{2,1,0:T(8,128)}, f32[16,8,128]{2,1,0:T(8,128)S(1)}, f32[104,32]{1,0:T(8,128)S(1)}, bf16[8,160,256]{2,1,0:T(8,128)(2,1)S(1)},...) custom-call(s32[4]{0:T(128)S(1)} %fusion.9.q_ref, s32[8]{0:T(128)S(1)} %fusion.11.j_ref, ...), custom_call_target="tpu_custom_call" | custom-call | flops 200000000 | bytes 8388608 | tf_op jit(solution)/shard_map/before_states/pallas_call | solution.py:334
  47.7 4.1 %all-to-all-done.1.moved_ref = bf16[8,8,4864]{2,1,0:T(8,128)(2,1)S(1)} async-done(((bf16[8,8,4864]{2,1,0:T(8,128)(2,1)}), bf16[8,8,4864]{2,1,0:T(8,128)(2,1)S(1)}, u32[]{:S(2)}, u32[]{:S(2)}) %all-to-all-start.1) | async-done | bytes 622624 | tf_op jit(solution)/shard_map/all_to_all | solution.py:541
  51.8 7.1 %after_states.1 = (bf16[8,16,1024]{2,1,0:T(8,128)(2,1)}, f32[128,2048]{1,0:T(8,128)}) custom-call(bf16[8,8,4864]{2,1,0:T(8,128)(2,1)S(1)} %all-to-all-done.1.moved_ref, s32[8,128]{1,0:T(8,128)S(1)} %broadcast_in_dim.57.acc_ref, f32[16,8,128]{2,1,0:T(8,128)S(1)} %get-tuple-element.19.at_ref, f32[104,32]{1,0:T(8,128)S(1)} %get-tuple-element.20.coef_ref, ...), custom_call_target="tpu_custom_call" | custom-call | flops 536870912 | bytes 12582912 | tf_op jit(solution)/shard_map/after_states/pallas_call | solution.py:510
  (27 shorter events, 0.2 us)
Async XLA Ops:
  0.6 14.4 %copy-start = (bf16[8,16,1024]{2,1,0:T(8,128)(2,1)S(1)}, bf16[8,16,1024]{2,1,0:T(8,128)(2,1)}, u32[]{:S(2)}) copy-start(bf16[8,16,1024]{2,1,0:T(8,128)(2,1)} %param.17) | copy-start | bytes 786436
  0.6 14.7 %copy-start.1 = (f32[1024]{0:T(1024)S(1)}, f32[1024]{0:T(1024)}, u32[]{:S(2)}) copy-start(f32[1024]{0:T(1024)} %param.18) | copy-start | bytes 12292
  3.3 16.9 %collective-permute-start.2 = (bf16[1,88,256]{2,1,0:T(8,128)(2,1)S(1)}, bf16[1,88,256]{2,1,0:T(8,128)(2,1)S(1)}, u32[]{:S(2)}, u32[]{:S(2)}) collective-permute-start(bf16[1,88,256]{2,1,0:T(8,128)(2,1)S(1)} %bitcast.28), channel_id=1, source_target_pairs={{0,24},{4,28},{8,16},{12,20},{16,8},{20,12},{24,0},{28,4},{1,25},{... | collective-permute-start | bytes 135176 | tf_op jit(solution)/shard_map/ppermute | solution.py:164
  8.4 11.8 %collective-permute-start.1 = (bf16[1,88,256]{2,1,0:T(8,128)(2,1)S(1)}, bf16[1,88,256]{2,1,0:T(8,128)(2,1)S(1)}, u32[]{:S(2)}, u32[]{:S(2)}) collective-permute-start(bf16[1,88,256]{2,1,0:T(8,128)(2,1)S(1)} %bitcast.29), channel_id=1, source_target_pairs={{0,8},{4,12},{8,0},{12,4},{16,24},{20,28},{24,16},{28,20},{1,9},{5... | collective-permute-start | bytes 135176 | tf_op jit(solution)/shard_map/ppermute | solution.py:164
  8.4 11.8 %collective-permute-start = (bf16[1,88,256]{2,1,0:T(8,128)(2,1)S(1)}, bf16[1,88,256]{2,1,0:T(8,128)(2,1)S(1)}, u32[]{:S(2)}, u32[]{:S(2)}) collective-permute-start(bf16[1,88,256]{2,1,0:T(8,128)(2,1)S(1)} %bitcast.30), channel_id=1, source_target_pairs={{0,16},{4,20},{8,24},{12,28},{16,0},{20,4},{24,8},{28,12},{1,17},{... | collective-permute-start | bytes 135176 | tf_op jit(solution)/shard_map/ppermute | solution.py:164
  9.0 21.7 %all-to-all-start = ((bf16[8,8,4864]{2,1,0:T(8,128)(2,1)}), bf16[8,8,4864]{2,1,0:T(8,128)(2,1)S(1)}, u32[]{:S(2)}, u32[]{:S(2)}) async-start(bf16[8,8,4864]{2,1,0:T(8,128)(2,1)} %get-tuple-element.16), calls=%async_computation | async-start | bytes 1245184 | tf_op jit(solution)/shard_map/all_to_all | solution.py:541
  15.3 4.9 %copy-start.3 = (s32[64]{0:T(128)S(1)}, s32[64]{0:T(128)}, u32[]{:S(2)}) copy-start(s32[64]{0:T(128)} %param.33) | copy-start | bytes 772
  15.3 4.8 %copy-start.4 = (s32[64]{0:T(128)S(1)}, s32[64]{0:T(128)}, u32[]{:S(2)}) copy-start(s32[64]{0:T(128)} %param.31) | copy-start | bytes 772
  15.4 14.8 %copy-start.2 = (s32[64]{0:T(128)S(1)}, s32[64]{0:T(128)}, u32[]{:S(2)}) copy-start(s32[64]{0:T(128)} %param.30) | copy-start | bytes 772
  20.3 8.3 %collective-permute-start.3 = (bf16[4,88,256]{2,1,0:T(8,128)(2,1)S(1)}, bf16[4,88,256]{2,1,0:T(8,128)(2,1)S(1)}, u32[]{:S(2)}, u32[]{:S(2)}) collective-permute-start(bf16[4,88,256]{2,1,0:T(8,128)(2,1)S(1)} %pad_maximum_fusion.2), channel_id=1, source_target_pairs={{0,4},{4,0},{8,12},{12,8},{16,20},{20,16},{24,28},{28,24},{1,5},{5... | collective-permute-start | bytes 540680 | tf_op jit(solution)/shard_map/ppermute | solution.py:164
  28.6 9.0 %copy-start.5 = (s32[64]{0:T(128)S(1)}, s32[64]{0:T(128)}, u32[]{:S(2)}) copy-start(s32[64]{0:T(128)} %param.32) | copy-start | bytes 772
  28.6 8.8 %collective-permute-start.4 = (bf16[1,8,88,256]{3,2,1,0:T(8,128)(2,1)S(1)}, bf16[1,8,88,256]{3,2,1,0:T(8,128)(2,1)S(1)}, u32[]{:S(2)}, u32[]{:S(2)}) collective-permute-start(bf16[1,8,88,256]{3,2,1,0:T(8,128)(2,1)S(1)} %bitcast.33), channel_id=1, source_target_pairs={{0,2},{1,3},{2,0},{3,1},{4,6},{5,7},{6,4},{7,5},{8,10},{9,11},{10,... | collective-permute-start | bytes 1081352 | tf_op jit(solution)/shard_map/ppermute | solution.py:164
  31.8 20.0 %all-to-all-start.1 = ((bf16[8,8,4864]{2,1,0:T(8,128)(2,1)}), bf16[8,8,4864]{2,1,0:T(8,128)(2,1)S(1)}, u32[]{:S(2)}, u32[]{:S(2)}) async-start(bf16[8,8,4864]{2,1,0:T(8,128)(2,1)} %bitcast.32), calls=%async_computation.1 | async-start | bytes 1245184 | tf_op jit(solution)/shard_map/all_to_all | solution.py:541
  37.4 2.4 %collective-permute-start.5 = (bf16[2,8,88,256]{3,2,1,0:T(8,128)(2,1)S(1)}, bf16[2,8,88,256]{3,2,1,0:T(8,128)(2,1)}, u32[]{:S(2)}, u32[]{:S(2)}) collective-permute-start(bf16[2,8,88,256]{3,2,1,0:T(8,128)(2,1)S(1)} %pad_maximum_fusion.1), channel_id=1, source_target_pairs={{0,1},{1,0},{2,3},{3,2},{4,5},{5,4},{6,7},{7,6},{8,9},{9,8},{10,11... | collective-permute-start | bytes 2162696 | tf_op jit(solution)/shard_map/ppermute | solution.py:164

commit v7 on v6

--- a/solution.py
+++ b/solution.py
@@ -617,21 +617,24 @@
         old_states, old_edges, x_weight, step_weight, conv_weight, conv_bias, step_bias, skip_gain, log_decay
     )
     arrived = exchange(packed.reshape(all_reqs, (state_size + span) * channels))
+    top = blocks // 2
+    weights = jnp.concatenate(
+        [share[None]] + [moved_by(share[None], "req", bits) for bits in (top, top // 2, top + top // 2)]
+    )
+    hidden, weights = lax.optimization_barrier((hidden, weights))
+    weights = doubled(weights, "req", top // 4)[None]
+
     old_slot = jnp.arange(all_reqs, dtype=jnp.int32)
     chosen = (anchor[:, None] == old_slot[None, :]) & (fresh_flag[:, None] == 0)
     masks = jnp.stack([chosen] + [chosen & (span - e <= request_ages)[:, None] for e in range(span)])
     token_major = jnp.swapaxes(hidden, 0, 1).reshape(tokens, width)
     normed = rms_normed(token_major, norm_gain)
     projected = jnp.dot(normed, in_weight, preferred_element_type=jnp.float32).astype(jnp.bfloat16)
-    masks, projected = lax.optimization_barrier((masks.astype(jnp.bfloat16), projected))
+    masks, projected, weights = lax.optimization_barrier((masks.astype(jnp.bfloat16), projected, weights))
     moved = exchange(select(masks, arrived))
 
-    top = blocks // 2
-    weights = jnp.concatenate(
-        [share[None]] + [moved_by(share[None], "req", bits) for bits in (top, top // 2, top + top // 2)]
-    )
-    weights = doubled(doubled(weights, "req", top // 4)[None], "grp", groups // 2)
     q_place, j_place = places("grp"), places("req")
+    weights = doubled(weights, "grp", groups // 2)
     if channels != BLOCK:
         moved = moved.reshape(blocks, local_reqs, state_size + span, channels).transpose(1, 2, 0, 3)
         moved = moved.reshape(local_reqs, state_size + span, -1, BLOCK).transpose(2, 0, 1, 3)

time: 59.3 us -> 59.3 us (level)
    all_to_all x2, waiting for transfers between devices: 4.52 us -> 8.9 us  [exchange(): lax.all_to_all(values, 'req', split_axis=0, concat_axis=0, tiled=True)]
    ppermute x6, waiting for transfers between devices: 10.2 us -> 5.97 us  [moved_by(): lax.ppermute(values, axis, [(i, i ^ bits) for i in range(lax.axis_size(ax...]
  transfers between devices with their start and end apart: 8 -> 8, of which waited for: 5 -> 4; matrix products, arithmetic and copies ran while one was open for 12% -> 12% of each run, Pallas kernels for 13% -> 13%
where the time goes in v7:
time: 59.3 us; the launch traced here: 58.9 us
  starting transfers between devices  19.1 us (32%)
  Pallas kernels  17.3 us (29%)
  waiting for transfers between devices  14.9 us (25%)
  matrix products  4.78 us (8%)
  other arithmetic  1.76 us (3%)
  between operations  0.85 us (1%)
    all_to_all x2, starting transfers between devices, exchange(): lax.all_to_all(values, 'req', split_axis=0, concat_axis=0, tiled=True)  9.6 us
    ppermute x6, starting transfers between devices, moved_by(): lax.ppermute(values, axis, [(i, i ^ bits) for i in range(lax.axis_size(ax...  9.49 us
    all_to_all x2, waiting for transfers between devices, exchange(): lax.all_to_all(values, 'req', split_axis=0, concat_axis=0, tiled=True)  8.9 us
    pallas_call x1, Pallas kernels, after(): pl.pallas_call(after_kernel, out_shape=(jax.ShapeDtypeStruct((reqs, draft...  7.14 us
    pallas_call x1, Pallas kernels, before(): pl.pallas_call(before_kernel, out_shape=(pltpu.HBM(rows, f32), jax.ShapeD...  6.54 us
    ppermute x6, waiting for transfers between devices, moved_by(): lax.ppermute(values, axis, [(i, i ^ bits) for i in range(lax.axis_size(ax...  5.97 us
    dot_general x1, matrix products, on_device(): jnp.dot(normed, in_weight, preferred_element_type=jnp.float32)  4.78 us
    pallas_call x1, Pallas kernels, prepared(): pl.pallas_call(send_kernel, out_shape=(pltpu.HBM((blocks, slots, (states...  2.61 us
  transfers between devices with their start and end apart: 8, of which 4 were waited for; matrix products, arithmetic and copies ran while one was open for 12% of the time, Pallas kernels for 13%

profile of v7, /device:TPU:0, one launch (start us, length us, event | category | flops | bytes accessed | tf_op | source)
XLA Modules:
  0.0 58.9 jit_solution(17638952315733612633)
XLA Ops:
  0.7 2.6 %send_states.1 = (bf16[8,8,4864]{2,1,0:T(8,128)(2,1)}, bf16[88,256]{1,0:T(8,128)(2,1)S(1)}) custom-call(s32[1]{0:T(128)} %bitcast.group_ref, f32[128,2048]{1,0:T(8,128)} %bitcast.33, bf16[3,8,2048]{2,1,0:T(8,128)(2,1)} %bitcast.34, bf16[160,256]{1,0:T(8,128)(2,1)} %bitcast.35, bf16[128,256]{1,0:T(8,128)(2,1)} %sw_ref.1, f32[4,256]{1,0:T(4,128)} %cw_ref.1, ...), custom_call_target="tpu_custom_call" | custom-call | tf_op jit(solution)/shard_map/send_states/pallas_call | solution.py:117
  3.3 5.1 %collective-permute-start.2 = (bf16[1,88,256]{2,1,0:T(8,128)(2,1)S(1)}, bf16[1,88,256]{2,1,0:T(8,128)(2,1)S(1)}, u32[]{:S(2)}, u32[]{:S(2)}) collective-permute-start(bf16[1,88,256]{2,1,0:T(8,128)(2,1)S(1)} %bitcast.28), channel_id=1, source_target_pairs={{0,24},{4,28},{8,16},{12,20},{16,8},{20,12},{24,0},{28,4},{1,25},{... | collective-permute-start | bytes 135176 | tf_op jit(solution)/shard_map/ppermute | solution.py:164
  8.4 0.6 %collective-permute-start = (bf16[1,88,256]{2,1,0:T(8,128)(2,1)S(1)}, bf16[1,88,256]{2,1,0:T(8,128)(2,1)S(1)}, u32[]{:S(2)}, u32[]{:S(2)}) collective-permute-start(bf16[1,88,256]{2,1,0:T(8,128)(2,1)S(1)} %bitcast.30), channel_id=1, source_target_pairs={{0,16},{4,20},{8,24},{12,28},{16,0},{20,4},{24,8},{28,12},{1,17},{... | collective-permute-start | bytes 135176 | tf_op jit(solution)/shard_map/ppermute | solution.py:164
  9.1 5.9 %all-to-all-start = ((bf16[8,8,4864]{2,1,0:T(8,128)(2,1)}), bf16[8,8,4864]{2,1,0:T(8,128)(2,1)S(1)}, u32[]{:S(2)}, u32[]{:S(2)}) async-start(bf16[8,8,4864]{2,1,0:T(8,128)(2,1)} %get-tuple-element.22), calls=%async_computation | async-start | bytes 1245184 | tf_op jit(solution)/shard_map/all_to_all | solution.py:541
  15.0 0.1 fusion.8
  15.3 0.2 fusion.3
  15.5 0.1 rsqrt.12
  15.6 2.1 %collective-permute-start.3 = (bf16[4,88,256]{2,1,0:T(8,128)(2,1)S(1)}, bf16[4,88,256]{2,1,0:T(8,128)(2,1)S(1)}, u32[]{:S(2)}, u32[]{:S(2)}) collective-permute-start(bf16[4,88,256]{2,1,0:T(8,128)(2,1)S(1)} %pad_maximum_fusion.2), channel_id=1, source_target_pairs={{0,4},{4,0},{8,12},{12,8},{16,20},{20,16},{24,28},{28,24},{1,5},{5... | collective-permute-start | bytes 540680 | tf_op jit(solution)/shard_map/ppermute | solution.py:164
  17.7 4.8 %convolution_convert_fusion.proj_ref = bf16[128,4096]{1,0:T(8,128)(2,1)S(1)} fusion(bf16[1024,4096]{1,0:T(8,128)(2,1)} %param.19, f32[1024]{0:T(1024)S(1)} %copy-done.1, f32[128]{0:T(128)S(1)} %rsqrt.12, bf16[8,16,1024]{2,1,0:T(8,128)(2,1)S(1)} %copy-done), kind=kOutput, calls=%fused_computation | convolution fusion | flops 1074790400 | bytes 9703936 | tf_op jit(solution)/shard_map/dot_general | solution.py:632
  22.5 3.8 %collective-permute-done.3 = bf16[4,88,256]{2,1,0:T(8,128)(2,1)S(1)} collective-permute-done((bf16[4,88,256]{2,1,0:T(8,128)(2,1)S(1)}, bf16[4,88,256]{2,1,0:T(8,128)(2,1)S(1)}, u32[]{:S(2)}, u32[]{:S(2)}) %collective-permute-start.3) | collective-permute-done | bytes 180256 | tf_op jit(solution)/shard_map/ppermute | solution.py:164
  26.3 0.0 copy-start.5
  26.3 1.6 %collective-permute-start.4 = (bf16[1,8,88,256]{3,2,1,0:T(8,128)(2,1)S(1)}, bf16[1,8,88,256]{3,2,1,0:T(8,128)(2,1)S(1)}, u32[]{:S(2)}, u32[]{:S(2)}) collective-permute-start(bf16[1,8,88,256]{3,2,1,0:T(8,128)(2,1)S(1)} %maximum_bitcast_fusion), channel_id=1, source_target_pairs={{0,2},{1,3},{2,0},{3,1},{4,6},{5,7},{6,4},{7,5},{8,10},{9,11},{10,... | collective-permute-start | bytes 1081352 | tf_op jit(solution)/shard_map/ppermute | solution.py:164
  27.9 3.0 %all-to-all-done = bf16[8,8,4864]{2,1,0:T(8,128)(2,1)S(1)} async-done(((bf16[8,8,4864]{2,1,0:T(8,128)(2,1)}), bf16[8,8,4864]{2,1,0:T(8,128)(2,1)S(1)}, u32[]{:S(2)}, u32[]{:S(2)}) %all-to-all-start) | async-done | bytes 622624 | tf_op jit(solution)/shard_map/all_to_all | solution.py:541
  30.8 1.0 %select_slots.1 = bf16[64,4864]{1,0:T(8,128)(2,1)} custom-call(bf16[4,64,64]{2,1,0:T(8,128)(2,1)S(1)} %add_convert_fusion.mask_ref, bf16[64,4864]{1,0:T(8,128)(2,1)S(1)} %bitcast.27), custom_call_target="tpu_custom_call" | custom-call | tf_op jit(solution)/shard_map/select_slots/pallas_call | solution.py:565
  31.9 3.7 %all-to-all-start.1 = ((bf16[8,8,4864]{2,1,0:T(8,128)(2,1)}), bf16[8,8,4864]{2,1,0:T(8,128)(2,1)S(1)}, u32[]{:S(2)}, u32[]{:S(2)}) async-start(bf16[8,8,4864]{2,1,0:T(8,128)(2,1)} %bitcast.32), calls=%async_computation.1 | async-start | bytes 1245184 | tf_op jit(solution)/shard_map/all_to_all | solution.py:541
  35.5 0.1 pad_maximum_fusion.1
  35.6 0.1 collective-permute-start.5
  35.7 0.1 dynamic_slice.3
  35.8 2.2 %collective-permute-done.5 = bf16[2,8,88,256]{3,2,1,0:T(8,128)(2,1)} collective-permute-done((bf16[2,8,88,256]{3,2,1,0:T(8,128)(2,1)S(1)}, bf16[2,8,88,256]{3,2,1,0:T(8,128)(2,1)}, u32[]{:S(2)}, u32[]{:S(2)}) %collective-permute-start.5) | collective-permute-done | bytes 720928 | tf_op jit(solution)/shard_map/ppermute | solution.py:164
  38.0 1.3 %pad_maximum_fusion.w_ref = bf16[4,8,88,256]{3,2,1,0:T(8,128)(2,1)S(1)} fusion(bf16[2,8,88,256]{3,2,1,0:T(8,128)(2,1)} %collective-permute-done.5, bf16[1,8,88,256]{3,2,1,0:T(8,128)(2,1)S(1)} %collective-permute-done.4, bf16[1,8,88,256]{3,2,1,0:T(8,128)(2,1)S(1)} %maximum_bitcast_fusion), kind=kLoop, calls=%fused_computation.1 | loop fusion | flops 1441792 | bytes 2883584 | tf_op jit(solution)/shard_map/concatenate | solution.py:169
  39.2 0.1 broadcast_in_dim.59.acc_ref
  39.3 6.5 %before_states.1 = (f32[16,464,128]{2,1,0:T(8,128)}, f32[16,8,128]{2,1,0:T(8,128)S(1)}, f32[104,32]{1,0:T(8,128)S(1)}, bf16[8,160,256]{2,1,0:T(8,128)(2,1)S(1)},...) custom-call(s32[4]{0:T(128)S(1)} %fusion.9.q_ref, s32[8]{0:T(128)S(1)} %fusion.11.j_ref, ...), custom_call_target="tpu_custom_call" | custom-call | flops 200000000 | bytes 8388608 | tf_op jit(solution)/shard_map/before_states/pallas_call | solution.py:334
  45.8 5.9 %all-to-all-done.1.moved_ref = bf16[8,8,4864]{2,1,0:T(8,128)(2,1)S(1)} async-done(((bf16[8,8,4864]{2,1,0:T(8,128)(2,1)}), bf16[8,8,4864]{2,1,0:T(8,128)(2,1)S(1)}, u32[]{:S(2)}, u32[]{:S(2)}) %all-to-all-start.1) | async-done | bytes 622624 | tf_op jit(solution)/shard_map/all_to_all | solution.py:541
  51.8 7.1 %after_states.1 = (bf16[8,16,1024]{2,1,0:T(8,128)(2,1)}, f32[128,2048]{1,0:T(8,128)}) custom-call(bf16[8,8,4864]{2,1,0:T(8,128)(2,1)S(1)} %all-to-all-done.1.moved_ref, s32[8,128]{1,0:T(8,128)S(1)} %broadcast_in_dim.59.acc_ref, f32[16,8,128]{2,1,0:T(8,128)S(1)} %get-tuple-element.25.at_ref, f32[104,32]{1,0:T(8,128)S(1)} %get-tuple-element.26.coef_ref, ...), custom_call_target="tpu_custom_call" | custom-call | flops 536870912 | bytes 12582912 | tf_op jit(solution)/shard_map/after_states/pallas_call | solution.py:510
  (23 shorter events, 0.2 us)
Async XLA Ops:
  0.6 14.4 %copy-start.3 = (s32[64]{0:T(128)S(1)}, s32[64]{0:T(128)}, u32[]{:S(2)}) copy-start(s32[64]{0:T(128)} %param.33) | copy-start | bytes 772
  0.6 14.4 %copy-start.4 = (s32[64]{0:T(128)S(1)}, s32[64]{0:T(128)}, u32[]{:S(2)}) copy-start(s32[64]{0:T(128)} %param.31) | copy-start | bytes 772
  0.7 14.4 %copy-start.2 = (s32[64]{0:T(128)S(1)}, s32[64]{0:T(128)}, u32[]{:S(2)}) copy-start(s32[64]{0:T(128)} %param.30) | copy-start | bytes 772
  0.7 14.6 %copy-start = (bf16[8,16,1024]{2,1,0:T(8,128)(2,1)S(1)}, bf16[8,16,1024]{2,1,0:T(8,128)(2,1)}, u32[]{:S(2)}) copy-start(bf16[8,16,1024]{2,1,0:T(8,128)(2,1)} %param.17) | copy-start | bytes 786436
  0.7 17.0 %copy-start.1 = (f32[1024]{0:T(1024)S(1)}, f32[1024]{0:T(1024)}, u32[]{:S(2)}) copy-start(f32[1024]{0:T(1024)} %param.18) | copy-start | bytes 12292
  3.3 11.9 %collective-permute-start.2 = (bf16[1,88,256]{2,1,0:T(8,128)(2,1)S(1)}, bf16[1,88,256]{2,1,0:T(8,128)(2,1)S(1)}, u32[]{:S(2)}, u32[]{:S(2)}) collective-permute-start(bf16[1,88,256]{2,1,0:T(8,128)(2,1)S(1)} %bitcast.28), channel_id=1, source_target_pairs={{0,24},{4,28},{8,16},{12,20},{16,8},{20,12},{24,0},{28,4},{1,25},{... | collective-permute-start | bytes 135176 | tf_op jit(solution)/shard_map/ppermute | solution.py:164
  8.4 6.8 %collective-permute-start.1 = (bf16[1,88,256]{2,1,0:T(8,128)(2,1)S(1)}, bf16[1,88,256]{2,1,0:T(8,128)(2,1)S(1)}, u32[]{:S(2)}, u32[]{:S(2)}) collective-permute-start(bf16[1,88,256]{2,1,0:T(8,128)(2,1)S(1)} %bitcast.29), channel_id=1, source_target_pairs={{0,8},{4,12},{8,0},{12,4},{16,24},{20,28},{24,16},{28,20},{1,9},{5... | collective-permute-start | bytes 135176 | tf_op jit(solution)/shard_map/ppermute | solution.py:164
  8.4 6.8 %collective-permute-start = (bf16[1,88,256]{2,1,0:T(8,128)(2,1)S(1)}, bf16[1,88,256]{2,1,0:T(8,128)(2,1)S(1)}, u32[]{:S(2)}, u32[]{:S(2)}) collective-permute-start(bf16[1,88,256]{2,1,0:T(8,128)(2,1)S(1)} %bitcast.30), channel_id=1, source_target_pairs={{0,16},{4,20},{8,24},{12,28},{16,0},{20,4},{24,8},{28,12},{1,17},{... | collective-permute-start | bytes 135176 | tf_op jit(solution)/shard_map/ppermute | solution.py:164
  9.1 21.7 %all-to-all-start = ((bf16[8,8,4864]{2,1,0:T(8,128)(2,1)}), bf16[8,8,4864]{2,1,0:T(8,128)(2,1)S(1)}, u32[]{:S(2)}, u32[]{:S(2)}) async-start(bf16[8,8,4864]{2,1,0:T(8,128)(2,1)} %get-tuple-element.22), calls=%async_computation | async-start | bytes 1245184 | tf_op jit(solution)/shard_map/all_to_all | solution.py:541
  15.6 10.6 %collective-permute-start.3 = (bf16[4,88,256]{2,1,0:T(8,128)(2,1)S(1)}, bf16[4,88,256]{2,1,0:T(8,128)(2,1)S(1)}, u32[]{:S(2)}, u32[]{:S(2)}) collective-permute-start(bf16[4,88,256]{2,1,0:T(8,128)(2,1)S(1)} %pad_maximum_fusion.2), channel_id=1, source_target_pairs={{0,4},{4,0},{8,12},{12,8},{16,20},{20,16},{24,28},{28,24},{1,5},{5... | collective-permute-start | bytes 540680 | tf_op jit(solution)/shard_map/ppermute | solution.py:164
  26.3 9.4 %copy-start.5 = (s32[64]{0:T(128)S(1)}, s32[64]{0:T(128)}, u32[]{:S(2)}) copy-start(s32[64]{0:T(128)} %param.32) | copy-start | bytes 772
  26.3 9.2 %collective-permute-start.4 = (bf16[1,8,88,256]{3,2,1,0:T(8,128)(2,1)S(1)}, bf16[1,8,88,256]{3,2,1,0:T(8,128)(2,1)S(1)}, u32[]{:S(2)}, u32[]{:S(2)}) collective-permute-start(bf16[1,8,88,256]{3,2,1,0:T(8,128)(2,1)S(1)} %maximum_bitcast_fusion), channel_id=1, source_target_pairs={{0,2},{1,3},{2,0},{3,1},{4,6},{5,7},{6,4},{7,5},{8,10},{9,11},{10,... | collective-permute-start | bytes 1081352 | tf_op jit(solution)/shard_map/ppermute | solution.py:164
  31.9 19.9 %all-to-all-start.1 = ((bf16[8,8,4864]{2,1,0:T(8,128)(2,1)}), bf16[8,8,4864]{2,1,0:T(8,128)(2,1)S(1)}, u32[]{:S(2)}, u32[]{:S(2)}) async-start(bf16[8,8,4864]{2,1,0:T(8,128)(2,1)} %bitcast.32), calls=%async_computation.1 | async-start | bytes 1245184 | tf_op jit(solution)/shard_map/all_to_all | solution.py:541
  35.6 2.4 %collective-permute-start.5 = (bf16[2,8,88,256]{3,2,1,0:T(8,128)(2,1)S(1)}, bf16[2,8,88,256]{3,2,1,0:T(8,128)(2,1)}, u32[]{:S(2)}, u32[]{:S(2)}) collective-permute-start(bf16[2,8,88,256]{3,2,1,0:T(8,128)(2,1)S(1)} %pad_maximum_fusion.1), channel_id=1, source_target_pairs={{0,1},{1,0},{2,3},{3,2},{4,5},{5,4},{6,7},{7,6},{8,9},{9,8},{10,11... | collective-permute-start | bytes 2162696 | tf_op jit(solution)/shard_map/ppermute | solution.py:164

commit v8 on v7

--- a/solution.py
+++ b/solution.py
@@ -618,19 +618,20 @@
     )
     arrived = exchange(packed.reshape(all_reqs, (state_size + span) * channels))
     top = blocks // 2
-    weights = jnp.concatenate(
-        [share[None]] + [moved_by(share[None], "req", bits) for bits in (top, top // 2, top + top // 2)]
-    )
-    hidden, weights = lax.optimization_barrier((hidden, weights))
+    own = share[None]
+    far, near = moved_by(own, "req", top), moved_by(own, "req", top // 2)
+    hidden, far = lax.optimization_barrier((hidden, far))
+    token_major = jnp.swapaxes(hidden, 0, 1).reshape(tokens, width)
+    normed = rms_normed(token_major, norm_gain)
+    projected = jnp.dot(normed, in_weight, preferred_element_type=jnp.float32).astype(jnp.bfloat16)
+    weights = jnp.concatenate([own, far, near, moved_by(far, "req", top // 2)])
+    weights, projected = lax.optimization_barrier((weights, projected))
     weights = doubled(weights, "req", top // 4)[None]
 
     old_slot = jnp.arange(all_reqs, dtype=jnp.int32)
     chosen = (anchor[:, None] == old_slot[None, :]) & (fresh_flag[:, None] == 0)
     masks = jnp.stack([chosen] + [chosen & (span - e <= request_ages)[:, None] for e in range(span)])
-    token_major = jnp.swapaxes(hidden, 0, 1).reshape(tokens, width)
-    normed = rms_normed(token_major, norm_gain)
-    projected = jnp.dot(normed, in_weight, preferred_element_type=jnp.float32).astype(jnp.bfloat16)
-    masks, projected, weights = lax.optimization_barrier((masks.astype(jnp.bfloat16), projected, weights))
+    masks, projected = lax.optimization_barrier((masks.astype(jnp.bfloat16), projected))
     moved = exchange(select(masks, arrived))
 
     q_place, j_place = places("grp"), places("req")

time: 59.3 us -> 59.7 us (level)
  starting transfers between devices: 19.1 us -> 20.9 us
  waiting for transfers between devices: 14.9 us -> 13.5 us
    all_to_all x2, waiting for transfers between devices: 8.9 us -> 3.34 us  [exchange(): lax.all_to_all(values, 'req', split_axis=0, concat_axis=0, tiled=True)]
    ppermute x6, waiting for transfers between devices: 5.97 us -> 10.2 us  [moved_by(): lax.ppermute(values, axis, [(i, i ^ bits) for i in range(lax.axis_size(ax...]
    ppermute x6, starting transfers between devices: 9.49 us -> 11 us  [moved_by(): lax.ppermute(values, axis, [(i, i ^ bits) for i in range(lax.axis_size(ax...]
  transfers between devices with their start and end apart: 8 -> 8, of which waited for: 4 -> 4; matrix products, arithmetic and copies ran while one was open for 12% -> 11% of each run, Pallas kernels for 13% -> 13%
where the time goes in v8:
time: 59.7 us; the launch traced here: 59.3 us
  starting transfers between devices  20.9 us (35%)
  Pallas kernels  17.2 us (29%)
  waiting for transfers between devices  13.5 us (23%)
  matrix products  4.78 us (8%)
  other arithmetic  1.76 us (3%)
  between operations  0.83 us (1%)
    ppermute x6, starting transfers between devices, moved_by(): lax.ppermute(values, axis, [(i, i ^ bits) for i in range(lax.axis_size(ax...  11 us
    ppermute x6, waiting for transfers between devices, moved_by(): lax.ppermute(values, axis, [(i, i ^ bits) for i in range(lax.axis_size(ax...  10.2 us
    all_to_all x2, starting transfers between devices, exchange(): lax.all_to_all(values, 'req', split_axis=0, concat_axis=0, tiled=True)  9.84 us
    pallas_call x1, Pallas kernels, after(): pl.pallas_call(after_kernel, out_shape=(jax.ShapeDtypeStruct((reqs, draft...  7.06 us
    pallas_call x1, Pallas kernels, before(): pl.pallas_call(before_kernel, out_shape=(pltpu.HBM(rows, f32), jax.ShapeD...  6.54 us
    dot_general x1, matrix products, on_device(): jnp.dot(normed, in_weight, preferred_element_type=jnp.float32)  4.78 us
    all_to_all x2, waiting for transfers between devices, exchange(): lax.all_to_all(values, 'req', split_axis=0, concat_axis=0, tiled=True)  3.34 us
    pallas_call x1, Pallas kernels, prepared(): pl.pallas_call(send_kernel, out_shape=(pltpu.HBM((blocks, slots, (states...  2.6 us
  transfers between devices with their start and end apart: 8, of which 4 were waited for; matrix products, arithmetic and copies ran while one was open for 11% of the time, Pallas kernels for 13%

profile of v8, /device:TPU:0, one launch (start us, length us, event | category | flops | bytes accessed | tf_op | source)
XLA Modules:
  0.0 59.3 jit_solution(13743289196895639975)
XLA Ops:
  0.7 2.6 %send_states.1 = (bf16[8,8,4864]{2,1,0:T(8,128)(2,1)}, bf16[88,256]{1,0:T(8,128)(2,1)S(1)}) custom-call(s32[1]{0:T(128)} %bitcast.group_ref, f32[128,2048]{1,0:T(8,128)} %bitcast.32, bf16[3,8,2048]{2,1,0:T(8,128)(2,1)} %bitcast.33, bf16[160,256]{1,0:T(8,128)(2,1)} %bitcast.34, bf16[128,256]{1,0:T(8,128)(2,1)} %sw_ref.1, f32[4,256]{1,0:T(4,128)} %cw_ref.1, ...), custom_call_target="tpu_custom_call" | custom-call | tf_op jit(solution)/shard_map/send_states/pallas_call | solution.py:117
  3.3 4.1 %collective-permute-start = (bf16[1,88,256]{2,1,0:T(8,128)(2,1)S(1)}, bf16[1,88,256]{2,1,0:T(8,128)(2,1)S(1)}, u32[]{:S(2)}, u32[]{:S(2)}) collective-permute-start(bf16[1,88,256]{2,1,0:T(8,128)(2,1)S(1)} %bitcast.28), channel_id=1, source_target_pairs={{0,16},{4,20},{8,24},{12,28},{16,0},{20,4},{24,8},{28,12},{1,17},{... | collective-permute-start | bytes 135176 | tf_op jit(solution)/shard_map/ppermute | solution.py:164
  7.4 1.6 %collective-permute-start.1 = (bf16[1,88,256]{2,1,0:T(8,128)(2,1)S(1)}, bf16[1,88,256]{2,1,0:T(8,128)(2,1)S(1)}, u32[]{:S(2)}, u32[]{:S(2)}) collective-permute-start(bf16[1,88,256]{2,1,0:T(8,128)(2,1)S(1)} %bitcast.29), channel_id=1, source_target_pairs={{0,8},{4,12},{8,0},{12,4},{16,24},{20,28},{24,16},{28,20},{1,9},{5... | collective-permute-start | bytes 135176 | tf_op jit(solution)/shard_map/ppermute | solution.py:164
  8.9 3.5 %all-to-all-start = ((bf16[8,8,4864]{2,1,0:T(8,128)(2,1)}), bf16[8,8,4864]{2,1,0:T(8,128)(2,1)S(1)}, u32[]{:S(2)}, u32[]{:S(2)}) async-start(bf16[8,8,4864]{2,1,0:T(8,128)(2,1)} %get-tuple-element.24), calls=%async_computation | async-start | bytes 1245184 | tf_op jit(solution)/shard_map/all_to_all | solution.py:541
  12.5 0.2 fusion.3
  12.7 0.1 rsqrt.12
  12.9 2.0 %collective-permute-start.2 = (bf16[1,88,256]{2,1,0:T(8,128)(2,1)S(1)}, bf16[1,88,256]{2,1,0:T(8,128)(2,1)S(1)}, u32[]{:S(2)}, u32[]{:S(2)}) collective-permute-start(bf16[1,88,256]{2,1,0:T(8,128)(2,1)S(1)} %collective-permute-done), channel_id=1, source_target_pairs={{0,8},{4,12},{8,0},{12,4},{16,24},{20,28},{24,16},{28,20},{1,9},{5... | collective-permute-start | bytes 135176 | tf_op jit(solution)/shard_map/ppermute | solution.py:164
  14.9 4.8 %convolution_convert_fusion.proj_ref = bf16[128,4096]{1,0:T(8,128)(2,1)S(1)} fusion(bf16[1024,4096]{1,0:T(8,128)(2,1)} %param.19, f32[1024]{0:T(1024)S(1)} %copy-done.1, f32[128]{0:T(128)S(1)} %rsqrt.12, bf16[8,16,1024]{2,1,0:T(8,128)(2,1)S(1)} %copy-done), kind=kOutput, calls=%fused_computation | convolution fusion | flops 1074790400 | bytes 9703936 | tf_op jit(solution)/shard_map/dot_general | solution.py:626
  19.7 3.7 %collective-permute-done.2 = bf16[1,88,256]{2,1,0:T(8,128)(2,1)S(1)} collective-permute-done((bf16[1,88,256]{2,1,0:T(8,128)(2,1)S(1)}, bf16[1,88,256]{2,1,0:T(8,128)(2,1)S(1)}, u32[]{:S(2)}, u32[]{:S(2)}) %collective-permute-start.2) | collective-permute-done | bytes 45088 | tf_op jit(solution)/shard_map/ppermute | solution.py:164
  23.4 1.7 %collective-permute-start.3 = (bf16[4,88,256]{2,1,0:T(8,128)(2,1)S(1)}, bf16[4,88,256]{2,1,0:T(8,128)(2,1)S(1)}, u32[]{:S(2)}, u32[]{:S(2)}) collective-permute-start(bf16[4,88,256]{2,1,0:T(8,128)(2,1)S(1)} %pad_maximum_fusion.2), channel_id=1, source_target_pairs={{0,4},{4,0},{8,12},{12,8},{16,20},{20,16},{24,28},{28,24},{1,5},{5... | collective-permute-start | bytes 540680 | tf_op jit(solution)/shard_map/ppermute | solution.py:164
  25.2 4.3 %collective-permute-done.3 = bf16[4,88,256]{2,1,0:T(8,128)(2,1)S(1)} collective-permute-done((bf16[4,88,256]{2,1,0:T(8,128)(2,1)S(1)}, bf16[4,88,256]{2,1,0:T(8,128)(2,1)S(1)}, u32[]{:S(2)}, u32[]{:S(2)}) %collective-permute-start.3) | collective-permute-done | bytes 180256 | tf_op jit(solution)/shard_map/ppermute | solution.py:164
  29.5 1.6 %collective-permute-start.4 = (bf16[1,8,88,256]{3,2,1,0:T(8,128)(2,1)S(1)}, bf16[1,8,88,256]{3,2,1,0:T(8,128)(2,1)S(1)}, u32[]{:S(2)}, u32[]{:S(2)}) collective-permute-start(bf16[1,8,88,256]{3,2,1,0:T(8,128)(2,1)S(1)} %maximum_bitcast_fusion), channel_id=1, source_target_pairs={{0,2},{1,3},{2,0},{3,1},{4,6},{5,7},{6,4},{7,5},{8,10},{9,11},{10,... | collective-permute-start | bytes 1081352 | tf_op jit(solution)/shard_map/ppermute | solution.py:164
  31.0 0.1 fusion.8
  31.2 1.0 %select_slots.1 = bf16[64,4864]{1,0:T(8,128)(2,1)} custom-call(bf16[4,64,64]{2,1,0:T(8,128)(2,1)S(1)} %add_convert_fusion.mask_ref, bf16[64,4864]{1,0:T(8,128)(2,1)S(1)} %bitcast.27), custom_call_target="tpu_custom_call" | custom-call | tf_op jit(solution)/shard_map/select_slots/pallas_call | solution.py:565
  32.2 6.3 %all-to-all-start.1 = ((bf16[8,8,4864]{2,1,0:T(8,128)(2,1)}), bf16[8,8,4864]{2,1,0:T(8,128)(2,1)S(1)}, u32[]{:S(2)}, u32[]{:S(2)}) async-start(bf16[8,8,4864]{2,1,0:T(8,128)(2,1)} %bitcast.31), calls=%async_computation.1 | async-start | bytes 1245184 | tf_op jit(solution)/shard_map/all_to_all | solution.py:541
  38.6 0.1 pad_maximum_fusion.1
  38.6 0.1 collective-permute-start.5
  38.7 0.1 dynamic_slice.3
  38.8 2.2 %collective-permute-done.5 = bf16[2,8,88,256]{3,2,1,0:T(8,128)(2,1)} collective-permute-done((bf16[2,8,88,256]{3,2,1,0:T(8,128)(2,1)S(1)}, bf16[2,8,88,256]{3,2,1,0:T(8,128)(2,1)}, u32[]{:S(2)}, u32[]{:S(2)}) %collective-permute-start.5) | collective-permute-done | bytes 720928 | tf_op jit(solution)/shard_map/ppermute | solution.py:164
  41.0 1.3 %pad_maximum_fusion.w_ref = bf16[4,8,88,256]{3,2,1,0:T(8,128)(2,1)S(1)} fusion(bf16[2,8,88,256]{3,2,1,0:T(8,128)(2,1)} %collective-permute-done.5, bf16[1,8,88,256]{3,2,1,0:T(8,128)(2,1)S(1)} %collective-permute-done.4, bf16[1,8,88,256]{3,2,1,0:T(8,128)(2,1)S(1)} %maximum_bitcast_fusion), kind=kLoop, calls=%fused_computation.1 | loop fusion | flops 1441792 | bytes 2883584 | tf_op jit(solution)/shard_map/concatenate | solution.py:169
  42.3 0.1 broadcast_in_dim.55.acc_ref
  42.3 6.5 %before_states.1 = (f32[16,464,128]{2,1,0:T(8,128)}, f32[16,8,128]{2,1,0:T(8,128)S(1)}, f32[104,32]{1,0:T(8,128)S(1)}, bf16[8,160,256]{2,1,0:T(8,128)(2,1)S(1)},...) custom-call(s32[4]{0:T(128)S(1)} %fusion.9.q_ref, s32[8]{0:T(128)S(1)} %fusion.11.j_ref, ...), custom_call_target="tpu_custom_call" | custom-call | flops 200000000 | bytes 8388608 | tf_op jit(solution)/shard_map/before_states/pallas_call | solution.py:334
  48.9 3.3 %all-to-all-done.1.moved_ref = bf16[8,8,4864]{2,1,0:T(8,128)(2,1)S(1)} async-done(((bf16[8,8,4864]{2,1,0:T(8,128)(2,1)}), bf16[8,8,4864]{2,1,0:T(8,128)(2,1)S(1)}, u32[]{:S(2)}, u32[]{:S(2)}) %all-to-all-start.1) | async-done | bytes 622624 | tf_op jit(solution)/shard_map/all_to_all | solution.py:541
  52.2 7.1 %after_states.1 = (bf16[8,16,1024]{2,1,0:T(8,128)(2,1)}, f32[128,2048]{1,0:T(8,128)}) custom-call(bf16[8,8,4864]{2,1,0:T(8,128)(2,1)S(1)} %all-to-all-done.1.moved_ref, s32[8,128]{1,0:T(8,128)S(1)} %broadcast_in_dim.55.acc_ref, f32[16,8,128]{2,1,0:T(8,128)S(1)} %get-tuple-element.27.at_ref, f32[104,32]{1,0:T(8,128)S(1)} %get-tuple-element.28.coef_ref, ...), custom_call_target="tpu_custom_call" | custom-call | flops 536870912 | bytes 12582912 | tf_op jit(solution)/shard_map/after_states/pallas_call | solution.py:510
  (23 shorter events, 0.2 us)
Async XLA Ops:
  0.6 11.9 %copy-start = (bf16[8,16,1024]{2,1,0:T(8,128)(2,1)S(1)}, bf16[8,16,1024]{2,1,0:T(8,128)(2,1)}, u32[]{:S(2)}) copy-start(bf16[8,16,1024]{2,1,0:T(8,128)(2,1)} %param.17) | copy-start | bytes 786436
  0.6 14.2 %copy-start.1 = (f32[1024]{0:T(1024)S(1)}, f32[1024]{0:T(1024)}, u32[]{:S(2)}) copy-start(f32[1024]{0:T(1024)} %param.18) | copy-start | bytes 12292
  3.3 9.2 %collective-permute-start = (bf16[1,88,256]{2,1,0:T(8,128)(2,1)S(1)}, bf16[1,88,256]{2,1,0:T(8,128)(2,1)S(1)}, u32[]{:S(2)}, u32[]{:S(2)}) collective-permute-start(bf16[1,88,256]{2,1,0:T(8,128)(2,1)S(1)} %bitcast.28), channel_id=1, source_target_pairs={{0,16},{4,20},{8,24},{12,28},{16,0},{20,4},{24,8},{28,12},{1,17},{... | collective-permute-start | bytes 135176 | tf_op jit(solution)/shard_map/ppermute | solution.py:164
  7.4 12.3 %collective-permute-start.1 = (bf16[1,88,256]{2,1,0:T(8,128)(2,1)S(1)}, bf16[1,88,256]{2,1,0:T(8,128)(2,1)S(1)}, u32[]{:S(2)}, u32[]{:S(2)}) collective-permute-start(bf16[1,88,256]{2,1,0:T(8,128)(2,1)S(1)} %bitcast.29), channel_id=1, source_target_pairs={{0,8},{4,12},{8,0},{12,4},{16,24},{20,28},{24,16},{28,20},{1,9},{5... | collective-permute-start | bytes 135176 | tf_op jit(solution)/shard_map/ppermute | solution.py:164
  8.9 22.2 %all-to-all-start = ((bf16[8,8,4864]{2,1,0:T(8,128)(2,1)}), bf16[8,8,4864]{2,1,0:T(8,128)(2,1)S(1)}, u32[]{:S(2)}, u32[]{:S(2)}) async-start(bf16[8,8,4864]{2,1,0:T(8,128)(2,1)} %get-tuple-element.24), calls=%async_computation | async-start | bytes 1245184 | tf_op jit(solution)/shard_map/all_to_all | solution.py:541
  12.8 12.3 %copy-start.3 = (s32[64]{0:T(128)S(1)}, s32[64]{0:T(128)}, u32[]{:S(2)}) copy-start(s32[64]{0:T(128)} %param.33) | copy-start | bytes 772
  12.9 12.3 %copy-start.4 = (s32[64]{0:T(128)S(1)}, s32[64]{0:T(128)}, u32[]{:S(2)}) copy-start(s32[64]{0:T(128)} %param.31) | copy-start | bytes 772
  12.9 18.2 %copy-start.2 = (s32[64]{0:T(128)S(1)}, s32[64]{0:T(128)}, u32[]{:S(2)}) copy-start(s32[64]{0:T(128)} %param.30) | copy-start | bytes 772
  12.9 10.5 %collective-permute-start.2 = (bf16[1,88,256]{2,1,0:T(8,128)(2,1)S(1)}, bf16[1,88,256]{2,1,0:T(8,128)(2,1)S(1)}, u32[]{:S(2)}, u32[]{:S(2)}) collective-permute-start(bf16[1,88,256]{2,1,0:T(8,128)(2,1)S(1)} %collective-permute-done), channel_id=1, source_target_pairs={{0,8},{4,12},{8,0},{12,4},{16,24},{20,28},{24,16},{28,20},{1,9},{5... | collective-permute-start | bytes 135176 | tf_op jit(solution)/shard_map/ppermute | solution.py:164
  23.4 6.0 %collective-permute-start.3 = (bf16[4,88,256]{2,1,0:T(8,128)(2,1)S(1)}, bf16[4,88,256]{2,1,0:T(8,128)(2,1)S(1)}, u32[]{:S(2)}, u32[]{:S(2)}) collective-permute-start(bf16[4,88,256]{2,1,0:T(8,128)(2,1)S(1)} %pad_maximum_fusion.2), channel_id=1, source_target_pairs={{0,4},{4,0},{8,12},{12,8},{16,20},{20,16},{24,28},{28,24},{1,5},{5... | collective-permute-start | bytes 540680 | tf_op jit(solution)/shard_map/ppermute | solution.py:164
  29.4 9.3 %copy-start.5 = (s32[64]{0:T(128)S(1)}, s32[64]{0:T(128)}, u32[]{:S(2)}) copy-start(s32[64]{0:T(128)} %param.32) | copy-start | bytes 772
  29.5 9.1 %collective-permute-start.4 = (bf16[1,8,88,256]{3,2,1,0:T(8,128)(2,1)S(1)}, bf16[1,8,88,256]{3,2,1,0:T(8,128)(2,1)S(1)}, u32[]{:S(2)}, u32[]{:S(2)}) collective-permute-start(bf16[1,8,88,256]{3,2,1,0:T(8,128)(2,1)S(1)} %maximum_bitcast_fusion), channel_id=1, source_target_pairs={{0,2},{1,3},{2,0},{3,1},{4,6},{5,7},{6,4},{7,5},{8,10},{9,11},{10,... | collective-permute-start | bytes 1081352 | tf_op jit(solution)/shard_map/ppermute | solution.py:164
  32.2 20.0 %all-to-all-start.1 = ((bf16[8,8,4864]{2,1,0:T(8,128)(2,1)}), bf16[8,8,4864]{2,1,0:T(8,128)(2,1)S(1)}, u32[]{:S(2)}, u32[]{:S(2)}) async-start(bf16[8,8,4864]{2,1,0:T(8,128)(2,1)} %bitcast.31), calls=%async_computation.1 | async-start | bytes 1245184 | tf_op jit(solution)/shard_map/all_to_all | solution.py:541
  38.6 2.4 %collective-permute-start.5 = (bf16[2,8,88,256]{3,2,1,0:T(8,128)(2,1)S(1)}, bf16[2,8,88,256]{3,2,1,0:T(8,128)(2,1)}, u32[]{:S(2)}, u32[]{:S(2)}) collective-permute-start(bf16[2,8,88,256]{3,2,1,0:T(8,128)(2,1)S(1)} %pad_maximum_fusion.1), channel_id=1, source_target_pairs={{0,1},{1,0},{2,3},{3,2},{4,5},{5,4},{6,7},{7,6},{8,9},{9,8},{10,11... | collective-permute-start | bytes 2162696 | tf_op jit(solution)/shard_map/ppermute | solution.py:164

commit v9 on v8

--- a/solution.py
+++ b/solution.py
@@ -164,21 +164,22 @@
     return lax.ppermute(values, axis, [(i, i ^ bits) for i in range(lax.axis_size(axis))])
 
 
-def doubled(values, axis, bit):
-    while bit:
+def doubled(values, axis, bits):
+    for bit in bits:
         values = jnp.concatenate([values, moved_by(values, axis, bit)], axis=0)
-        bit //= 2
     return values
 
 
-def places(axis):
+def halvings(size):
+    return [size >> k for k in range(1, size.bit_length())]
+
+
+def places(axis, bits):
     size = lax.axis_size(axis)
     offset = jnp.arange(size, dtype=jnp.int32) ^ lax.axis_index(axis).astype(jnp.int32)
     place = jnp.zeros_like(offset)
-    bit, top = 1, size // 2
-    while top:
-        place = place | jnp.where((offset & bit) != 0, top, 0)
-        bit, top = bit * 2, top // 2
+    for k, bit in enumerate(bits):
+        place = place | jnp.where((offset & bit) != 0, 1 << k, 0)
     return place
 
 
@@ -617,16 +618,17 @@
         old_states, old_edges, x_weight, step_weight, conv_weight, conv_bias, step_bias, skip_gain, log_decay
     )
     arrived = exchange(packed.reshape(all_reqs, (state_size + span) * channels))
-    top = blocks // 2
+    order = halvings(blocks)
+    order = [order[0], order[-1]] + order[1:-1]
     own = share[None]
-    far, near = moved_by(own, "req", top), moved_by(own, "req", top // 2)
+    far, near = moved_by(own, "req", order[0]), moved_by(own, "req", order[1])
     hidden, far = lax.optimization_barrier((hidden, far))
     token_major = jnp.swapaxes(hidden, 0, 1).reshape(tokens, width)
     normed = rms_normed(token_major, norm_gain)
     projected = jnp.dot(normed, in_weight, preferred_element_type=jnp.float32).astype(jnp.bfloat16)
-    weights = jnp.concatenate([own, far, near, moved_by(far, "req", top // 2)])
+    weights = jnp.concatenate([own, far, near, moved_by(far, "req", order[1])])
     weights, projected = lax.optimization_barrier((weights, projected))
-    weights = doubled(weights, "req", top // 4)[None]
+    weights = doubled(weights, "req", order[2:])[None]
 
     old_slot = jnp.arange(all_reqs, dtype=jnp.int32)
     chosen = (anchor[:, None] == old_slot[None, :]) & (fresh_flag[:, None] == 0)
@@ -634,8 +636,8 @@
     masks, projected = lax.optimization_barrier((masks.astype(jnp.bfloat16), projected))
     moved = exchange(select(masks, arrived))
 
-    q_place, j_place = places("grp"), places("req")
-    weights = doubled(weights, "grp", groups // 2)
+    q_place, j_place = places("grp", halvings(groups)), places("req", order)
+    weights = doubled(weights, "grp", halvings(groups))
     if channels != BLOCK:
         moved = moved.reshape(blocks, local_reqs, state_size + span, channels).transpose(1, 2, 0, 3)
         moved = moved.reshape(local_reqs, state_size + span, -1, BLOCK).transpose(2, 0, 1, 3)

time: 59.7 us -> 58.5 us (0.980)
  starting transfers between devices: 20.9 us -> 19.8 us
    ppermute x6, waiting for transfers between devices: 10.2 us -> 8.53 us  [moved_by(): lax.ppermute(values, axis, [(i, i ^ bits) for i in range(lax.axis_size(ax...]
    all_to_all x2, waiting for transfers between devices: 3.34 us -> 4.85 us  [exchange(): lax.all_to_all(values, 'req', split_axis=0, concat_axis=0, tiled=True)]
    all_to_all x2, starting transfers between devices: 9.84 us -> 9.08 us  [exchange(): lax.all_to_all(values, 'req', split_axis=0, concat_axis=0, tiled=True)]
  transfers between devices with their start and end apart: 8 -> 8, of which waited for: 4 -> 3; matrix products, arithmetic and copies ran while one was open for 11% -> 12% of each run, Pallas kernels for 13% -> 13%
where the time goes in v9:
time: 58.5 us; the launch traced here: 58.1 us
  starting transfers between devices  19.8 us (34%)
  Pallas kernels  17.2 us (29%)
  waiting for transfers between devices  13.4 us (23%)
  matrix products  4.78 us (8%)
  other arithmetic  1.76 us (3%)
  between operations  0.84 us (1%)
    ppermute x6, starting transfers between devices, moved_by(): lax.ppermute(values, axis, [(i, i ^ bits) for i in range(lax.axis_size(ax...  10.8 us
    all_to_all x2, starting transfers between devices, exchange(): lax.all_to_all(values, 'req', split_axis=0, concat_axis=0, tiled=True)  9.08 us
    ppermute x6, waiting for transfers between devices, moved_by(): lax.ppermute(values, axis, [(i, i ^ bits) for i in range(lax.axis_size(ax...  8.53 us
    pallas_call x1, Pallas kernels, after(): pl.pallas_call(after_kernel, out_shape=(jax.ShapeDtypeStruct((reqs, draft...  7.06 us
    pallas_call x1, Pallas kernels, before(): pl.pallas_call(before_kernel, out_shape=(pltpu.HBM(rows, f32), jax.ShapeD...  6.54 us
    all_to_all x2, waiting for transfers between devices, exchange(): lax.all_to_all(values, 'req', split_axis=0, concat_axis=0, tiled=True)  4.85 us
    dot_general x1, matrix products, on_device(): jnp.dot(normed, in_weight, preferred_element_type=jnp.float32)  4.78 us
    pallas_call x1, Pallas kernels, prepared(): pl.pallas_call(send_kernel, out_shape=(pltpu.HBM((blocks, slots, (states...  2.6 us
  transfers between devices with their start and end apart: 8, of which 3 were waited for; matrix products, arithmetic and copies ran while one was open for 12% of the time, Pallas kernels for 13%

profile of v9, /device:TPU:0, one launch (start us, length us, event | category | flops | bytes accessed | tf_op | source)
XLA Modules:
  0.0 58.1 jit_solution(16552840696525037068)
XLA Ops:
  0.7 2.6 %send_states.1 = (bf16[8,8,4864]{2,1,0:T(8,128)(2,1)}, bf16[88,256]{1,0:T(8,128)(2,1)S(1)}) custom-call(s32[1]{0:T(128)} %bitcast.group_ref, f32[128,2048]{1,0:T(8,128)} %bitcast.32, bf16[3,8,2048]{2,1,0:T(8,128)(2,1)} %bitcast.33, bf16[160,256]{1,0:T(8,128)(2,1)} %bitcast.34, bf16[128,256]{1,0:T(8,128)(2,1)} %sw_ref.1, f32[4,256]{1,0:T(4,128)} %cw_ref.1, ...), custom_call_target="tpu_custom_call" | custom-call | tf_op jit(solution)/shard_map/send_states/pallas_call | solution.py:117
  3.3 4.1 %collective-permute-start = (bf16[1,88,256]{2,1,0:T(8,128)(2,1)S(1)}, bf16[1,88,256]{2,1,0:T(8,128)(2,1)S(1)}, u32[]{:S(2)}, u32[]{:S(2)}) collective-permute-start(bf16[1,88,256]{2,1,0:T(8,128)(2,1)S(1)} %bitcast.28), channel_id=1, source_target_pairs={{0,16},{4,20},{8,24},{12,28},{16,0},{20,4},{24,8},{28,12},{1,17},{... | collective-permute-start | bytes 135176 | tf_op jit(solution)/shard_map/ppermute | solution.py:164
  7.4 1.5 %collective-permute-start.1 = (bf16[1,88,256]{2,1,0:T(8,128)(2,1)S(1)}, bf16[1,88,256]{2,1,0:T(8,128)(2,1)S(1)}, u32[]{:S(2)}, u32[]{:S(2)}) collective-permute-start(bf16[1,88,256]{2,1,0:T(8,128)(2,1)S(1)} %bitcast.29), channel_id=1, source_target_pairs={{0,4},{4,0},{8,12},{12,8},{16,20},{20,16},{24,28},{28,24},{1,5},{5... | collective-permute-start | bytes 135176 | tf_op jit(solution)/shard_map/ppermute | solution.py:164
  8.9 3.5 %all-to-all-start = ((bf16[8,8,4864]{2,1,0:T(8,128)(2,1)}), bf16[8,8,4864]{2,1,0:T(8,128)(2,1)S(1)}, u32[]{:S(2)}, u32[]{:S(2)}) async-start(bf16[8,8,4864]{2,1,0:T(8,128)(2,1)} %get-tuple-element.24), calls=%async_computation | async-start | bytes 1245184 | tf_op jit(solution)/shard_map/all_to_all | solution.py:542
  12.4 0.2 fusion.3
  12.7 0.1 rsqrt.12
  12.8 0.0 copy-start.3
  12.8 2.0 %collective-permute-start.2 = (bf16[1,88,256]{2,1,0:T(8,128)(2,1)S(1)}, bf16[1,88,256]{2,1,0:T(8,128)(2,1)S(1)}, u32[]{:S(2)}, u32[]{:S(2)}) collective-permute-start(bf16[1,88,256]{2,1,0:T(8,128)(2,1)S(1)} %collective-permute-done), channel_id=1, source_target_pairs={{0,4},{4,0},{8,12},{12,8},{16,20},{20,16},{24,28},{28,24},{1,5},{5... | collective-permute-start | bytes 135176 | tf_op jit(solution)/shard_map/ppermute | solution.py:164
  14.8 4.8 %convolution_convert_fusion.proj_ref = bf16[128,4096]{1,0:T(8,128)(2,1)S(1)} fusion(bf16[1024,4096]{1,0:T(8,128)(2,1)} %param.19, f32[1024]{0:T(1024)S(1)} %copy-done.1, f32[128]{0:T(128)S(1)} %rsqrt.12, bf16[8,16,1024]{2,1,0:T(8,128)(2,1)S(1)} %copy-done), kind=kOutput, calls=%fused_computation | convolution fusion | flops 1074790400 | bytes 9703936 | tf_op jit(solution)/shard_map/dot_general | solution.py:628
  19.6 1.5 %collective-permute-start.3 = (bf16[4,88,256]{2,1,0:T(8,128)(2,1)S(1)}, bf16[4,88,256]{2,1,0:T(8,128)(2,1)S(1)}, u32[]{:S(2)}, u32[]{:S(2)}) collective-permute-start(bf16[4,88,256]{2,1,0:T(8,128)(2,1)S(1)} %pad_maximum_fusion.2), channel_id=1, source_target_pairs={{0,8},{4,12},{8,0},{12,4},{16,24},{20,28},{24,16},{28,20},{1,9},{5... | collective-permute-start | bytes 540680 | tf_op jit(solution)/shard_map/ppermute | solution.py:164
  21.2 6.3 %collective-permute-done.3 = bf16[4,88,256]{2,1,0:T(8,128)(2,1)S(1)} collective-permute-done((bf16[4,88,256]{2,1,0:T(8,128)(2,1)S(1)}, bf16[4,88,256]{2,1,0:T(8,128)(2,1)S(1)}, u32[]{:S(2)}, u32[]{:S(2)}) %collective-permute-start.3) | collective-permute-done | bytes 180256 | tf_op jit(solution)/shard_map/ppermute | solution.py:164
  27.5 1.6 %collective-permute-start.4 = (bf16[1,8,88,256]{3,2,1,0:T(8,128)(2,1)S(1)}, bf16[1,8,88,256]{3,2,1,0:T(8,128)(2,1)S(1)}, u32[]{:S(2)}, u32[]{:S(2)}) collective-permute-start(bf16[1,8,88,256]{3,2,1,0:T(8,128)(2,1)S(1)} %maximum_bitcast_fusion), channel_id=1, source_target_pairs={{0,2},{1,3},{2,0},{3,1},{4,6},{5,7},{6,4},{7,5},{8,10},{9,11},{10,... | collective-permute-start | bytes 1081352 | tf_op jit(solution)/shard_map/ppermute | solution.py:164
  29.1 0.1 fusion.8
  29.3 1.0 %select_slots.1 = bf16[64,4864]{1,0:T(8,128)(2,1)} custom-call(bf16[4,64,64]{2,1,0:T(8,128)(2,1)S(1)} %add_convert_fusion.mask_ref, bf16[64,4864]{1,0:T(8,128)(2,1)S(1)} %bitcast.27), custom_call_target="tpu_custom_call" | custom-call | tf_op jit(solution)/shard_map/select_slots/pallas_call | solution.py:566
  30.3 5.5 %all-to-all-start.1 = ((bf16[8,8,4864]{2,1,0:T(8,128)(2,1)}), bf16[8,8,4864]{2,1,0:T(8,128)(2,1)S(1)}, u32[]{:S(2)}, u32[]{:S(2)}) async-start(bf16[8,8,4864]{2,1,0:T(8,128)(2,1)} %bitcast.31), calls=%async_computation.1 | async-start | bytes 1245184 | tf_op jit(solution)/shard_map/all_to_all | solution.py:542
  35.9 0.1 pad_maximum_fusion.1
  35.9 0.1 collective-permute-start.5
  36.0 0.1 dynamic_slice.3
  36.1 2.2 %collective-permute-done.5 = bf16[2,8,88,256]{3,2,1,0:T(8,128)(2,1)} collective-permute-done((bf16[2,8,88,256]{3,2,1,0:T(8,128)(2,1)S(1)}, bf16[2,8,88,256]{3,2,1,0:T(8,128)(2,1)}, u32[]{:S(2)}, u32[]{:S(2)}) %collective-permute-start.5) | collective-permute-done | bytes 720928 | tf_op jit(solution)/shard_map/ppermute | solution.py:164
  38.3 1.3 %pad_maximum_fusion.w_ref = bf16[4,8,88,256]{3,2,1,0:T(8,128)(2,1)S(1)} fusion(bf16[2,8,88,256]{3,2,1,0:T(8,128)(2,1)} %collective-permute-done.5, bf16[1,8,88,256]{3,2,1,0:T(8,128)(2,1)S(1)} %collective-permute-done.4, bf16[1,8,88,256]{3,2,1,0:T(8,128)(2,1)S(1)} %maximum_bitcast_fusion), kind=kLoop, calls=%fused_computation.1 | loop fusion | flops 1441792 | bytes 2883584 | tf_op jit(solution)/shard_map/concatenate | solution.py:169
  39.6 0.1 broadcast_in_dim.57.acc_ref
  39.7 6.5 %before_states.1 = (f32[16,464,128]{2,1,0:T(8,128)}, f32[16,8,128]{2,1,0:T(8,128)S(1)}, f32[104,32]{1,0:T(8,128)S(1)}, bf16[8,160,256]{2,1,0:T(8,128)(2,1)S(1)},...) custom-call(s32[4]{0:T(128)S(1)} %fusion.9.q_ref, s32[8]{0:T(128)S(1)} %fusion.11.j_ref, ...), custom_call_target="tpu_custom_call" | custom-call | flops 200000000 | bytes 8388608 | tf_op jit(solution)/shard_map/before_states/pallas_call | solution.py:335
  46.2 4.9 %all-to-all-done.1.moved_ref = bf16[8,8,4864]{2,1,0:T(8,128)(2,1)S(1)} async-done(((bf16[8,8,4864]{2,1,0:T(8,128)(2,1)}), bf16[8,8,4864]{2,1,0:T(8,128)(2,1)S(1)}, u32[]{:S(2)}, u32[]{:S(2)}) %all-to-all-start.1) | async-done | bytes 622624 | tf_op jit(solution)/shard_map/all_to_all | solution.py:542
  51.1 7.1 %after_states.1 = (bf16[8,16,1024]{2,1,0:T(8,128)(2,1)}, f32[128,2048]{1,0:T(8,128)}) custom-call(bf16[8,8,4864]{2,1,0:T(8,128)(2,1)S(1)} %all-to-all-done.1.moved_ref, s32[8,128]{1,0:T(8,128)S(1)} %broadcast_in_dim.57.acc_ref, f32[16,8,128]{2,1,0:T(8,128)S(1)} %get-tuple-element.27.at_ref, f32[104,32]{1,0:T(8,128)S(1)} %get-tuple-element.28.coef_ref, ...), custom_call_target="tpu_custom_call" | custom-call | flops 536870912 | bytes 12582912 | tf_op jit(solution)/shard_map/after_states/pallas_call | solution.py:511
  (23 shorter events, 0.2 us)
Async XLA Ops:
  0.6 11.8 %copy-start = (bf16[8,16,1024]{2,1,0:T(8,128)(2,1)S(1)}, bf16[8,16,1024]{2,1,0:T(8,128)(2,1)}, u32[]{:S(2)}) copy-start(bf16[8,16,1024]{2,1,0:T(8,128)(2,1)} %param.17) | copy-start | bytes 786436
  0.6 14.1 %copy-start.1 = (f32[1024]{0:T(1024)S(1)}, f32[1024]{0:T(1024)}, u32[]{:S(2)}) copy-start(f32[1024]{0:T(1024)} %param.18) | copy-start | bytes 12292
  3.3 9.1 %collective-permute-start = (bf16[1,88,256]{2,1,0:T(8,128)(2,1)S(1)}, bf16[1,88,256]{2,1,0:T(8,128)(2,1)S(1)}, u32[]{:S(2)}, u32[]{:S(2)}) collective-permute-start(bf16[1,88,256]{2,1,0:T(8,128)(2,1)S(1)} %bitcast.28), channel_id=1, source_target_pairs={{0,16},{4,20},{8,24},{12,28},{16,0},{20,4},{24,8},{28,12},{1,17},{... | collective-permute-start | bytes 135176 | tf_op jit(solution)/shard_map/ppermute | solution.py:164
  7.4 12.2 %collective-permute-start.1 = (bf16[1,88,256]{2,1,0:T(8,128)(2,1)S(1)}, bf16[1,88,256]{2,1,0:T(8,128)(2,1)S(1)}, u32[]{:S(2)}, u32[]{:S(2)}) collective-permute-start(bf16[1,88,256]{2,1,0:T(8,128)(2,1)S(1)} %bitcast.29), channel_id=1, source_target_pairs={{0,4},{4,0},{8,12},{12,8},{16,20},{20,16},{24,28},{28,24},{1,5},{5... | collective-permute-start | bytes 135176 | tf_op jit(solution)/shard_map/ppermute | solution.py:164
  8.9 20.4 %all-to-all-start = ((bf16[8,8,4864]{2,1,0:T(8,128)(2,1)}), bf16[8,8,4864]{2,1,0:T(8,128)(2,1)S(1)}, u32[]{:S(2)}, u32[]{:S(2)}) async-start(bf16[8,8,4864]{2,1,0:T(8,128)(2,1)} %get-tuple-element.24), calls=%async_computation | async-start | bytes 1245184 | tf_op jit(solution)/shard_map/all_to_all | solution.py:542
  12.8 8.4 %copy-start.3 = (s32[64]{0:T(128)S(1)}, s32[64]{0:T(128)}, u32[]{:S(2)}) copy-start(s32[64]{0:T(128)} %param.33) | copy-start | bytes 772
  12.8 8.4 %copy-start.4 = (s32[64]{0:T(128)S(1)}, s32[64]{0:T(128)}, u32[]{:S(2)}) copy-start(s32[64]{0:T(128)} %param.31) | copy-start | bytes 772
  12.8 16.3 %copy-start.2 = (s32[64]{0:T(128)S(1)}, s32[64]{0:T(128)}, u32[]{:S(2)}) copy-start(s32[64]{0:T(128)} %param.30) | copy-start | bytes 772
  12.8 6.8 %collective-permute-start.2 = (bf16[1,88,256]{2,1,0:T(8,128)(2,1)S(1)}, bf16[1,88,256]{2,1,0:T(8,128)(2,1)S(1)}, u32[]{:S(2)}, u32[]{:S(2)}) collective-permute-start(bf16[1,88,256]{2,1,0:T(8,128)(2,1)S(1)} %collective-permute-done), channel_id=1, source_target_pairs={{0,4},{4,0},{8,12},{12,8},{16,20},{20,16},{24,28},{28,24},{1,5},{5... | collective-permute-start | bytes 135176 | tf_op jit(solution)/shard_map/ppermute | solution.py:164
  19.6 7.9 %collective-permute-start.3 = (bf16[4,88,256]{2,1,0:T(8,128)(2,1)S(1)}, bf16[4,88,256]{2,1,0:T(8,128)(2,1)S(1)}, u32[]{:S(2)}, u32[]{:S(2)}) collective-permute-start(bf16[4,88,256]{2,1,0:T(8,128)(2,1)S(1)} %pad_maximum_fusion.2), channel_id=1, source_target_pairs={{0,8},{4,12},{8,0},{12,4},{16,24},{20,28},{24,16},{28,20},{1,9},{5... | collective-permute-start | bytes 540680 | tf_op jit(solution)/shard_map/ppermute | solution.py:164
  27.5 8.5 %copy-start.5 = (s32[64]{0:T(128)S(1)}, s32[64]{0:T(128)}, u32[]{:S(2)}) copy-start(s32[64]{0:T(128)} %param.32) | copy-start | bytes 772
  27.5 8.3 %collective-permute-start.4 = (bf16[1,8,88,256]{3,2,1,0:T(8,128)(2,1)S(1)}, bf16[1,8,88,256]{3,2,1,0:T(8,128)(2,1)S(1)}, u32[]{:S(2)}, u32[]{:S(2)}) collective-permute-start(bf16[1,8,88,256]{3,2,1,0:T(8,128)(2,1)S(1)} %maximum_bitcast_fusion), channel_id=1, source_target_pairs={{0,2},{1,3},{2,0},{3,1},{4,6},{5,7},{6,4},{7,5},{8,10},{9,11},{10,... | collective-permute-start | bytes 1081352 | tf_op jit(solution)/shard_map/ppermute | solution.py:164
  30.3 20.7 %all-to-all-start.1 = ((bf16[8,8,4864]{2,1,0:T(8,128)(2,1)}), bf16[8,8,4864]{2,1,0:T(8,128)(2,1)S(1)}, u32[]{:S(2)}, u32[]{:S(2)}) async-start(bf16[8,8,4864]{2,1,0:T(8,128)(2,1)} %bitcast.31), calls=%async_computation.1 | async-start | bytes 1245184 | tf_op jit(solution)/shard_map/all_to_all | solution.py:542
  35.9 2.4 %collective-permute-start.5 = (bf16[2,8,88,256]{3,2,1,0:T(8,128)(2,1)S(1)}, bf16[2,8,88,256]{3,2,1,0:T(8,128)(2,1)}, u32[]{:S(2)}, u32[]{:S(2)}) collective-permute-start(bf16[2,8,88,256]{3,2,1,0:T(8,128)(2,1)S(1)} %pad_maximum_fusion.1), channel_id=1, source_target_pairs={{0,1},{1,0},{2,3},{3,2},{4,5},{5,4},{6,7},{7,6},{8,9},{9,8},{10,11... | collective-permute-start | bytes 2162696 | tf_op jit(solution)/shard_map/ppermute | solution.py:164

commit v10 on v9

--- a/solution.py
+++ b/solution.py
@@ -622,18 +622,17 @@
     order = [order[0], order[-1]] + order[1:-1]
     own = share[None]
     far, near = moved_by(own, "req", order[0]), moved_by(own, "req", order[1])
-    hidden, far = lax.optimization_barrier((hidden, far))
+    weights = jnp.concatenate([own, far, near, moved_by(far, "req", order[1])])
+    hidden, weights = lax.optimization_barrier((hidden, weights))
     token_major = jnp.swapaxes(hidden, 0, 1).reshape(tokens, width)
     normed = rms_normed(token_major, norm_gain)
     projected = jnp.dot(normed, in_weight, preferred_element_type=jnp.float32).astype(jnp.bfloat16)
-    weights = jnp.concatenate([own, far, near, moved_by(far, "req", order[1])])
-    weights, projected = lax.optimization_barrier((weights, projected))
     weights = doubled(weights, "req", order[2:])[None]
 
     old_slot = jnp.arange(all_reqs, dtype=jnp.int32)
     chosen = (anchor[:, None] == old_slot[None, :]) & (fresh_flag[:, None] == 0)
     masks = jnp.stack([chosen] + [chosen & (span - e <= request_ages)[:, None] for e in range(span)])
-    masks, projected = lax.optimization_barrier((masks.astype(jnp.bfloat16), projected))
+    masks, projected, weights = lax.optimization_barrier((masks.astype(jnp.bfloat16), projected, weights))
     moved = exchange(select(masks, arrived))
 
     q_place, j_place = places("grp", halvings(groups)), places("req", order)

time: 58.5 us -> 59.3 us (1.014)
  waiting for transfers between devices: 13.4 us -> 14.7 us
  starting transfers between devices: 19.8 us -> 19.2 us
    ppermute x6, starting transfers between devices: 10.8 us -> 9.63 us  [moved_by(): lax.ppermute(values, axis, [(i, i ^ bits) for i in range(lax.axis_size(ax...]
    ppermute x6, waiting for transfers between devices: 8.53 us -> 9.36 us  [moved_by(): lax.ppermute(values, axis, [(i, i ^ bits) for i in range(lax.axis_size(ax...]
  transfers between devices with their start and end apart: 8 -> 8, of which waited for: 3 -> 4; matrix products, arithmetic and copies ran while one was open for 12% -> 12% of each run, Pallas kernels for 13% -> 13%
where the time goes in v10:
time: 59.3 us; the launch traced here: 58.9 us
  starting transfers between devices  19.2 us (32%)
  Pallas kernels  17.3 us (29%)
  waiting for transfers between devices  14.7 us (25%)
  matrix products  4.78 us (8%)
  other arithmetic  1.76 us (3%)
  between operations  0.84 us (1%)
    ppermute x6, starting transfers between devices, moved_by(): lax.ppermute(values, axis, [(i, i ^ bits) for i in range(lax.axis_size(ax...  9.63 us
    all_to_all x2, starting transfers between devices, exchange(): lax.all_to_all(values, 'req', split_axis=0, concat_axis=0, tiled=True)  9.6 us
    ppermute x6, waiting for transfers between devices, moved_by(): lax.ppermute(values, axis, [(i, i ^ bits) for i in range(lax.axis_size(ax...  9.36 us
    pallas_call x1, Pallas kernels, after(): pl.pallas_call(after_kernel, out_shape=(jax.ShapeDtypeStruct((reqs, draft...  7.14 us
    pallas_call x1, Pallas kernels, before(): pl.pallas_call(before_kernel, out_shape=(pltpu.HBM(rows, f32), jax.ShapeD...  6.54 us
    all_to_all x2, waiting for transfers between devices, exchange(): lax.all_to_all(values, 'req', split_axis=0, concat_axis=0, tiled=True)  5.35 us
    dot_general x1, matrix products, on_device(): jnp.dot(normed, in_weight, preferred_element_type=jnp.float32)  4.78 us
    pallas_call x1, Pallas kernels, prepared(): pl.pallas_call(send_kernel, out_shape=(pltpu.HBM((blocks, slots, (states...  2.61 us
  transfers between devices with their start and end apart: 8, of which 4 were waited for; matrix products, arithmetic and copies ran while one was open for 12% of the time, Pallas kernels for 13%

profile of v10, /device:TPU:0, one launch (start us, length us, event | category | flops | bytes accessed | tf_op | source)
XLA Modules:
  0.0 58.9 jit_solution(1151491647070598740)
XLA Ops:
  0.7 2.6 %send_states.1 = (bf16[8,8,4864]{2,1,0:T(8,128)(2,1)}, bf16[88,256]{1,0:T(8,128)(2,1)S(1)}) custom-call(s32[1]{0:T(128)} %bitcast.group_ref, f32[128,2048]{1,0:T(8,128)} %bitcast.32, bf16[3,8,2048]{2,1,0:T(8,128)(2,1)} %bitcast.33, bf16[160,256]{1,0:T(8,128)(2,1)} %bitcast.34, bf16[128,256]{1,0:T(8,128)(2,1)} %sw_ref.1, f32[4,256]{1,0:T(4,128)} %cw_ref.1, ...), custom_call_target="tpu_custom_call" | custom-call | tf_op jit(solution)/shard_map/send_states/pallas_call | solution.py:117
  3.3 3.0 %collective-permute-start.1 = (bf16[1,88,256]{2,1,0:T(8,128)(2,1)S(1)}, bf16[1,88,256]{2,1,0:T(8,128)(2,1)S(1)}, u32[]{:S(2)}, u32[]{:S(2)}) collective-permute-start(bf16[1,88,256]{2,1,0:T(8,128)(2,1)S(1)} %bitcast.28), channel_id=1, source_target_pairs={{0,4},{4,0},{8,12},{12,8},{16,20},{20,16},{24,28},{28,24},{1,5},{5... | collective-permute-start | bytes 135176 | tf_op jit(solution)/shard_map/ppermute | solution.py:164
  6.3 2.6 %collective-permute-start = (bf16[1,88,256]{2,1,0:T(8,128)(2,1)S(1)}, bf16[1,88,256]{2,1,0:T(8,128)(2,1)S(1)}, u32[]{:S(2)}, u32[]{:S(2)}) collective-permute-start(bf16[1,88,256]{2,1,0:T(8,128)(2,1)S(1)} %bitcast.29), channel_id=1, source_target_pairs={{0,16},{4,20},{8,24},{12,28},{16,0},{20,4},{24,8},{28,12},{1,17},{... | collective-permute-start | bytes 135176 | tf_op jit(solution)/shard_map/ppermute | solution.py:164
  8.9 3.5 %all-to-all-start = ((bf16[8,8,4864]{2,1,0:T(8,128)(2,1)}), bf16[8,8,4864]{2,1,0:T(8,128)(2,1)S(1)}, u32[]{:S(2)}, u32[]{:S(2)}) async-start(bf16[8,8,4864]{2,1,0:T(8,128)(2,1)} %get-tuple-element.22), calls=%async_computation | async-start | bytes 1245184 | tf_op jit(solution)/shard_map/all_to_all | solution.py:542
  12.5 0.1 fusion.8
  12.6 2.0 %collective-permute-start.2 = (bf16[1,88,256]{2,1,0:T(8,128)(2,1)S(1)}, bf16[1,88,256]{2,1,0:T(8,128)(2,1)S(1)}, u32[]{:S(2)}, u32[]{:S(2)}) collective-permute-start(bf16[1,88,256]{2,1,0:T(8,128)(2,1)S(1)} %collective-permute-done), channel_id=1, source_target_pairs={{0,4},{4,0},{8,12},{12,8},{16,20},{20,16},{24,28},{28,24},{1,5},{5... | collective-permute-start | bytes 135176 | tf_op jit(solution)/shard_map/ppermute | solution.py:164
  14.6 5.0 %collective-permute-done.2 = bf16[1,88,256]{2,1,0:T(8,128)(2,1)S(1)} collective-permute-done((bf16[1,88,256]{2,1,0:T(8,128)(2,1)S(1)}, bf16[1,88,256]{2,1,0:T(8,128)(2,1)S(1)}, u32[]{:S(2)}, u32[]{:S(2)}) %collective-permute-start.2) | collective-permute-done | bytes 45088 | tf_op jit(solution)/shard_map/ppermute | solution.py:164
  19.6 0.2 fusion.3
  19.9 0.1 rsqrt.12
  20.0 0.4 collective-permute-start.3
  20.4 4.8 %convolution_convert_fusion.proj_ref = bf16[128,4096]{1,0:T(8,128)(2,1)S(1)} fusion(bf16[1024,4096]{1,0:T(8,128)(2,1)} %param.19, f32[1024]{0:T(1024)S(1)} %copy-done.1, f32[128]{0:T(128)S(1)} %rsqrt.12, bf16[8,16,1024]{2,1,0:T(8,128)(2,1)S(1)} %copy-done), kind=kOutput, calls=%fused_computation | convolution fusion | flops 1074790400 | bytes 9703936 | tf_op jit(solution)/shard_map/dot_general | solution.py:629
  25.2 2.2 %collective-permute-done.3 = bf16[4,88,256]{2,1,0:T(8,128)(2,1)S(1)} collective-permute-done((bf16[4,88,256]{2,1,0:T(8,128)(2,1)S(1)}, bf16[4,88,256]{2,1,0:T(8,128)(2,1)S(1)}, u32[]{:S(2)}, u32[]{:S(2)}) %collective-permute-start.3) | collective-permute-done | bytes 180256 | tf_op jit(solution)/shard_map/ppermute | solution.py:164
  27.4 1.6 %collective-permute-start.4 = (bf16[1,8,88,256]{3,2,1,0:T(8,128)(2,1)S(1)}, bf16[1,8,88,256]{3,2,1,0:T(8,128)(2,1)S(1)}, u32[]{:S(2)}, u32[]{:S(2)}) collective-permute-start(bf16[1,8,88,256]{3,2,1,0:T(8,128)(2,1)S(1)} %maximum_bitcast_fusion), channel_id=1, source_target_pairs={{0,2},{1,3},{2,0},{3,1},{4,6},{5,7},{6,4},{7,5},{8,10},{9,11},{10,... | collective-permute-start | bytes 1081352 | tf_op jit(solution)/shard_map/ppermute | solution.py:164
  29.0 1.0 %select_slots.1 = bf16[64,4864]{1,0:T(8,128)(2,1)} custom-call(bf16[4,64,64]{2,1,0:T(8,128)(2,1)S(1)} %add_convert_fusion.mask_ref, bf16[64,4864]{1,0:T(8,128)(2,1)S(1)} %bitcast.27), custom_call_target="tpu_custom_call" | custom-call | tf_op jit(solution)/shard_map/select_slots/pallas_call | solution.py:566
  30.0 6.1 %all-to-all-start.1 = ((bf16[8,8,4864]{2,1,0:T(8,128)(2,1)}), bf16[8,8,4864]{2,1,0:T(8,128)(2,1)S(1)}, u32[]{:S(2)}, u32[]{:S(2)}) async-start(bf16[8,8,4864]{2,1,0:T(8,128)(2,1)} %bitcast.31), calls=%async_computation.1 | async-start | bytes 1245184 | tf_op jit(solution)/shard_map/all_to_all | solution.py:542
  36.1 0.1 pad_maximum_fusion.1
  36.2 0.1 collective-permute-start.5
  36.3 0.1 dynamic_slice.3
  36.4 2.2 %collective-permute-done.5 = bf16[2,8,88,256]{3,2,1,0:T(8,128)(2,1)} collective-permute-done((bf16[2,8,88,256]{3,2,1,0:T(8,128)(2,1)S(1)}, bf16[2,8,88,256]{3,2,1,0:T(8,128)(2,1)}, u32[]{:S(2)}, u32[]{:S(2)}) %collective-permute-start.5) | collective-permute-done | bytes 720928 | tf_op jit(solution)/shard_map/ppermute | solution.py:164
  38.6 1.3 %pad_maximum_fusion.w_ref = bf16[4,8,88,256]{3,2,1,0:T(8,128)(2,1)S(1)} fusion(bf16[2,8,88,256]{3,2,1,0:T(8,128)(2,1)} %collective-permute-done.5, bf16[1,8,88,256]{3,2,1,0:T(8,128)(2,1)S(1)} %collective-permute-done.4, bf16[1,8,88,256]{3,2,1,0:T(8,128)(2,1)S(1)} %maximum_bitcast_fusion), kind=kLoop, calls=%fused_computation.1 | loop fusion | flops 1441792 | bytes 2883584 | tf_op jit(solution)/shard_map/concatenate | solution.py:169
  39.8 0.1 broadcast_in_dim.58.acc_ref
  39.9 6.5 %before_states.1 = (f32[16,464,128]{2,1,0:T(8,128)}, f32[16,8,128]{2,1,0:T(8,128)S(1)}, f32[104,32]{1,0:T(8,128)S(1)}, bf16[8,160,256]{2,1,0:T(8,128)(2,1)S(1)},...) custom-call(s32[4]{0:T(128)S(1)} %fusion.9.q_ref, s32[8]{0:T(128)S(1)} %fusion.11.j_ref, ...), custom_call_target="tpu_custom_call" | custom-call | flops 200000000 | bytes 8388608 | tf_op jit(solution)/shard_map/before_states/pallas_call | solution.py:335
  46.4 5.3 %all-to-all-done.1.moved_ref = bf16[8,8,4864]{2,1,0:T(8,128)(2,1)S(1)} async-done(((bf16[8,8,4864]{2,1,0:T(8,128)(2,1)}), bf16[8,8,4864]{2,1,0:T(8,128)(2,1)S(1)}, u32[]{:S(2)}, u32[]{:S(2)}) %all-to-all-start.1) | async-done | bytes 622624 | tf_op jit(solution)/shard_map/all_to_all | solution.py:542
  51.8 7.1 %after_states.1 = (bf16[8,16,1024]{2,1,0:T(8,128)(2,1)}, f32[128,2048]{1,0:T(8,128)}) custom-call(bf16[8,8,4864]{2,1,0:T(8,128)(2,1)S(1)} %all-to-all-done.1.moved_ref, s32[8,128]{1,0:T(8,128)S(1)} %broadcast_in_dim.58.acc_ref, f32[16,8,128]{2,1,0:T(8,128)S(1)} %get-tuple-element.25.at_ref, f32[104,32]{1,0:T(8,128)S(1)} %get-tuple-element.26.coef_ref, ...), custom_call_target="tpu_custom_call" | custom-call | flops 536870912 | bytes 12582912 | tf_op jit(solution)/shard_map/after_states/pallas_call | solution.py:511
  (23 shorter events, 0.1 us)
Async XLA Ops:
  0.6 11.8 %copy-start.3 = (s32[64]{0:T(128)S(1)}, s32[64]{0:T(128)}, u32[]{:S(2)}) copy-start(s32[64]{0:T(128)} %param.33) | copy-start | bytes 772
  0.6 11.8 %copy-start.4 = (s32[64]{0:T(128)S(1)}, s32[64]{0:T(128)}, u32[]{:S(2)}) copy-start(s32[64]{0:T(128)} %param.31) | copy-start | bytes 772
  0.7 11.8 %copy-start.2 = (s32[64]{0:T(128)S(1)}, s32[64]{0:T(128)}, u32[]{:S(2)}) copy-start(s32[64]{0:T(128)} %param.30) | copy-start | bytes 772
  0.7 19.0 %copy-start = (bf16[8,16,1024]{2,1,0:T(8,128)(2,1)S(1)}, bf16[8,16,1024]{2,1,0:T(8,128)(2,1)}, u32[]{:S(2)}) copy-start(bf16[8,16,1024]{2,1,0:T(8,128)(2,1)} %param.17) | copy-start | bytes 786436
  0.7 19.7 %copy-start.1 = (f32[1024]{0:T(1024)S(1)}, f32[1024]{0:T(1024)}, u32[]{:S(2)}) copy-start(f32[1024]{0:T(1024)} %param.18) | copy-start | bytes 12292
  3.3 11.3 %collective-permute-start.1 = (bf16[1,88,256]{2,1,0:T(8,128)(2,1)S(1)}, bf16[1,88,256]{2,1,0:T(8,128)(2,1)S(1)}, u32[]{:S(2)}, u32[]{:S(2)}) collective-permute-start(bf16[1,88,256]{2,1,0:T(8,128)(2,1)S(1)} %bitcast.28), channel_id=1, source_target_pairs={{0,4},{4,0},{8,12},{12,8},{16,20},{20,16},{24,28},{28,24},{1,5},{5... | collective-permute-start | bytes 135176 | tf_op jit(solution)/shard_map/ppermute | solution.py:164
  6.3 6.3 %collective-permute-start = (bf16[1,88,256]{2,1,0:T(8,128)(2,1)S(1)}, bf16[1,88,256]{2,1,0:T(8,128)(2,1)S(1)}, u32[]{:S(2)}, u32[]{:S(2)}) collective-permute-start(bf16[1,88,256]{2,1,0:T(8,128)(2,1)S(1)} %bitcast.29), channel_id=1, source_target_pairs={{0,16},{4,20},{8,24},{12,28},{16,0},{20,4},{24,8},{28,12},{1,17},{... | collective-permute-start | bytes 135176 | tf_op jit(solution)/shard_map/ppermute | solution.py:164
  8.9 20.1 %all-to-all-start = ((bf16[8,8,4864]{2,1,0:T(8,128)(2,1)}), bf16[8,8,4864]{2,1,0:T(8,128)(2,1)S(1)}, u32[]{:S(2)}, u32[]{:S(2)}) async-start(bf16[8,8,4864]{2,1,0:T(8,128)(2,1)} %get-tuple-element.22), calls=%async_computation | async-start | bytes 1245184 | tf_op jit(solution)/shard_map/all_to_all | solution.py:542
  12.6 7.0 %collective-permute-start.2 = (bf16[1,88,256]{2,1,0:T(8,128)(2,1)S(1)}, bf16[1,88,256]{2,1,0:T(8,128)(2,1)S(1)}, u32[]{:S(2)}, u32[]{:S(2)}) collective-permute-start(bf16[1,88,256]{2,1,0:T(8,128)(2,1)S(1)} %collective-permute-done), channel_id=1, source_target_pairs={{0,4},{4,0},{8,12},{12,8},{16,20},{20,16},{24,28},{28,24},{1,5},{5... | collective-permute-start | bytes 135176 | tf_op jit(solution)/shard_map/ppermute | solution.py:164
  20.0 7.4 %collective-permute-start.3 = (bf16[4,88,256]{2,1,0:T(8,128)(2,1)S(1)}, bf16[4,88,256]{2,1,0:T(8,128)(2,1)S(1)}, u32[]{:S(2)}, u32[]{:S(2)}) collective-permute-start(bf16[4,88,256]{2,1,0:T(8,128)(2,1)S(1)} %pad_maximum_fusion.2), channel_id=1, source_target_pairs={{0,8},{4,12},{8,0},{12,4},{16,24},{20,28},{24,16},{28,20},{1,9},{5... | collective-permute-start | bytes 540680 | tf_op jit(solution)/shard_map/ppermute | solution.py:164
  27.4 8.9 %copy-start.5 = (s32[64]{0:T(128)S(1)}, s32[64]{0:T(128)}, u32[]{:S(2)}) copy-start(s32[64]{0:T(128)} %param.32) | copy-start | bytes 772
  27.4 8.7 %collective-permute-start.4 = (bf16[1,8,88,256]{3,2,1,0:T(8,128)(2,1)S(1)}, bf16[1,8,88,256]{3,2,1,0:T(8,128)(2,1)S(1)}, u32[]{:S(2)}, u32[]{:S(2)}) collective-permute-start(bf16[1,8,88,256]{3,2,1,0:T(8,128)(2,1)S(1)} %maximum_bitcast_fusion), channel_id=1, source_target_pairs={{0,2},{1,3},{2,0},{3,1},{4,6},{5,7},{6,4},{7,5},{8,10},{9,11},{10,... | collective-permute-start | bytes 1081352 | tf_op jit(solution)/shard_map/ppermute | solution.py:164
  30.0 21.8 %all-to-all-start.1 = ((bf16[8,8,4864]{2,1,0:T(8,128)(2,1)}), bf16[8,8,4864]{2,1,0:T(8,128)(2,1)S(1)}, u32[]{:S(2)}, u32[]{:S(2)}) async-start(bf16[8,8,4864]{2,1,0:T(8,128)(2,1)} %bitcast.31), calls=%async_computation.1 | async-start | bytes 1245184 | tf_op jit(solution)/shard_map/all_to_all | solution.py:542
  36.2 2.4 %collective-permute-start.5 = (bf16[2,8,88,256]{3,2,1,0:T(8,128)(2,1)S(1)}, bf16[2,8,88,256]{3,2,1,0:T(8,128)(2,1)}, u32[]{:S(2)}, u32[]{:S(2)}) collective-permute-start(bf16[2,8,88,256]{3,2,1,0:T(8,128)(2,1)S(1)} %pad_maximum_fusion.1), channel_id=1, source_target_pairs={{0,1},{1,0},{2,3},{3,2},{4,5},{5,4},{6,7},{7,6},{8,9},{9,8},{10,11... | collective-permute-start | bytes 2162696 | tf_op jit(solution)/shard_map/ppermute | solution.py:164
